TPU v7x, 256 devices: a whole 4x4x8 slice. The times are simulated.
256 devices in a mesh: edge: 64 (over y, z, core), pix: 4 (over x).
Axes of the slice: x: 4, y: 4, z: 8, core: 2. Of those that a mesh axis runs over, the one named last changes fastest.
Arguments:
- features: bfloat16 [128, 48, 64, 128], P('edge', 'pix'), may hold values from -6 to 6
- poses: float32 [128, 6], replicated, may hold values from -1.5 to 1.5
- inv_depth: float32 [128, 3072], P('edge', 'pix'), may hold values from 0.25 to 2
- hidden: bfloat16 [256, 48, 64, 128], P('edge', 'pix'), may hold values from -1 to 1
- edges: int32 [256, 2], P('edge'), may hold values from 0 to 127, as said below
- counts: int32 [64], P('edge'), may hold values from 1 to 4, 128 in all
- w_gates: bfloat16 [9, 256, 256], replicated, may hold values from -0.125 to 0.125
- w_cand: bfloat16 [9, 256, 128], replicated, may hold values from -0.125 to 0.125
- w_head: bfloat16 [4, 128], replicated, may hold values from -0.5 to 0.5
Outputs:
- hidden_out: bfloat16 [256, 48, 64, 128], P('edge', 'pix')
- pose_update: float32 [128, 6], P('edge')
- depth_update: float32 [128, 3072], P('edge', 'pix')
Inputs may be any that keep to these rules, and one draw needn't show every extreme that they name: `edges`: slot s lies on node n = s // 4; its source frame is 2n or 2n + 1 and its target is one of the frames 2n to 2n + 3 other than the source; on the last node the target is the other frame of its own pair. The first slot of node n goes from frame 2n to frame 2n + 2 (on the last node to 2n + 1). Dead slots hold such pairs too.
All inputs are finite; a program needn't handle non-finite values. No bound on the sum of `counts` on one device may be relied on, other than what follows from the above.
Results may differ from a plain program's by a relative error of at most 0.011.
Values may be sent and summed in bfloat16 or wider, within the bound.
No kernel may reach another device: no remote copies, remote signals or barrier semaphores. Data moves between devices by JAX's collectives and lax.ppermute only.
A program may use at most 192 MiB of HBM per device.

v0:
```python
import functools
import math

import jax
import jax.numpy as jnp
from jax import lax
from jax.experimental import pallas as pl
from jax.experimental.pallas import tpu as pltpu
from jax.sharding import Mesh
from jax.sharding import PartitionSpec as P

PRECISE = lax.Precision.HIGHEST
POSE_DAMPING = 0.1
DEPTH_DAMPING = 0.1

EDGE = ("y", "z", "core")


def swapped(value, axis, step):
    count = lax.axis_size(axis)
    return lax.ppermute(value, axis, [(i, i ^ step) for i in range(count)])


def gathered_blocks(block):
    pair = block + swapped(block, "x", 1)
    block = pair + (swapped(block, "x", 2) + swapped(block, "x", 3))
    parts = lax.all_gather(block, "core", axis=0)
    parts = jnp.stack([parts] + [swapped(parts, "z", s) for s in (1, 2, 3)])
    parts = jnp.stack([parts, swapped(parts, "z", 4)])
    parts = jnp.stack([parts] + [swapped(parts, "y", s) for s in (1, 2, 3)])
    return parts.reshape((-1,) + block.shape)


def bundle_body(slots, rows_all, cols, info, poses, rho_ref, head, out, h_ref, dd_ref, a_ref, w_ref):
    pix = rho_ref.shape[1]
    rows = pix // cols
    shift = cols.bit_length() - 1
    base = 2 * info[2 * slots + 1]
    live = info[2 * slots]
    lane = lax.broadcasted_iota(jnp.int32, (1, pix), 1)
    col = (lane & (cols - 1)).astype(jnp.float32)
    row = ((lane >> shift) + info[2 * slots + 2] * rows).astype(jnp.float32)
    half = cols / 2.0
    u = (col - (cols - 1) / 2.0) / half
    v = (row - (rows_all - 1) / 2.0) / half
    sub = lax.broadcasted_iota(jnp.int32, (8, pix), 0)
    zero = jnp.zeros((8, pix), jnp.float32)
    lead_h = jnp.where(sub == 0, 1.0, jnp.where(sub == 2, -u, zero))
    rest_h = jnp.where(sub == 3, -u * v, jnp.where(sub == 4, 1.0 + u * u, jnp.where(sub == 5, -v, zero)))
    lead_v = jnp.where(sub == 1, 1.0, jnp.where(sub == 2, -v, zero))
    rest_v = jnp.where(sub == 3, -(1.0 + v * v), jnp.where(sub == 4, u * v, jnp.where(sub == 5, u, zero)))
    sub1 = lax.broadcasted_iota(jnp.int32, (8, 1), 0)
    eye = lax.broadcasted_iota(jnp.int32, (8, 6), 0) == lax.broadcasted_iota(jnp.int32, (8, 6), 1)
    picks, sels = [], []
    for s in range(slots):
        src, tgt = info[2 * s], info[2 * s + 1]
        a_loc, b_loc = src - base, tgt - base
        alive = jnp.where(s < live, 1.0, 0.0)
        picks.append([jnp.where(a_loc == f, 1.0, 0.0) for f in range(2)])
        sels.append([jnp.where(b_loc == g, 1.0, 0.0) - jnp.where(a_loc == g, 1.0, 0.0) for g in range(4)])
        d_row = poses[pl.ds(tgt, 1), :] - poses[pl.ds(src, 1), :]
        d = jnp.sum(jnp.where(eye, jnp.broadcast_to(d_row, (8, 6)), 0.0), axis=1, keepdims=True)
        rho = rho_ref[pl.ds(a_loc, 1), :]
        conf_h = jax.nn.sigmoid(head[8 * s + 2 : 8 * s + 3, :]) * alive
        conf_v = jax.nn.sigmoid(head[8 * s + 3 : 8 * s + 4, :]) * alive
        a_h = rho * lead_h + rest_h
        a_v = rho * lead_v + rest_v
        e_h = head[8 * s : 8 * s + 1, :] - jnp.sum(a_h * d, axis=0, keepdims=True)
        e_v = head[8 * s + 1 : 8 * s + 2, :] - jnp.sum(a_v * d, axis=0, keepdims=True)
        k_h = jnp.sum(lead_h * d, axis=0, keepdims=True)
        k_v = jnp.sum(lead_v * d, axis=0, keepdims=True)
        a_h = jnp.where(sub == 6, e_h, a_h)
        a_v = jnp.where(sub == 6, e_v, a_v)
        w_h = conf_h * a_h
        w_v = conf_v * a_v
        at = slice(8 * s, 8 * s + 8)
        a_ref[at, :pix] = a_h
        a_ref[at, pix:] = a_v
        w_ref[at, :pix] = w_h
        w_ref[at, pix:] = w_v
        k_s = w_h * k_h + w_v * k_v
        dd = conf_h * k_h * k_h + conf_v * k_v * k_v
        for f in range(2):
            pick = picks[s][f]
            old = dd_ref[f : f + 1, :] if s else jnp.full((1, pix), DEPTH_DAMPING, jnp.float32)
            dd_ref[f : f + 1, :] = old + pick * dd
            for g in range(4):
                term = jnp.where(sub1 == 6, pick, pick * sels[s][g]) * k_s
                at = (slice(8 * g, 8 * g + 8), slice(f * pix, (f + 1) * pix))
                h_ref[at] = h_ref[at] + term if s else term
    nt = (((1,), (1,)), ((), ()))
    gram = lax.dot_general(w_ref[...], a_ref[...], nt, precision=PRECISE, preferred_element_type=jnp.float32)
    for f in range(2):
        at = slice(f * pix, (f + 1) * pix)
        w_ref[:, at] = h_ref[:, at] * (1.0 / dd_ref[f : f + 1, :])
    schur = lax.dot_general(w_ref[...], h_ref[...], nt, precision=PRECISE, preferred_element_type=jnp.float32)
    pad = jnp.zeros((32, 96), jnp.float32)
    gram = jnp.concatenate([gram, pad], axis=1)
    schur = jnp.concatenate([schur, pad], axis=1)
    lanes = lax.broadcasted_iota(jnp.int32, (8, 128), 1)
    group, inner = lanes >> 3, lanes & 7
    terms = []
    for s in range(slots):
        y = jnp.where(group == s, gram[8 * s : 8 * s + 8, :], 0.0)
        y = pltpu.roll(y, 128 - 8 * s, 1) if s else y
        y = y + pltpu.roll(y, 8, 1)
        y = y + pltpu.roll(y, 16, 1)
        coef = jnp.zeros((8, 128), jnp.float32)
        for g in range(4):
            coef = jnp.where(group == g, sels[s][g], coef)
        terms.append(y * jnp.where(inner == 6, 1.0, coef))
    total = None
    for g in range(4):
        part = -schur[8 * g : 8 * g + 8, :]
        for s in range(slots):
            part = part + sels[s][g] * terms[s]
        part = jnp.where(lanes < 32, part, 0.0)
        total = part if g == 0 else total + pltpu.roll(part, 32 * g, 1)
    out[...] = total


REAL = (0, 1, 2, 3, 4, 5, 8, 9, 10, 11, 12, 13)


def down(x, width=16):
    return jnp.broadcast_to(x, (width, 128))


def eliminate(diag, sides):
    diag, sides = list(diag), [list(side) for side in sides]
    count = len(REAL)
    for k in range(count):
        at = slice(REAL[k], REAL[k] + 1)
        scale = down(1.0 / diag[k][at, :])
        diag[k] = diag[k] * scale
        for side in sides:
            side[k] = side[k] * scale
        for i in range(count):
            if i != k:
                f = down(diag[i][at, :])
                diag[i] = diag[i] - f * diag[k]
                for side in sides:
                    side[i] = side[i] - f * side[k]
    return diag, sides


def solve_body(nodes, pix, info, g_ref, h_ref, dd_ref, pose_ref, depth_ref, t_ref, d_ref, l_ref, u_ref, near):
    count = len(REAL)
    lane = lax.broadcasted_iota(jnp.int32, (16, 128), 1)
    sub = lax.broadcasted_iota(jnp.int32, (16, 128), 0)
    me = info[0]
    flip = me - (me & 1)
    for n in range(nodes):
        t_ref[n] = g_ref[n ^ flip]
    rest = jnp.zeros((128 - nodes, 128), jnp.float32)
    for k in range(6):
        t = jnp.concatenate([t_ref[:, k, :], rest], axis=0).T
        for f in range(2):
            i = 6 * f + k
            far = jnp.where(lane < nodes, pltpu.roll(t[32 * f + 80 : 32 * f + 96], 1, 1), 0.0)
            d_ref[i] = t[32 * f : 32 * f + 16] + far + jnp.where(sub == REAL[i], POSE_DAMPING, 0.0)
            u_ref[i] = jnp.where(lane < nodes - 1, t[32 * f + 16 : 32 * f + 32], 0.0)
            l_ref[i] = jnp.where(lane < nodes, pltpu.roll(t[32 * f + 64 : 32 * f + 80], 1, 1), 0.0)

    def level(step, carry):
        s = jnp.left_shift(1, step)
        diag, (low, up) = eliminate(
            [d_ref[i] for i in range(count)], [[l_ref[i] for i in range(count)], [u_ref[i] for i in range(count)]]
        )
        for k in range(count):
            low_r = jnp.where(sub == 6, diag[k], low[k])
            up_r = jnp.where(sub == 6, diag[k], up[k])
            near[0, k] = pltpu.roll(up_r, s, 1)
            near[1, k] = pltpu.roll(low[k], s, 1)
            near[2, k] = pltpu.roll(low_r, 128 - s, 1)
            near[3, k] = pltpu.roll(up[k], 128 - s, 1)
        for i in range(count):
            d_new = d_ref[i]
            l_old, u_old = l_ref[i], u_ref[i]
            l_new = jnp.zeros((16, 128), jnp.float32)
            u_new = jnp.zeros((16, 128), jnp.float32)
            for k in range(count):
                at = slice(REAL[k], REAL[k] + 1)
                fl, fu = down(l_old[at, :]), down(u_old[at, :])
                d_new = d_new - fl * near[0, k] - fu * near[2, k]
                l_new = l_new - fl * near[1, k]
                u_new = u_new - fu * near[3, k]
            d_ref[i] = d_new
            l_ref[i] = l_new
            u_ref[i] = u_new
        return carry

    levels = max(1, (nodes - 1).bit_length())
    lax.fori_loop(0, levels, level, 0)
    diag, _ = eliminate([d_ref[i] for i in range(count)], [])
    x = jnp.zeros((16, 128), jnp.float32)
    for i in range(count):
        x = jnp.where(sub == REAL[i], down(diag[i][6:7, :]), x)
    own = jnp.sum(jnp.where(lane == me, x, 0.0), axis=1, keepdims=True)
    after = jnp.sum(jnp.where((lane == me + 1) & (lane < nodes), x, 0.0), axis=1, keepdims=True)
    spread = jnp.where((sub & 7) == lane, jnp.broadcast_to(own, (16, 128)), 0.0)
    for f in range(2):
        pose_ref[f : f + 1, :] = jnp.sum(spread[8 * f : 8 * f + 8], axis=0, keepdims=True)[:, :6]
    column = jnp.concatenate([own, after], axis=0)
    column = jnp.where(lax.broadcasted_iota(jnp.int32, (32, 1), 0) == 6, -1.0, column)
    for f in range(2):
        pull = jnp.sum(h_ref[:, f * pix : (f + 1) * pix] * column, axis=0, keepdims=True)
        depth_ref[f : f + 1, :] = -pull / dd_ref[f : f + 1, :]


def solve_call(me, gathered, h, dd):
    nodes = gathered.shape[0]
    pix = dd.shape[1]
    vmem = pl.BlockSpec(memory_space=pltpu.VMEM)
    return pl.pallas_call(
        functools.partial(solve_body, nodes, pix),
        out_shape=(
            jax.ShapeDtypeStruct((2, 6), jnp.float32),
            jax.ShapeDtypeStruct((2, pix), jnp.float32),
        ),
        in_specs=[pl.BlockSpec(memory_space=pltpu.SMEM), vmem, vmem, vmem],
        out_specs=(vmem, vmem),
        scratch_shapes=[
            pltpu.VMEM((nodes, 8, 128), jnp.float32),
            pltpu.VMEM((12, 16, 128), jnp.float32),
            pltpu.VMEM((12, 16, 128), jnp.float32),
            pltpu.VMEM((12, 16, 128), jnp.float32),
            pltpu.VMEM((4, 12, 16, 128), jnp.float32),
        ],
        name="pose_solve",
    )(me, gathered, h, dd)


NT = (((1,), (1,)), ((), ()))
TILE = 256
CHUNK = 768


def gate(value):
    return 0.5 * jnp.tanh(0.5 * value) + 0.5


def spots(info, slots, pix, halo):
    odd = (info[2 * slots + 2] & 1) == 1
    at1 = pl.multiple_of(jnp.where(odd, 0, halo + pix), halo)
    at3 = pl.multiple_of(jnp.where(odd, halo + pix, 0), halo)
    return at1, at3


def load_keys(near, owns, nexts, k_ref, vt_ref):
    channels = k_ref.shape[1]

    @pl.when(near)
    def _():
        base = 0
        for part in owns:
            k_ref[base : base + part.shape[1], :] = part[0]
            base += part.shape[1]

    @pl.when(jnp.logical_not(near))
    def _():
        base = 0
        for part in nexts:
            k_ref[base : base + part.shape[1], :] = part[0]
            base += part.shape[1]

    vt_ref[:channels, :] = k_ref[...].T
    vt_ref[channels:, :] = jnp.ones((vt_ref.shape[0] - channels, vt_ref.shape[1]), jnp.bfloat16)


def add_keys(k_ref, vt_ref, qt_ref, acc_ref, old, factor):
    keys, ext = k_ref.shape[0], qt_ref.shape[1]
    for t in range(ext // TILE):
        at = slice(t * TILE, (t + 1) * TILE)
        acc = None if old is None else old[0, :, at]
        for j in range(keys // CHUNK):
            span = slice(j * CHUNK, (j + 1) * CHUNK)
            s = jnp.dot(k_ref[span, :], qt_ref[:, at], preferred_element_type=jnp.float32)
            p = jnp.exp2(s * factor).astype(jnp.bfloat16)
            part = jnp.dot(vt_ref[:, span], p, preferred_element_type=jnp.float32)
            acc = part if acc is None else acc + part
        acc_ref[0, :, at] = acc


def load_queries(info, slots, own_q, side1, side3, q_ref, qt_ref):
    pix, halo = own_q.shape[1], side1.shape[1]
    at1, at3 = spots(info, slots, pix, halo)
    q_ref[halo : halo + pix, :] = own_q[0]
    q_ref[pl.ds(at1, halo), :] = side1[0]
    q_ref[pl.ds(at3, halo), :] = side3[0]
    qt_ref[...] = q_ref[...].T


def match_factor(channels):
    return 2.0 / math.sqrt(channels) * math.log2(math.e)


def match_body(dims, info, own_q, side1, side3, *refs):
    slots, parts, chained = dims
    owns, refs = refs[:parts], refs[parts:]
    nexts, refs = refs[:parts], refs[parts:]
    old = refs[0] if chained else None
    acc_ref, q_ref, qt_ref, k_ref, vt_ref = refs[chained:]
    slot = pl.program_id(0)

    @pl.when(slot < info[2 * slots])
    def _():
        near = info[2 * slot + 1] - 2 * info[2 * slots + 1] < 2
        load_queries(info, slots, own_q, side1, side3, q_ref, qt_ref)
        load_keys(near, owns, nexts, k_ref, vt_ref)
        add_keys(k_ref, vt_ref, qt_ref, acc_ref, old, match_factor(q_ref.shape[1]))


def fused_body(dims, info, *refs):
    slots, total_rows, rows, cols, last, parts = dims
    (own_q, side1, side3, old), refs = refs[:4], refs[4:]
    (state, hide1, hide3), refs = refs[:3], refs[3:]
    owns, refs = refs[:parts], refs[parts:]
    nexts, refs = refs[:parts], refs[parts:]
    (wg, wc01, wc2, wh, poses, rho_ref), refs = refs[:6], refs[6:]
    (fresh_ref, block_ref, pull_ref, scale_ref), refs = refs[:4], refs[4:]
    q_ref, qt_ref, k_ref, vt_ref, acc_ref, kall_ref, vtall_ref, x_ref, h_ref, head_ref, a_ref, w_ref = refs
    slot = pl.program_id(0)
    live = slot < info[2 * slots]
    pix_rank = info[2 * slots + 2]
    pix = rows * cols
    halo = 2 * cols
    ext = pix + 2 * halo
    channels = own_q.shape[-1]
    factor = match_factor(channels)
    at1, at3 = spots(info, slots, pix, halo)
    px = lax.broadcasted_iota(jnp.int32, (ext, 1), 0)

    def inside(px):
        grow = (px >> (cols.bit_length() - 1)) - 2 + rows * pix_rank
        return jnp.where((grow >= 0) & (grow < total_rows), 1.0, 0.0)

    valid = inside(px)

    @pl.when(jnp.logical_not(live))
    def _():
        fresh_ref[...] = state[...]
        head_ref[pl.ds(pl.multiple_of(8 * slot, 8), 8), :] = jnp.zeros((8, pix), jnp.float32)

    @pl.when(live)
    def _():
        near = info[2 * slot + 1] - 2 * info[2 * slots + 1] < 2
        load_queries(info, slots, own_q, side1, side3, q_ref, qt_ref)
        load_keys(near, owns[parts - last :], nexts[parts - last :], k_ref, vt_ref)
        add_keys(k_ref, vt_ref, qt_ref, acc_ref, old, factor)
        sums = acc_ref[0, channels : channels + 1, :]
        fits = (jnp.min(sums) > 1e-20) & (jnp.max(sums) < 1e25)

        @pl.when(jnp.logical_not(fits))
        def _():
            load_keys(near, owns, nexts, kall_ref, vtall_ref)
            chunks = kall_ref.shape[0] // CHUNK

            def exact(t, carry):
                at = pl.ds(pl.multiple_of(t * TILE, TILE), TILE)
                q = qt_ref[:, at]

                def scores(j):
                    span = pl.ds(pl.multiple_of(j * CHUNK, CHUNK), CHUNK)
                    return jnp.dot(kall_ref[span, :], q, preferred_element_type=jnp.float32)

                top = lax.fori_loop(
                    0,
                    chunks,
                    lambda j, top: jnp.maximum(top, jnp.max(scores(j), axis=0, keepdims=True)),
                    jnp.full((1, TILE), -3e38, jnp.float32),
                )

                def add(j, acc):
                    span = pl.ds(pl.multiple_of(j * CHUNK, CHUNK), CHUNK)
                    p = jnp.exp2((scores(j) - top) * factor).astype(jnp.bfloat16)
                    return acc + jnp.dot(vtall_ref[:, span], p, preferred_element_type=jnp.float32)

                acc_ref[0, :, at] = lax.fori_loop(
                    0, chunks, add, jnp.zeros((acc_ref.shape[1], TILE), jnp.float32)
                )
                return carry

            lax.fori_loop(0, ext // TILE, exact, 0)

        h_ref[halo : halo + pix, :] = state[0]
        h_ref[pl.ds(at1, halo), :] = hide1[0]
        h_ref[pl.ds(at3, halo), :] = hide3[0]
        col = px & (cols - 1)
        first, final = col == 0, col == cols - 1

        def spread(value, at, lane):
            size = value.shape[0]
            span = slice(lane, lane + channels)
            x_ref[at, span] = jnp.where(first[at], 0.0, pltpu.roll(value, 1, 0)).astype(jnp.bfloat16)
            span = slice(lane + 2 * channels, lane + 3 * channels)
            x_ref[at, span] = value.astype(jnp.bfloat16)
            span = slice(lane + 4 * channels, lane + 5 * channels)
            x_ref[at, span] = jnp.where(final[at], 0.0, pltpu.roll(value, size - 1, 0)).astype(jnp.bfloat16)

        wide = h_ref[...].astype(jnp.float32) * valid
        spread(wide, slice(0, ext), 0)
        weight = inside(lax.broadcasted_iota(jnp.int32, (1, ext), 1)) / acc_ref[0, channels : channels + 1, :]
        spread((acc_ref[0, :channels, :] * weight).T, slice(0, ext), channels)
        mid = ext - 2 * cols
        gates = None
        for r in range(3):
            part = jnp.dot(x_ref[r * cols : r * cols + mid, :], wg[r], preferred_element_type=jnp.float32)
            gates = part if r == 0 else gates + part
        inner = slice(cols, cols + mid)
        spread(gate(gates[:, channels:]) * wide[inner], inner, 0)
        pair = jnp.dot(x_ref[cols : 2 * cols + pix, :], wc01[...], preferred_element_type=jnp.float32)
        cand = jnp.dot(x_ref[3 * cols : 3 * cols + pix, :], wc2[...], preferred_element_type=jnp.float32)
        cand = cand + pair[:pix, :channels] + pair[cols : cols + pix, channels:]
        update = gate(gates[cols : cols + pix, :channels])
        kept = wide[halo : halo + pix]
        fresh = ((1.0 - update) * kept + update * jnp.tanh(cand)).astype(jnp.bfloat16)
        fresh_ref[0] = fresh
        head = lax.dot_general(wh[...], fresh, NT, preferred_element_type=jnp.float32)
        head_ref[pl.ds(pl.multiple_of(8 * slot, 8), 8), :] = head

    @pl.when(slot == slots - 1)
    def _():
        bundle_body(
            slots, total_rows, cols, info, poses, rho_ref, head_ref, block_ref, pull_ref, scale_ref, a_ref, w_ref
        )


class Specs:
    def __init__(self, slots, pix, channels, halo):
        self.slots, self.pix, self.channels, self.halo = slots, pix, channels, halo
        self.at = 2 * slots + 1

    def source(self, s, info):
        return jnp.clip(info[2 * s] - 2 * info[self.at], 0, 1)

    def target(self, s, info):
        return info[2 * s + 1] - 2 * info[self.at]

    def side(self, flip):
        far = self.pix // self.halo - 1

        def index(s, info):
            low = (info[self.at + 1] & 1) == flip
            return (self.source(s, info), jnp.where(low, far, 0), 0)

        return pl.BlockSpec((1, self.halo, self.channels), index)

    def queries(self):
        main = pl.BlockSpec((1, self.pix, self.channels), lambda s, info: (self.source(s, info), 0, 0))
        return [main, self.side(1), self.side(0)]

    def parts(self, parts, base):
        return [
            pl.BlockSpec(
                (1, part.shape[1], self.channels),
                lambda s, info: (jnp.clip(self.target(s, info) - base, 0, 1), 0, 0),
            )
            for part in parts
        ]

    def slot(self, rows, lanes):
        return pl.BlockSpec((1, rows, lanes), lambda s, info: (s, 0, 0))

    def whole(self, shape):
        return pl.BlockSpec(shape, lambda s, info: (0,) * len(shape))


def match_call(info, slots, cols, queries, owns, nexts, old):
    pix, channels = queries[0].shape[1:]
    halo = 2 * cols
    ext = pix + 2 * halo
    keys = sum(part.shape[1] for part in owns)
    specs = Specs(slots, pix, channels, halo)
    chained = () if old is None else (old,)
    return pl.pallas_call(
        functools.partial(match_body, (slots, len(owns), len(chained))),
        grid_spec=pltpu.PrefetchScalarGridSpec(
            num_scalar_prefetch=1,
            grid=(slots,),
            in_specs=specs.queries()
            + specs.parts(owns, 0)
            + specs.parts(nexts, 2)
            + [specs.slot(channels + 8, ext) for _ in chained],
            out_specs=specs.slot(channels + 8, ext),
            scratch_shapes=[
                pltpu.VMEM((ext, channels), jnp.bfloat16),
                pltpu.VMEM((channels, ext), jnp.bfloat16),
                pltpu.VMEM((keys, channels), jnp.bfloat16),
                pltpu.VMEM((channels + 8, keys), jnp.bfloat16),
            ],
        ),
        out_shape=jax.ShapeDtypeStruct((slots, channels + 8, ext), jnp.float32),
        cost_estimate=pl.CostEstimate(
            flops=4 * slots * ext * keys * 2 * channels,
            bytes_accessed=slots * ext * (channels + 8) * 8,
            transcendentals=slots * ext * keys,
        ),
        compiler_params=pltpu.CompilerParams(vmem_limit_bytes=32 << 20),
        name="match_part",
    )(info, *queries, *owns, *nexts, *chained)


def fused_call(info, queries, old, state, hide1, hide3, owns, nexts, last, weights, poses, inv_depth, total_rows, cols):
    slots, pix, channels = state.shape
    halo = 2 * cols
    ext = pix + 2 * halo
    keys = sum(part.shape[1] for part in owns)
    part_keys = sum(part.shape[1] for part in owns[len(owns) - last :])
    specs = Specs(slots, pix, channels, halo)
    dims = (slots, total_rows, pix // cols, cols, last, len(owns))
    wide = channels + 8
    return pl.pallas_call(
        functools.partial(fused_body, dims),
        grid_spec=pltpu.PrefetchScalarGridSpec(
            num_scalar_prefetch=1,
            grid=(slots,),
            in_specs=specs.queries()
            + [specs.slot(wide, ext), specs.slot(pix, channels), specs.slot(halo, channels), specs.slot(halo, channels)]
            + specs.parts(owns, 0)
            + specs.parts(nexts, 2)
            + [specs.whole(value.shape) for value in (*weights, poses, inv_depth)],
            out_specs=(
                specs.slot(pix, channels),
                specs.whole((8, 128)),
                specs.whole((32, 2 * pix)),
                specs.whole((2, pix)),
            ),
            scratch_shapes=[
                pltpu.VMEM((ext, channels), jnp.bfloat16),
                pltpu.VMEM((channels, ext), jnp.bfloat16),
                pltpu.VMEM((part_keys, channels), jnp.bfloat16),
                pltpu.VMEM((wide, part_keys), jnp.bfloat16),
                pltpu.VMEM((1, wide, ext), jnp.float32),
                pltpu.VMEM((keys, channels), jnp.bfloat16),
                pltpu.VMEM((wide, keys), jnp.bfloat16),
                pltpu.VMEM((ext, 6 * channels), jnp.bfloat16),
                pltpu.VMEM((ext, channels), jnp.bfloat16),
                pltpu.VMEM((8 * slots, pix), jnp.float32),
                pltpu.VMEM((8 * slots, 2 * pix), jnp.float32),
                pltpu.VMEM((8 * slots, 2 * pix), jnp.float32),
            ],
        ),
        out_shape=(
            jax.ShapeDtypeStruct((slots, pix, channels), jnp.bfloat16),
            jax.ShapeDtypeStruct((8, 128), jnp.float32),
            jax.ShapeDtypeStruct((32, 2 * pix), jnp.float32),
            jax.ShapeDtypeStruct((2, pix), jnp.float32),
        ),
        compiler_params=pltpu.CompilerParams(vmem_limit_bytes=40 << 20),
        name="match_update",
    )(info, *queries, old, state, hide1, hide3, *owns, *nexts, *weights, poses, inv_depth)


def shards(features, poses, inv_depth, hidden, edges, counts, w_gates, w_cand, w_head):
    slot_count, row_count, col_count, hid_width = hidden.shape
    channels = features.shape[3]
    node_rank = lax.axis_index(EDGE)
    pix_rank = lax.axis_index("x")
    total_rows = row_count * lax.axis_size("x")
    pix = row_count * col_count
    nodes = lax.axis_size(EDGE)
    halo = 2 * col_count
    info = jnp.concatenate([edges.reshape(-1), counts, jnp.stack([node_rank, pix_rank])]).astype(jnp.int32)

    def following(value):
        return lax.ppermute(value, EDGE, [(i + 1, i) for i in range(nodes - 1)])

    own = features.reshape(2, pix, channels)
    state = hidden.reshape(slot_count, pix, hid_width)
    own1, own3 = swapped(own, "x", 1), swapped(own, "x", 3)
    next0 = following(own)
    odd = pix_rank & 1
    send1 = lax.dynamic_slice_in_dim(state, (1 - odd) * (pix - halo), halo, axis=1)
    send3 = lax.dynamic_slice_in_dim(state, odd * (pix - halo), halo, axis=1)
    hide1, hide3 = swapped(send1, "x", 1), swapped(send3, "x", 3)
    half = pix // 2
    own2a = swapped(own1[:, :half], "x", 3)
    own2b = swapped(own3[:, half:], "x", 1)
    next1, next3 = following(own1), following(own3)
    next2a, next2b = following(own2a), following(own2b)
    queries = (own, own1, own3)
    first = match_call(info, slot_count, col_count, queries, (own,), (next0,), None)
    second = match_call(info, slot_count, col_count, queries, (own1, own3), (next1, next3), first)
    wg = w_gates.reshape(3, -1, w_gates.shape[2])
    wc = w_cand.reshape(3, -1, w_cand.shape[2])
    wc01 = jnp.concatenate([wc[0], wc[1]], axis=1)
    wh = jnp.concatenate([w_head, jnp.zeros_like(w_head)], axis=0)
    fresh, block, pull, scale = fused_call(
        info,
        queries,
        second,
        state,
        hide1,
        hide3,
        (own, own1, own3, own2a, own2b),
        (next0, next1, next3, next2a, next2b),
        2,
        (wg, wc01, wc[2], wh),
        poses,
        inv_depth,
        total_rows,
        col_count,
    )
    gathered = gathered_blocks(block)
    pose_update, depth_update = solve_call(info[2 * slot_count + 1 :], gathered, pull, scale)
    return (fresh.reshape(hidden.shape), pose_update, depth_update)


def solution(mesh):
    nodes, pix = mesh.devices.shape
    fine = Mesh(mesh.devices.reshape(nodes // 16, 8, 2, pix), EDGE + ("x",))
    placed = (
        P(EDGE, "x", None, None),
        P(),
        P(EDGE, "x"),
        P(EDGE, "x", None, None),
        P(EDGE, None),
        P(EDGE),
        P(),
        P(),
        P(),
    )
    return jax.shard_map(
        shards,
        mesh=fine,
        in_specs=placed,
        out_specs=(P(EDGE, "x", None, None), P(EDGE, None), P(EDGE, "x")),
        check_vma=False,
    )
```

profile of v0, /device:TPU:6, one launch (start us, length us, event | category | flops | bytes accessed | tf_op | source)
XLA Modules:
  0.0 163.7 jit_solution(14061156358623132556)
XLA Ops:
  0.6 0.0 copy-start
  0.6 0.9 collective-permute-start
  1.6 1.5 collective-permute-start.1
  3.0 1.3 collective-permute-start.4
  4.3 1.0 constant_dynamic-slice_fusion
  5.3 1.4 collective-permute-start.5
  6.7 0.8 copy.14
  7.5 0.1 reshape.31
  8.2 0.8 copy.15.refs_21_
  9.0 0.7 concatenate.12.refs_20_
  9.7 1.2 fusion.2
  10.9 2.0 %collective-permute-done.side1.refs_0_.refs_1_.refs_8_ = bf16[2,768,128]{2,1,0:T(8,128)(2,1)S(1)} collective-permute-done((bf16[2,768,128]{2,1,0:T(8,128)(2,1)}, bf16[2,768,128]{2,1,0:T(8,128)(2,1)S(1)}, u32[]{:S(2)}, u32[]{:S(2)}) %collective-permute-start) | collective-permute-done | bytes 393248 | tf_op jit(solution)/shard_map/ppermute | solution.py:21
  12.9 1.3 collective-permute-start.2
  14.2 0.0 collective-permute-done.1.side3.refs_1_.refs_2_.refs_9_
  14.2 1.3 collective-permute-start.3
  15.5 0.1 pad_add_fusion.info
  15.6 0.9 collective-permute-start.8
  16.6 0.0 collective-permute-done.4.refs_1_.refs_12_
  16.6 1.5 collective-permute-start.7
  18.1 0.0 copy-done
  18.1 4.2 %match_part.2.refs_4_ = f32[4,136,1024]{2,1,0:T(8,128)S(1)} custom-call(s32[11]{0:T(128)S(1)} %pad_add_fusion.info, bf16[2,768,128]{2,1,0:T(8,128)(2,1)S(1)} %bitcast.26, bf16[2,768,128]{2,1,0:T(8,128)(2,1)S(1)} %collective-permute-done.side1.refs_0_.refs_1_.refs_8_, bf16[2,768,128]{2,1,0:T(8,128)(2,1)S(1)} %collective-permute-done.1.side3.refs_1_.refs_2_.refs_9_, ...), custom_call_target="tpu_custom_call" | custom-call | flops 3221225472 | bytes 4456448 | tf_op jit(solution)/shard_map/match_part/pallas_call | solution.py:476
  22.3 0.5 collective-permute-done.8.refs_11_
  22.7 0.0 copy-start.1
  22.7 1.5 collective-permute-start.6
  24.3 1.0 collective-permute-done.7.refs_10_
  25.2 1.3 collective-permute-start.10
  26.5 0.0 collective-permute-done.2.refs_2_.refs_13_
  26.5 1.5 collective-permute-start.9
  28.0 0.0 collective-permute-done.3.refs_3_.refs_14_
  28.0 5.8 %match_part.3.refs_3_ = f32[4,136,1024]{2,1,0:T(8,128)S(1)} custom-call(s32[11]{0:T(128)S(1)} %pad_add_fusion.info, bf16[2,768,128]{2,1,0:T(8,128)(2,1)S(1)} %bitcast.28, bf16[2,768,128]{2,1,0:T(8,128)(2,1)S(1)} %collective-permute-done.side1.refs_0_.refs_1_.refs_8_, bf16[2,768,128]{2,1,0:T(8,128)(2,1)S(1)} %collective-permute-done.1.side3.refs_1_.refs_2_.refs_9_, ...), custom_call_target="tpu_custom_call" | custom-call | flops 6442450944 | bytes 4456448 | tf_op jit(solution)/shard_map/match_part/pallas_call | solution.py:476
  33.8 0.0 collective-permute-done.5.refs_5_
  33.8 0.0 collective-permute-done.6.refs_6_
  33.8 0.0 collective-permute-done.10.refs_16_
  33.8 0.0 collective-permute-done.9.refs_15_
  33.8 0.0 copy-done.1
  33.8 0.0 copy-done.2
  33.9 0.0 copy-done.4
  33.9 39.4 %match_update.1 = (bf16[4,768,128]{2,1,0:T(8,128)(2,1)}, f32[8,128]{1,0:T(8,128)S(1)}, f32[32,1536]{1,0:T(8,128)S(1)}, f32[2,768]{1,0:T(2,128)S(1)}) custom-call(s32[11]{0:T(128)S(1)} %pad_add_fusion.info, bf16[2,768,128]{2,1,0:T(8,128)(2,1)S(1)} %bitcast.29, bf16[2,768,128]{2,1,0:T(8,128)(2,1)S(1)} %collective-permute-done.side1.refs_0_.refs_1_.refs_8_, ...), custom_call_target="tpu_custom_call" | custom-call | tf_op jit(solution)/shard_map/match_update/pallas_call | solution.py:513
  73.3 0.7 copy-done.3
  73.9 0.6 copy-done.5
  74.5 0.0 collective-permute-start.11
  74.5 2.9 %collective-permute-start.12 = (f32[8,128]{1,0:T(8,128)S(1)}, f32[8,128]{1,0:T(8,128)S(1)}, u32[]{:S(2)}, u32[]{:S(2)}) collective-permute-start(f32[8,128]{1,0:T(8,128)S(1)} %get-tuple-element.10), channel_id=1, source_target_pairs={{0,2},{1,3},{2,0},{3,1},{4,6},{5,7},{6,4},{7,5},{8,10},{9,11},{10,... | collective-permute-start | bytes 12296 | tf_op jit(solution)/shard_map/ppermute | solution.py:21
  77.4 1.8 %collective-permute-start.13 = (f32[8,128]{1,0:T(8,128)S(1)}, f32[8,128]{1,0:T(8,128)S(1)}, u32[]{:S(2)}, u32[]{:S(2)}) collective-permute-start(f32[8,128]{1,0:T(8,128)S(1)} %get-tuple-element.10), channel_id=1, source_target_pairs={{0,3},{1,2},{2,1},{3,0},{4,7},{5,6},{6,5},{7,4},{8,11},{9,10},{10,... | collective-permute-start | bytes 12296 | tf_op jit(solution)/shard_map/ppermute | solution.py:21
  79.2 0.0 collective-permute-done.11
  79.2 0.4 collective-permute-done.12
  79.6 2.6 %collective-permute-done.13 = f32[8,128]{1,0:T(8,128)S(1)} collective-permute-done((f32[8,128]{1,0:T(8,128)S(1)}, f32[8,128]{1,0:T(8,128)S(1)}, u32[]{:S(2)}, u32[]{:S(2)}) %collective-permute-start.13) | collective-permute-done | bytes 4128 | tf_op jit(solution)/shard_map/ppermute | solution.py:21
  82.2 22.7 %all-gather = f32[16,128]{1,0:T(8,128)S(1)} all-gather(f32[8,128]{1,0:T(8,128)S(1)} %add_add_fusion), channel_id=2, replica_groups=mesh['y'=4,'z'=8,'core'=2,'x'=4] {'core'}, dimensions={0}, use_global_device_ids=true | all-gather | bytes 12288 | tf_op jit(solution)/shard_map/all_gather | solution.py:27
  104.9 4.6 %collective-permute-start.14 = (f32[2,8,128]{2,1,0:T(8,128)S(1)}, f32[2,8,128]{2,1,0:T(8,128)S(1)}, u32[]{:S(2)}, u32[]{:S(2)}) collective-permute-start(f32[2,8,128]{2,1,0:T(8,128)S(1)} %bitcast.41), channel_id=1, source_target_pairs={{0,8},{8,0},{16,24},{24,16},{32,40},{40,32},{48,56},{56,48},{1,9},... | collective-permute-start | bytes 24584 | tf_op jit(solution)/shard_map/ppermute | solution.py:21
  109.5 20.7 %collective-permute-start.15 = (f32[2,8,128]{2,1,0:T(8,128)S(1)}, f32[2,8,128]{2,1,0:T(8,128)S(1)}, u32[]{:S(2)}, u32[]{:S(2)}) collective-permute-start(f32[2,8,128]{2,1,0:T(8,128)S(1)} %bitcast.42), channel_id=1, source_target_pairs={{0,16},{8,24},{16,0},{24,8},{32,48},{40,56},{48,32},{56,40},{1,17}... | collective-permute-start | bytes 24584 | tf_op jit(solution)/shard_map/ppermute | solution.py:21
  130.1 1.5 collective-permute-start.16
  131.6 0.0 collective-permute-done.14
  131.6 0.1 collective-permute-done.15
  131.8 3.8 %collective-permute-done.16 = f32[2,8,128]{2,1,0:T(8,128)S(1)} collective-permute-done((f32[2,8,128]{2,1,0:T(8,128)S(1)}, f32[2,8,128]{2,1,0:T(8,128)S(1)}, u32[]{:S(2)}, u32[]{:S(2)}) %collective-permute-start.16) | collective-permute-done | bytes 8224 | tf_op jit(solution)/shard_map/ppermute | solution.py:21
  135.6 7.1 %collective-permute-start.17 = (f32[4,2,8,128]{3,2,1,0:T(8,128)S(1)}, f32[4,2,8,128]{3,2,1,0:T(8,128)S(1)}, u32[]{:S(2)}, u32[]{:S(2)}) collective-permute-start(f32[4,2,8,128]{3,2,1,0:T(8,128)S(1)} %get-tuple-element.23), channel_id=1, source_target_pairs={{0,32},{8,40},{16,48},{24,56},{32,0},{40,8},{48,16},{56,24},{1,33}... | collective-permute-start | bytes 98312 | tf_op jit(solution)/shard_map/ppermute | solution.py:21
  142.7 1.9 %collective-permute-done.17 = f32[4,2,8,128]{3,2,1,0:T(8,128)S(1)} collective-permute-done((f32[4,2,8,128]{3,2,1,0:T(8,128)S(1)}, f32[4,2,8,128]{3,2,1,0:T(8,128)S(1)}, u32[]{:S(2)}, u32[]{:S(2)}) %collective-permute-start.17) | collective-permute-done | bytes 32800 | tf_op jit(solution)/shard_map/ppermute | solution.py:21
  144.6 0.1 collective-permute-start.18
  144.7 6.6 %collective-permute-start.19 = (f32[2,4,2,8,128]{4,3,2,1,0:T(8,128)S(1)}, f32[2,4,2,8,128]{4,3,2,1,0:T(8,128)S(1)}, u32[]{:S(2)}, u32[]{:S(2)}) collective-permute-start(f32[2,4,2,8,128]{4,3,2,1,0:T(8,128)S(1)} %get-tuple-element.21), channel_id=1, source_target_pairs={{0,128},{64,192},{128,0},{192,64},{1,129},{65,193},{129,1},{193,65... | collective-permute-start | bytes 196616 | tf_op jit(solution)/shard_map/ppermute | solution.py:21
  151.4 0.5 collective-permute-start.20
  151.8 0.6 pad_add_fusion.1.info
  152.4 0.0 collective-permute-done.18
  152.4 1.8 %collective-permute-done.19 = f32[2,4,2,8,128]{4,3,2,1,0:T(8,128)S(1)} collective-permute-done((f32[2,4,2,8,128]{4,3,2,1,0:T(8,128)S(1)}, f32[2,4,2,8,128]{4,3,2,1,0:T(8,128)S(1)}, u32[]{:S(2)}, u32[]{:S(2)}) %collective-permute-start.19) | collective-permute-done | bytes 65568 | tf_op jit(solution)/shard_map/ppermute | solution.py:21
  154.2 2.6 %collective-permute-done.20 = f32[2,4,2,8,128]{4,3,2,1,0:T(8,128)S(1)} collective-permute-done((f32[2,4,2,8,128]{4,3,2,1,0:T(8,128)S(1)}, f32[2,4,2,8,128]{4,3,2,1,0:T(8,128)S(1)}, u32[]{:S(2)}, u32[]{:S(2)}) %collective-permute-start.20) | collective-permute-done | bytes 65568 | tf_op jit(solution)/shard_map/ppermute | solution.py:21
  156.8 0.7 pad_maximum_fusion.1
  157.5 6.1 %pose_solve.1 = (f32[2,6]{1,0:T(2,128)}, f32[2,768]{1,0:T(2,128)}) custom-call(s32[2]{0:T(128)} %pad_add_fusion.1.info, f32[64,8,128]{2,1,0:T(8,128)} %bitcast.35, f32[32,1536]{1,0:T(8,128)} %copy-done.3, f32[2,768]{1,0:T(2,128)} %copy-done.5), custom_call_target="tpu_custom_call" | custom-call | tf_op jit(solution)/shard_map/pose_solve/pallas_call | solution.py:215
  (10 shorter events, 0.1 us)
Async XLA Ops:
  0.6 17.4 %copy-start = (bf16[2,12,64,128]{3,2,1,0:T(8,128)(2,1)S(1)}, bf16[2,12,64,128]{3,2,1,0:T(8,128)(2,1)}, u32[]{:S(2)}) copy-start(bf16[2,12,64,128]{3,2,1,0:T(8,128)(2,1)} %param.9) | copy-start | bytes 1179652
  0.6 12.3 %collective-permute-start = (bf16[2,768,128]{2,1,0:T(8,128)(2,1)}, bf16[2,768,128]{2,1,0:T(8,128)(2,1)S(1)}, u32[]{:S(2)}, u32[]{:S(2)}) collective-permute-start(bf16[2,768,128]{2,1,0:T(8,128)(2,1)} %bitcast.23), channel_id=1, source_target_pairs={{0,1},{1,0},{2,3},{3,2},{4,5},{5,4},{6,7},{7,6},{8,9},{9,8},{10,11... | collective-permute-start | bytes 1179656 | tf_op jit(solution)/shard_map/ppermute | solution.py:21
  1.6 12.7 %collective-permute-start.1 = (bf16[2,768,128]{2,1,0:T(8,128)(2,1)}, bf16[2,768,128]{2,1,0:T(8,128)(2,1)S(1)}, u32[]{:S(2)}, u32[]{:S(2)}) collective-permute-start(bf16[2,768,128]{2,1,0:T(8,128)(2,1)} %bitcast.24), channel_id=1, source_target_pairs={{0,3},{1,2},{2,1},{3,0},{4,7},{5,6},{6,5},{7,4},{8,11},{9,10},{10,... | collective-permute-start | bytes 1179656 | tf_op jit(solution)/shard_map/ppermute | solution.py:21
  3.0 13.5 %collective-permute-start.4 = (bf16[2,768,128]{2,1,0:T(8,128)(2,1)}, bf16[2,768,128]{2,1,0:T(8,128)(2,1)S(1)}, u32[]{:S(2)}, u32[]{:S(2)}) collective-permute-start(bf16[2,768,128]{2,1,0:T(8,128)(2,1)} %bitcast.25), channel_id=1, source_target_pairs={{4,0},{8,4},{12,8},{16,12},{20,16},{24,20},{28,24},{32,28},{36,32}... | collective-permute-start | bytes 1179656 | tf_op jit(solution)/shard_map/ppermute | solution.py:567
  5.3 28.5 %collective-permute-start.5 = (bf16[4,128,128]{2,1,0:T(8,128)(2,1)S(1)}, bf16[4,128,128]{2,1,0:T(8,128)(2,1)S(1)}, u32[]{:S(2)}, u32[]{:S(2)}) collective-permute-start(bf16[4,128,128]{2,1,0:T(8,128)(2,1)S(1)} %get-tuple-element.16), channel_id=1, source_target_pairs={{0,1},{1,0},{2,3},{3,2},{4,5},{5,4},{6,7},{7,6},{8,9},{9,8},{10,11... | collective-permute-start | bytes 393224 | tf_op jit(solution)/shard_map/ppermute | solution.py:21
  12.9 13.6 %collective-permute-start.2 = (bf16[2,768,128]{2,1,0:T(8,128)(2,1)S(1)}, bf16[2,768,128]{2,1,0:T(8,128)(2,1)S(1)}, u32[]{:S(2)}, u32[]{:S(2)}) collective-permute-start(bf16[2,768,128]{2,1,0:T(8,128)(2,1)S(1)} %collective-permute-done.side1.refs_0_.refs_1_.refs_8_), channel_id=1, source_target_pairs={{4,0},{8,4},{12,8},{16,12},{20,16},{24,20},{28,24},{32,28},{36,32}... | collective-permute-start | bytes 1179656 | tf_op jit(solution)/shard_map/ppermute | solution.py:567
  14.2 13.8 %collective-permute-start.3 = (bf16[2,768,128]{2,1,0:T(8,128)(2,1)S(1)}, bf16[2,768,128]{2,1,0:T(8,128)(2,1)S(1)}, u32[]{:S(2)}, u32[]{:S(2)}) collective-permute-start(bf16[2,768,128]{2,1,0:T(8,128)(2,1)S(1)} %collective-permute-done.1.side3.refs_1_.refs_2_.refs_9_), channel_id=1, source_target_pairs={{4,0},{8,4},{12,8},{16,12},{20,16},{24,20},{28,24},{32,28},{36,32}... | collective-permute-start | bytes 1179656 | tf_op jit(solution)/shard_map/ppermute | solution.py:567
  15.6 7.1 %collective-permute-start.8 = (bf16[2,384,128]{2,1,0:T(8,128)(2,1)S(1)}, bf16[2,384,128]{2,1,0:T(8,128)(2,1)S(1)}, u32[]{:S(2)}, u32[]{:S(2)}) collective-permute-start(bf16[2,384,128]{2,1,0:T(8,128)(2,1)S(1)} %slice.24), channel_id=1, source_target_pairs={{0,1},{1,0},{2,3},{3,2},{4,5},{5,4},{6,7},{7,6},{8,9},{9,8},{10,11... | collective-permute-start | bytes 589832 | tf_op jit(solution)/shard_map/ppermute | solution.py:21
  16.6 8.6 %collective-permute-start.7 = (bf16[2,384,128]{2,1,0:T(8,128)(2,1)S(1)}, bf16[2,384,128]{2,1,0:T(8,128)(2,1)S(1)}, u32[]{:S(2)}, u32[]{:S(2)}) collective-permute-start(bf16[2,384,128]{2,1,0:T(8,128)(2,1)S(1)} %slice.23), channel_id=1, source_target_pairs={{0,3},{1,2},{2,1},{3,0},{4,7},{5,6},{6,5},{7,4},{8,11},{9,10},{10,... | collective-permute-start | bytes 589832 | tf_op jit(solution)/shard_map/ppermute | solution.py:21
  22.7 11.1 %copy-start.1 = (bf16[4,12,64,128]{3,2,1,0:T(8,128)(2,1)S(1)}, bf16[4,12,64,128]{3,2,1,0:T(8,128)(2,1)}, u32[]{:S(2)}) copy-start(bf16[4,12,64,128]{3,2,1,0:T(8,128)(2,1)} %param.12) | copy-start | bytes 2359300
  22.7 11.1 %copy-start.2 = (bf16[9,256,256]{2,1,0:T(8,128)(2,1)S(1)}, bf16[9,256,256]{2,1,0:T(8,128)(2,1)}, u32[]{:S(2)}) copy-start(bf16[9,256,256]{2,1,0:T(8,128)(2,1)} %param.15) | copy-start | bytes 3538948
  22.7 11.1 %copy-start.4 = (f32[2,768]{1,0:T(2,128)S(1)}, f32[2,768]{1,0:T(2,128)}, u32[]{:S(2)}) copy-start(f32[2,768]{1,0:T(2,128)} %refs_22_.1) | copy-start | bytes 18436
  22.7 11.1 %collective-permute-start.6 = (bf16[4,128,128]{2,1,0:T(8,128)(2,1)S(1)}, bf16[4,128,128]{2,1,0:T(8,128)(2,1)S(1)}, u32[]{:S(2)}, u32[]{:S(2)}) collective-permute-start(bf16[4,128,128]{2,1,0:T(8,128)(2,1)S(1)} %get-tuple-element.15), channel_id=1, source_target_pairs={{0,3},{1,2},{2,1},{3,0},{4,7},{5,6},{6,5},{7,4},{8,11},{9,10},{10,... | collective-permute-start | bytes 393224 | tf_op jit(solution)/shard_map/ppermute | solution.py:21
  25.2 8.6 %collective-permute-start.10 = (bf16[2,384,128]{2,1,0:T(8,128)(2,1)S(1)}, bf16[2,384,128]{2,1,0:T(8,128)(2,1)S(1)}, u32[]{:S(2)}, u32[]{:S(2)}) collective-permute-start(bf16[2,384,128]{2,1,0:T(8,128)(2,1)S(1)} %collective-permute-done.8.refs_11_), channel_id=1, source_target_pairs={{4,0},{8,4},{12,8},{16,12},{20,16},{24,20},{28,24},{32,28},{36,32}... | collective-permute-start | bytes 589832 | tf_op jit(solution)/shard_map/ppermute | solution.py:567
  26.5 7.3 %collective-permute-start.9 = (bf16[2,384,128]{2,1,0:T(8,128)(2,1)S(1)}, bf16[2,384,128]{2,1,0:T(8,128)(2,1)S(1)}, u32[]{:S(2)}, u32[]{:S(2)}) collective-permute-start(bf16[2,384,128]{2,1,0:T(8,128)(2,1)S(1)} %collective-permute-done.7.refs_10_), channel_id=1, source_target_pairs={{4,0},{8,4},{12,8},{16,12},{20,16},{24,20},{28,24},{32,28},{36,32}... | collective-permute-start | bytes 589832 | tf_op jit(solution)/shard_map/ppermute | solution.py:567
  73.3 0.7 copy-start.3
  73.9 0.6 copy-start.5
  74.5 4.7 %collective-permute-start.11 = (f32[8,128]{1,0:T(8,128)S(1)}, f32[8,128]{1,0:T(8,128)S(1)}, u32[]{:S(2)}, u32[]{:S(2)}) collective-permute-start(f32[8,128]{1,0:T(8,128)S(1)} %get-tuple-element.10), channel_id=1, source_target_pairs={{0,1},{1,0},{2,3},{3,2},{4,5},{5,4},{6,7},{7,6},{8,9},{9,8},{10,11... | collective-permute-start | bytes 12296 | tf_op jit(solution)/shard_map/ppermute | solution.py:21
  74.5 5.1 %collective-permute-start.12 = (f32[8,128]{1,0:T(8,128)S(1)}, f32[8,128]{1,0:T(8,128)S(1)}, u32[]{:S(2)}, u32[]{:S(2)}) collective-permute-start(f32[8,128]{1,0:T(8,128)S(1)} %get-tuple-element.10), channel_id=1, source_target_pairs={{0,2},{1,3},{2,0},{3,1},{4,6},{5,7},{6,4},{7,5},{8,10},{9,11},{10,... | collective-permute-start | bytes 12296 | tf_op jit(solution)/shard_map/ppermute | solution.py:21
  77.4 4.8 %collective-permute-start.13 = (f32[8,128]{1,0:T(8,128)S(1)}, f32[8,128]{1,0:T(8,128)S(1)}, u32[]{:S(2)}, u32[]{:S(2)}) collective-permute-start(f32[8,128]{1,0:T(8,128)S(1)} %get-tuple-element.10), channel_id=1, source_target_pairs={{0,3},{1,2},{2,1},{3,0},{4,7},{5,6},{6,5},{7,4},{8,11},{9,10},{10,... | collective-permute-start | bytes 12296 | tf_op jit(solution)/shard_map/ppermute | solution.py:21
  104.9 26.7 %collective-permute-start.14 = (f32[2,8,128]{2,1,0:T(8,128)S(1)}, f32[2,8,128]{2,1,0:T(8,128)S(1)}, u32[]{:S(2)}, u32[]{:S(2)}) collective-permute-start(f32[2,8,128]{2,1,0:T(8,128)S(1)} %bitcast.41), channel_id=1, source_target_pairs={{0,8},{8,0},{16,24},{24,16},{32,40},{40,32},{48,56},{56,48},{1,9},... | collective-permute-start | bytes 24584 | tf_op jit(solution)/shard_map/ppermute | solution.py:21
  109.5 22.3 %collective-permute-start.15 = (f32[2,8,128]{2,1,0:T(8,128)S(1)}, f32[2,8,128]{2,1,0:T(8,128)S(1)}, u32[]{:S(2)}, u32[]{:S(2)}) collective-permute-start(f32[2,8,128]{2,1,0:T(8,128)S(1)} %bitcast.42), channel_id=1, source_target_pairs={{0,16},{8,24},{16,0},{24,8},{32,48},{40,56},{48,32},{56,40},{1,17}... | collective-permute-start | bytes 24584 | tf_op jit(solution)/shard_map/ppermute | solution.py:21
  130.1 5.4 %collective-permute-start.16 = (f32[2,8,128]{2,1,0:T(8,128)S(1)}, f32[2,8,128]{2,1,0:T(8,128)S(1)}, u32[]{:S(2)}, u32[]{:S(2)}) collective-permute-start(f32[2,8,128]{2,1,0:T(8,128)S(1)} %bitcast.43), channel_id=1, source_target_pairs={{0,24},{8,16},{16,8},{24,0},{32,56},{40,48},{48,40},{56,32},{1,25}... | collective-permute-start | bytes 24584 | tf_op jit(solution)/shard_map/ppermute | solution.py:21
  135.6 9.0 %collective-permute-start.17 = (f32[4,2,8,128]{3,2,1,0:T(8,128)S(1)}, f32[4,2,8,128]{3,2,1,0:T(8,128)S(1)}, u32[]{:S(2)}, u32[]{:S(2)}) collective-permute-start(f32[4,2,8,128]{3,2,1,0:T(8,128)S(1)} %get-tuple-element.23), channel_id=1, source_target_pairs={{0,32},{8,40},{16,48},{24,56},{32,0},{40,8},{48,16},{56,24},{1,33}... | collective-permute-start | bytes 98312 | tf_op jit(solution)/shard_map/ppermute | solution.py:21
  144.6 7.8 %collective-permute-start.18 = (f32[2,4,2,8,128]{4,3,2,1,0:T(8,128)S(1)}, f32[2,4,2,8,128]{4,3,2,1,0:T(8,128)S(1)}, u32[]{:S(2)}, u32[]{:S(2)}) collective-permute-start(f32[2,4,2,8,128]{4,3,2,1,0:T(8,128)S(1)} %get-tuple-element.21), channel_id=1, source_target_pairs={{0,64},{64,0},{128,192},{192,128},{1,65},{65,1},{129,193},{193,129... | collective-permute-start | bytes 196616 | tf_op jit(solution)/shard_map/ppermute | solution.py:21
  144.7 9.5 %collective-permute-start.19 = (f32[2,4,2,8,128]{4,3,2,1,0:T(8,128)S(1)}, f32[2,4,2,8,128]{4,3,2,1,0:T(8,128)S(1)}, u32[]{:S(2)}, u32[]{:S(2)}) collective-permute-start(f32[2,4,2,8,128]{4,3,2,1,0:T(8,128)S(1)} %get-tuple-element.21), channel_id=1, source_target_pairs={{0,128},{64,192},{128,0},{192,64},{1,129},{65,193},{129,1},{193,65... | collective-permute-start | bytes 196616 | tf_op jit(solution)/shard_map/ppermute | solution.py:21
  151.4 5.5 %collective-permute-start.20 = (f32[2,4,2,8,128]{4,3,2,1,0:T(8,128)S(1)}, f32[2,4,2,8,128]{4,3,2,1,0:T(8,128)S(1)}, u32[]{:S(2)}, u32[]{:S(2)}) collective-permute-start(f32[2,4,2,8,128]{4,3,2,1,0:T(8,128)S(1)} %get-tuple-element.21), channel_id=1, source_target_pairs={{0,192},{64,128},{128,64},{192,0},{1,193},{65,129},{129,65},{193,1... | collective-permute-start | bytes 196616 | tf_op jit(solution)/shard_map/ppermute | solution.py:21
where the time goes:
time: 165 us; the launch traced here: 164 us
  starting transfers between devices  60 us (36%)
  Pallas kernels  55.5 us (34%)
  blocking collectives  22.7 us (14%)
  waiting for transfers between devices  16.7 us (10%)
  local copies, waits for them, and re-layouts  5.79 us (4%)
    ppermute x16, starting transfers between devices, swapped(): return lax.ppermute(value, axis, [(i, i ^ step) for i in range(count)])  53.4 us
    pallas_call x1, Pallas kernels, fused_call(): pl.pallas_call(functools.partial(fused_body, dims), grid_spec=pltpu.Prefe...  39.4 us
    all_gather x1, blocking collectives, gathered_blocks(): parts = lax.all_gather(block, 'core', axis=0)  22.7 us
    ppermute x16, waiting for transfers between devices, swapped(): return lax.ppermute(value, axis, [(i, i ^ step) for i in range(count)])  16.7 us
    pallas_call x2, Pallas kernels, match_call(): pl.pallas_call(functools.partial(match_body, (slots, len(owns), len(chain...  9.99 us
    ppermute x5, starting transfers between devices, following(): return lax.ppermute(value, EDGE, [(i + 1, i) for i in range(nodes - 1)])  6.61 us
    pallas_call x1, Pallas kernels, solve_call(): pl.pallas_call(functools.partial(solve_body, nodes, pix), out_shape=(jax....  6.11 us
  transfers between devices with their start and end apart: 21, of which 10 were waited for; matrix products, arithmetic and copies ran while one was open for 3% of the time, Pallas kernels for 6%

commit v1 on v0

--- a/solution.py
+++ b/solution.py
@@ -31,7 +31,7 @@
     return parts.reshape((-1,) + block.shape)
 
 
-def bundle_body(slots, rows_all, cols, info, poses, rho_ref, head, out, h_ref, dd_ref, a_ref, w_ref):
+def bundle_body(slots, rows_all, cols, info, poses, rho_ref, head, out, h_ref, h_out, a_ref, w_ref, sem):
     pix = rho_ref.shape[1]
     rows = pix // cols
     shift = cols.bit_length() - 1
@@ -82,18 +82,21 @@
         dd = conf_h * k_h * k_h + conf_v * k_v * k_v
         for f in range(2):
             pick = picks[s][f]
-            old = dd_ref[f : f + 1, :] if s else jnp.full((1, pix), DEPTH_DAMPING, jnp.float32)
-            dd_ref[f : f + 1, :] = old + pick * dd
+            at = slice(f * pix, (f + 1) * pix)
+            old = h_ref[32:33, at] if s else jnp.full((1, pix), DEPTH_DAMPING, jnp.float32)
+            h_ref[32:33, at] = old + pick * dd
             for g in range(4):
                 term = jnp.where(sub1 == 6, pick, pick * sels[s][g]) * k_s
                 at = (slice(8 * g, 8 * g + 8), slice(f * pix, (f + 1) * pix))
                 h_ref[at] = h_ref[at] + term if s else term
+    copy = pltpu.make_async_copy(h_ref, h_out, sem)
+    copy.start()
     nt = (((1,), (1,)), ((), ()))
     gram = lax.dot_general(w_ref[...], a_ref[...], nt, precision=PRECISE, preferred_element_type=jnp.float32)
     for f in range(2):
         at = slice(f * pix, (f + 1) * pix)
-        w_ref[:, at] = h_ref[:, at] * (1.0 / dd_ref[f : f + 1, :])
-    schur = lax.dot_general(w_ref[...], h_ref[...], nt, precision=PRECISE, preferred_element_type=jnp.float32)
+        w_ref[:, at] = h_ref[:32, at] * (1.0 / h_ref[32:33, at])
+    schur = lax.dot_general(w_ref[...], h_ref[:32, :], nt, precision=PRECISE, preferred_element_type=jnp.float32)
     pad = jnp.zeros((32, 96), jnp.float32)
     gram = jnp.concatenate([gram, pad], axis=1)
     schur = jnp.concatenate([schur, pad], axis=1)
@@ -117,6 +120,7 @@
         part = jnp.where(lanes < 32, part, 0.0)
         total = part if g == 0 else total + pltpu.roll(part, 32 * g, 1)
     out[...] = total
+    copy.wait()
 
 
 REAL = (0, 1, 2, 3, 4, 5, 8, 9, 10, 11, 12, 13)
@@ -144,7 +148,7 @@
     return diag, sides
 
 
-def solve_body(nodes, pix, info, g_ref, h_ref, dd_ref, pose_ref, depth_ref, t_ref, d_ref, l_ref, u_ref, near):
+def solve_body(nodes, pix, info, g_ref, h_ref, pose_ref, depth_ref, t_ref, d_ref, l_ref, u_ref, near):
     count = len(REAL)
     lane = lax.broadcasted_iota(jnp.int32, (16, 128), 1)
     sub = lax.broadcasted_iota(jnp.int32, (16, 128), 0)
@@ -204,13 +208,13 @@
     column = jnp.concatenate([own, after], axis=0)
     column = jnp.where(lax.broadcasted_iota(jnp.int32, (32, 1), 0) == 6, -1.0, column)
     for f in range(2):
-        pull = jnp.sum(h_ref[:, f * pix : (f + 1) * pix] * column, axis=0, keepdims=True)
-        depth_ref[f : f + 1, :] = -pull / dd_ref[f : f + 1, :]
-
-
-def solve_call(me, gathered, h, dd):
+        at = slice(f * pix, (f + 1) * pix)
+        depth_ref[f : f + 1, :] = -jnp.sum(h_ref[:32, at] * column, axis=0, keepdims=True) / h_ref[32:33, at]
+
+
+def solve_call(me, gathered, h):
     nodes = gathered.shape[0]
-    pix = dd.shape[1]
+    pix = h.shape[1] // 2
     vmem = pl.BlockSpec(memory_space=pltpu.VMEM)
     return pl.pallas_call(
         functools.partial(solve_body, nodes, pix),
@@ -218,7 +222,7 @@
             jax.ShapeDtypeStruct((2, 6), jnp.float32),
             jax.ShapeDtypeStruct((2, pix), jnp.float32),
         ),
-        in_specs=[pl.BlockSpec(memory_space=pltpu.SMEM), vmem, vmem, vmem],
+        in_specs=[pl.BlockSpec(memory_space=pltpu.SMEM), vmem, vmem],
         out_specs=(vmem, vmem),
         scratch_shapes=[
             pltpu.VMEM((nodes, 8, 128), jnp.float32),
@@ -228,16 +232,12 @@
             pltpu.VMEM((4, 12, 16, 128), jnp.float32),
         ],
         name="pose_solve",
-    )(me, gathered, h, dd)
+    )(me, gathered, h)
 
 
 NT = (((1,), (1,)), ((), ()))
 TILE = 256
 CHUNK = 768
-
-
-def gate(value):
-    return 0.5 * jnp.tanh(0.5 * value) + 0.5
 
 
 def spots(info, slots, pix, halo):
@@ -247,86 +247,118 @@
     return at1, at3
 
 
-def load_keys(near, owns, nexts, k_ref, vt_ref):
+def turned(value):
+    return value.astype(jnp.float32).T.astype(jnp.bfloat16)
+
+
+def load_keys(target, owns, nexts, k_ref, vt_ref):
     channels = k_ref.shape[1]
 
-    @pl.when(near)
+    @pl.when(target < 2)
     def _():
         base = 0
         for part in owns:
-            k_ref[base : base + part.shape[1], :] = part[0]
+            k_ref[base : base + part.shape[1], :] = part[target]
             base += part.shape[1]
 
-    @pl.when(jnp.logical_not(near))
+    @pl.when(target >= 2)
     def _():
         base = 0
         for part in nexts:
-            k_ref[base : base + part.shape[1], :] = part[0]
+            k_ref[base : base + part.shape[1], :] = part[target - 2]
             base += part.shape[1]
 
-    vt_ref[:channels, :] = k_ref[...].T
+    vt_ref[:channels, :] = turned(k_ref[...])
     vt_ref[channels:, :] = jnp.ones((vt_ref.shape[0] - channels, vt_ref.shape[1]), jnp.bfloat16)
 
 
-def add_keys(k_ref, vt_ref, qt_ref, acc_ref, old, factor):
-    keys, ext = k_ref.shape[0], qt_ref.shape[1]
-    for t in range(ext // TILE):
-        at = slice(t * TILE, (t + 1) * TILE)
-        acc = None if old is None else old[0, :, at]
-        for j in range(keys // CHUNK):
-            span = slice(j * CHUNK, (j + 1) * CHUNK)
-            s = jnp.dot(k_ref[span, :], qt_ref[:, at], preferred_element_type=jnp.float32)
-            p = jnp.exp2(s * factor).astype(jnp.bfloat16)
-            part = jnp.dot(vt_ref[:, span], p, preferred_element_type=jnp.float32)
-            acc = part if acc is None else acc + part
-        acc_ref[0, :, at] = acc
-
-
-def load_queries(info, slots, own_q, side1, side3, q_ref, qt_ref):
-    pix, halo = own_q.shape[1], side1.shape[1]
+def add_keys(slot, k_ref, vt_ref, qt_ref, old, factor, put):
+    chunks = k_ref.shape[0] // CHUNK
+    spots_t = [slice(t * TILE, (t + 1) * TILE) for t in range(qt_ref.shape[2] // TILE)]
+
+    def scores(j):
+        keys = k_ref[j * CHUNK : (j + 1) * CHUNK, :]
+        return [jnp.dot(keys, qt_ref[slot, :, at], preferred_element_type=jnp.float32) for at in spots_t]
+
+    held = scores(0)
+    sums = [None if old is None else old[slot, :, at] for at in spots_t]
+    for j in range(chunks):
+        later = scores(j + 1) if j + 1 < chunks else None
+        for t in range(len(spots_t)):
+            p = jnp.exp2(held[t] * factor).astype(jnp.bfloat16)
+            part = jnp.dot(vt_ref[:, j * CHUNK : (j + 1) * CHUNK], p, preferred_element_type=jnp.float32)
+            sums[t] = part if sums[t] is None else sums[t] + part
+        held = later
+    for at, value in zip(spots_t, sums):
+        put(at, value)
+
+
+def load_queries(info, slots, slot, own_q, side1, side3, qt_ref):
+    pix, halo = own_q.shape[1], qt_ref.shape[2] - own_q.shape[1]
+    halo = halo // 2
     at1, at3 = spots(info, slots, pix, halo)
-    q_ref[halo : halo + pix, :] = own_q[0]
-    q_ref[pl.ds(at1, halo), :] = side1[0]
-    q_ref[pl.ds(at3, halo), :] = side3[0]
-    qt_ref[...] = q_ref[...].T
+    odd = (info[2 * slots + 2] & 1) == 1
+    from1 = pl.multiple_of(jnp.where(odd, pix - halo, 0), halo)
+    from3 = pl.multiple_of(jnp.where(odd, 0, pix - halo), halo)
+    src = info[2 * slot] - 2 * info[2 * slots + 1]
+    qt_ref[slot, :, halo : halo + pix] = turned(own_q[src])
+    qt_ref[slot, :, pl.ds(at1, halo)] = turned(side1[src, pl.ds(from1, halo), :])
+    qt_ref[slot, :, pl.ds(at3, halo)] = turned(side3[src, pl.ds(from3, halo), :])
 
 
 def match_factor(channels):
     return 2.0 / math.sqrt(channels) * math.log2(math.e)
 
 
-def match_body(dims, info, own_q, side1, side3, *refs):
-    slots, parts, chained = dims
-    owns, refs = refs[:parts], refs[parts:]
-    nexts, refs = refs[:parts], refs[parts:]
-    old = refs[0] if chained else None
-    acc_ref, q_ref, qt_ref, k_ref, vt_ref = refs[chained:]
-    slot = pl.program_id(0)
-
-    @pl.when(slot < info[2 * slots])
-    def _():
-        near = info[2 * slot + 1] - 2 * info[2 * slots + 1] < 2
-        load_queries(info, slots, own_q, side1, side3, q_ref, qt_ref)
-        load_keys(near, owns, nexts, k_ref, vt_ref)
-        add_keys(k_ref, vt_ref, qt_ref, acc_ref, old, match_factor(q_ref.shape[1]))
+def first_body(slots, info, own_q, side1, side3, own, after, acc_ref, qt_ref, k_ref, vt_ref):
+    def one(slot, carry):
+        target = info[2 * slot + 1] - 2 * info[2 * slots + 1]
+        load_queries(info, slots, slot, own_q, side1, side3, qt_ref)
+        load_keys(target, (own,), (after,), k_ref, vt_ref)
+
+
+        def put(at, value):
+            acc_ref[slot, :, at] = value
+
+        add_keys(slot, k_ref, vt_ref, qt_ref, None, match_factor(k_ref.shape[1]), put)
+        return carry
+
+    lax.fori_loop(0, info[2 * slots], one, 0)
+
+
+def second_body(slots, parts, info, qt_ref, old, *refs):
+    owns, nexts = refs[:parts], refs[parts : 2 * parts]
+    acc_ref, k_ref, vt_ref = refs[2 * parts :]
+
+    def one(slot, carry):
+        target = info[2 * slot + 1] - 2 * info[2 * slots + 1]
+        load_keys(target, owns, nexts, k_ref, vt_ref)
+
+
+        def put(at, value):
+            acc_ref[slot, :, at] = value
+
+        add_keys(slot, k_ref, vt_ref, qt_ref, old, match_factor(k_ref.shape[1]), put)
+        return carry
+
+    lax.fori_loop(0, info[2 * slots], one, 0)
 
 
 def fused_body(dims, info, *refs):
     slots, total_rows, rows, cols, last, parts = dims
-    (own_q, side1, side3, old), refs = refs[:4], refs[4:]
+    (qt_ref, old), refs = refs[:2], refs[2:]
     (state, hide1, hide3), refs = refs[:3], refs[3:]
     owns, refs = refs[:parts], refs[parts:]
     nexts, refs = refs[:parts], refs[parts:]
     (wg, wc01, wc2, wh, poses, rho_ref), refs = refs[:6], refs[6:]
-    (fresh_ref, block_ref, pull_ref, scale_ref), refs = refs[:4], refs[4:]
-    q_ref, qt_ref, k_ref, vt_ref, acc_ref, kall_ref, vtall_ref, x_ref, h_ref, head_ref, a_ref, w_ref = refs
-    slot = pl.program_id(0)
-    live = slot < info[2 * slots]
+    (fresh_out, block_ref, pull_out), refs = refs[:3], refs[3:]
+    fresh_ref, pull_ref, k_ref, vt_ref, acc_ref, kall_ref, vtall_ref, x_ref, h_ref = refs[:9]
+    head_ref, a_ref, w_ref, sems = refs[9:]
     pix_rank = info[2 * slots + 2]
     pix = rows * cols
     halo = 2 * cols
     ext = pix + 2 * halo
-    channels = own_q.shape[-1]
+    channels = state.shape[-1]
     factor = match_factor(channels)
     at1, at3 = spots(info, slots, pix, halo)
     px = lax.broadcasted_iota(jnp.int32, (ext, 1), 0)
@@ -337,28 +369,36 @@
 
     valid = inside(px)
 
-    @pl.when(jnp.logical_not(live))
-    def _():
-        fresh_ref[...] = state[...]
+    def send(slot):
+        return pltpu.make_async_copy(fresh_ref.at[slot], fresh_out.at[slot], sems.at[slot])
+
+    def keep(slot, carry):
+        fresh_ref[slot] = state[slot]
         head_ref[pl.ds(pl.multiple_of(8 * slot, 8), 8), :] = jnp.zeros((8, pix), jnp.float32)
-
-    @pl.when(live)
-    def _():
-        near = info[2 * slot + 1] - 2 * info[2 * slots + 1] < 2
-        load_queries(info, slots, own_q, side1, side3, q_ref, qt_ref)
-        load_keys(near, owns[parts - last :], nexts[parts - last :], k_ref, vt_ref)
-        add_keys(k_ref, vt_ref, qt_ref, acc_ref, old, factor)
+        send(slot).start()
+        return carry
+
+    lax.fori_loop(info[2 * slots], slots, keep, 0)
+
+    def one(slot, carry):
+        target = info[2 * slot + 1] - 2 * info[2 * slots + 1]
+        load_keys(target, owns[parts - last :], nexts[parts - last :], k_ref, vt_ref)
+
+        def put(at, value):
+            acc_ref[0, :, at] = value
+
+        add_keys(slot, k_ref, vt_ref, qt_ref, old, factor, put)
         sums = acc_ref[0, channels : channels + 1, :]
         fits = (jnp.min(sums) > 1e-20) & (jnp.max(sums) < 1e25)
 
         @pl.when(jnp.logical_not(fits))
         def _():
-            load_keys(near, owns, nexts, kall_ref, vtall_ref)
+            load_keys(target, owns, nexts, kall_ref, vtall_ref)
             chunks = kall_ref.shape[0] // CHUNK
 
             def exact(t, carry):
                 at = pl.ds(pl.multiple_of(t * TILE, TILE), TILE)
-                q = qt_ref[:, at]
+                q = qt_ref[slot, :, at]
 
                 def scores(j):
                     span = pl.ds(pl.multiple_of(j * CHUNK, CHUNK), CHUNK)
@@ -383,9 +423,9 @@
 
             lax.fori_loop(0, ext // TILE, exact, 0)
 
-        h_ref[halo : halo + pix, :] = state[0]
-        h_ref[pl.ds(at1, halo), :] = hide1[0]
-        h_ref[pl.ds(at3, halo), :] = hide3[0]
+        h_ref[halo : halo + pix, :] = state[slot]
+        h_ref[pl.ds(at1, halo), :] = hide1[slot]
+        h_ref[pl.ds(at3, halo), :] = hide3[slot]
         col = px & (cols - 1)
         first, final = col == 0, col == cols - 1
 
@@ -408,148 +448,106 @@
             part = jnp.dot(x_ref[r * cols : r * cols + mid, :], wg[r], preferred_element_type=jnp.float32)
             gates = part if r == 0 else gates + part
         inner = slice(cols, cols + mid)
-        spread(gate(gates[:, channels:]) * wide[inner], inner, 0)
+        spread(jax.nn.sigmoid(gates[:, channels:]) * wide[inner], inner, 0)
         pair = jnp.dot(x_ref[cols : 2 * cols + pix, :], wc01[...], preferred_element_type=jnp.float32)
         cand = jnp.dot(x_ref[3 * cols : 3 * cols + pix, :], wc2[...], preferred_element_type=jnp.float32)
         cand = cand + pair[:pix, :channels] + pair[cols : cols + pix, channels:]
-        update = gate(gates[cols : cols + pix, :channels])
+        update = jax.nn.sigmoid(gates[cols : cols + pix, :channels])
         kept = wide[halo : halo + pix]
         fresh = ((1.0 - update) * kept + update * jnp.tanh(cand)).astype(jnp.bfloat16)
-        fresh_ref[0] = fresh
+        fresh_ref[slot] = fresh
         head = lax.dot_general(wh[...], fresh, NT, preferred_element_type=jnp.float32)
         head_ref[pl.ds(pl.multiple_of(8 * slot, 8), 8), :] = head
-
-    @pl.when(slot == slots - 1)
-    def _():
-        bundle_body(
-            slots, total_rows, cols, info, poses, rho_ref, head_ref, block_ref, pull_ref, scale_ref, a_ref, w_ref
-        )
-
-
-class Specs:
-    def __init__(self, slots, pix, channels, halo):
-        self.slots, self.pix, self.channels, self.halo = slots, pix, channels, halo
-        self.at = 2 * slots + 1
-
-    def source(self, s, info):
-        return jnp.clip(info[2 * s] - 2 * info[self.at], 0, 1)
-
-    def target(self, s, info):
-        return info[2 * s + 1] - 2 * info[self.at]
-
-    def side(self, flip):
-        far = self.pix // self.halo - 1
-
-        def index(s, info):
-            low = (info[self.at + 1] & 1) == flip
-            return (self.source(s, info), jnp.where(low, far, 0), 0)
-
-        return pl.BlockSpec((1, self.halo, self.channels), index)
-
-    def queries(self):
-        main = pl.BlockSpec((1, self.pix, self.channels), lambda s, info: (self.source(s, info), 0, 0))
-        return [main, self.side(1), self.side(0)]
-
-    def parts(self, parts, base):
-        return [
-            pl.BlockSpec(
-                (1, part.shape[1], self.channels),
-                lambda s, info: (jnp.clip(self.target(s, info) - base, 0, 1), 0, 0),
-            )
-            for part in parts
-        ]
-
-    def slot(self, rows, lanes):
-        return pl.BlockSpec((1, rows, lanes), lambda s, info: (s, 0, 0))
-
-    def whole(self, shape):
-        return pl.BlockSpec(shape, lambda s, info: (0,) * len(shape))
-
-
-def match_call(info, slots, cols, queries, owns, nexts, old):
-    pix, channels = queries[0].shape[1:]
-    halo = 2 * cols
-    ext = pix + 2 * halo
+        send(slot).start()
+        return carry
+
+    lax.fori_loop(0, info[2 * slots], one, 0)
+    bundle_body(
+        slots, total_rows, cols, info, poses, rho_ref, head_ref, block_ref, pull_ref, pull_out, a_ref, w_ref, sems.at[slots]
+    )
+    for slot in range(slots):
+        send(slot).wait()
+
+
+VMEM = pl.BlockSpec(memory_space=pltpu.VMEM)
+SMEM = pl.BlockSpec(memory_space=pltpu.SMEM)
+
+
+def work(slots, ext, keys, channels):
+    return pl.CostEstimate(
+        flops=4 * slots * ext * keys * 2 * channels,
+        bytes_accessed=slots * ext * (channels + 8) * 8,
+        transcendentals=slots * ext * keys,
+    )
+
+
+def first_call(info, slots, cols, queries, own, after):
+    pix, channels = own.shape[1:]
+    ext = pix + 4 * cols
+    return pl.pallas_call(
+        functools.partial(first_body, slots),
+        in_specs=[SMEM] + [VMEM] * 5,
+        out_specs=(VMEM, VMEM),
+        scratch_shapes=[pltpu.VMEM((pix, channels), jnp.bfloat16), pltpu.VMEM((channels + 8, pix), jnp.bfloat16)],
+        out_shape=(
+            jax.ShapeDtypeStruct((slots, channels + 8, ext), jnp.float32),
+            jax.ShapeDtypeStruct((slots, channels, ext), jnp.bfloat16),
+        ),
+        cost_estimate=work(slots, ext, pix, channels),
+        compiler_params=pltpu.CompilerParams(vmem_limit_bytes=14 << 20),
+        name="match_first",
+    )(info, *queries, own, after)
+
+
+def second_call(info, qt, old, owns, nexts):
+    slots, channels, ext = qt.shape
     keys = sum(part.shape[1] for part in owns)
-    specs = Specs(slots, pix, channels, halo)
-    chained = () if old is None else (old,)
     return pl.pallas_call(
-        functools.partial(match_body, (slots, len(owns), len(chained))),
-        grid_spec=pltpu.PrefetchScalarGridSpec(
-            num_scalar_prefetch=1,
-            grid=(slots,),
-            in_specs=specs.queries()
-            + specs.parts(owns, 0)
-            + specs.parts(nexts, 2)
-            + [specs.slot(channels + 8, ext) for _ in chained],
-            out_specs=specs.slot(channels + 8, ext),
-            scratch_shapes=[
-                pltpu.VMEM((ext, channels), jnp.bfloat16),
-                pltpu.VMEM((channels, ext), jnp.bfloat16),
-                pltpu.VMEM((keys, channels), jnp.bfloat16),
-                pltpu.VMEM((channels + 8, keys), jnp.bfloat16),
-            ],
-        ),
-        out_shape=jax.ShapeDtypeStruct((slots, channels + 8, ext), jnp.float32),
-        cost_estimate=pl.CostEstimate(
-            flops=4 * slots * ext * keys * 2 * channels,
-            bytes_accessed=slots * ext * (channels + 8) * 8,
-            transcendentals=slots * ext * keys,
-        ),
-        compiler_params=pltpu.CompilerParams(vmem_limit_bytes=32 << 20),
-        name="match_part",
-    )(info, *queries, *owns, *nexts, *chained)
-
-
-def fused_call(info, queries, old, state, hide1, hide3, owns, nexts, last, weights, poses, inv_depth, total_rows, cols):
+        functools.partial(second_body, slots, len(owns)),
+        in_specs=[SMEM] + [VMEM] * (2 + 2 * len(owns)),
+        out_specs=VMEM,
+        scratch_shapes=[pltpu.VMEM((keys, channels), jnp.bfloat16), pltpu.VMEM((channels + 8, keys), jnp.bfloat16)],
+        out_shape=jax.ShapeDtypeStruct(old.shape, jnp.float32),
+        cost_estimate=work(slots, ext, keys, channels),
+        compiler_params=pltpu.CompilerParams(vmem_limit_bytes=14 << 20),
+        name="match_second",
+    )(info, qt, old, *owns, *nexts)
+
+
+def fused_call(info, qt, old, state, hide1, hide3, owns, nexts, last, weights, poses, inv_depth, total_rows, cols):
     slots, pix, channels = state.shape
-    halo = 2 * cols
-    ext = pix + 2 * halo
+    ext = qt.shape[2]
     keys = sum(part.shape[1] for part in owns)
     part_keys = sum(part.shape[1] for part in owns[len(owns) - last :])
-    specs = Specs(slots, pix, channels, halo)
     dims = (slots, total_rows, pix // cols, cols, last, len(owns))
     wide = channels + 8
     return pl.pallas_call(
         functools.partial(fused_body, dims),
-        grid_spec=pltpu.PrefetchScalarGridSpec(
-            num_scalar_prefetch=1,
-            grid=(slots,),
-            in_specs=specs.queries()
-            + [specs.slot(wide, ext), specs.slot(pix, channels), specs.slot(halo, channels), specs.slot(halo, channels)]
-            + specs.parts(owns, 0)
-            + specs.parts(nexts, 2)
-            + [specs.whole(value.shape) for value in (*weights, poses, inv_depth)],
-            out_specs=(
-                specs.slot(pix, channels),
-                specs.whole((8, 128)),
-                specs.whole((32, 2 * pix)),
-                specs.whole((2, pix)),
-            ),
-            scratch_shapes=[
-                pltpu.VMEM((ext, channels), jnp.bfloat16),
-                pltpu.VMEM((channels, ext), jnp.bfloat16),
-                pltpu.VMEM((part_keys, channels), jnp.bfloat16),
-                pltpu.VMEM((wide, part_keys), jnp.bfloat16),
-                pltpu.VMEM((1, wide, ext), jnp.float32),
-                pltpu.VMEM((keys, channels), jnp.bfloat16),
-                pltpu.VMEM((wide, keys), jnp.bfloat16),
-                pltpu.VMEM((ext, 6 * channels), jnp.bfloat16),
-                pltpu.VMEM((ext, channels), jnp.bfloat16),
-                pltpu.VMEM((8 * slots, pix), jnp.float32),
-                pltpu.VMEM((8 * slots, 2 * pix), jnp.float32),
-                pltpu.VMEM((8 * slots, 2 * pix), jnp.float32),
-            ],
-        ),
+        in_specs=[SMEM] + [VMEM] * (5 + 2 * len(owns) + len(weights) + 2),
+        out_specs=(pl.BlockSpec(memory_space=pltpu.HBM), VMEM, pl.BlockSpec(memory_space=pltpu.HBM)),
+        scratch_shapes=[
+            pltpu.VMEM((slots, pix, channels), jnp.bfloat16),
+            pltpu.VMEM((40, 2 * pix), jnp.float32),
+            pltpu.VMEM((part_keys, channels), jnp.bfloat16),
+            pltpu.VMEM((wide, part_keys), jnp.bfloat16),
+            pltpu.VMEM((1, wide, ext), jnp.float32),
+            pltpu.VMEM((keys, channels), jnp.bfloat16),
+            pltpu.VMEM((wide, keys), jnp.bfloat16),
+            pltpu.VMEM((ext, 6 * channels), jnp.bfloat16),
+            pltpu.VMEM((ext, channels), jnp.bfloat16),
+            pltpu.VMEM((8 * slots, pix), jnp.float32),
+            pltpu.VMEM((8 * slots, 2 * pix), jnp.float32),
+            pltpu.VMEM((8 * slots, 2 * pix), jnp.float32),
+            pltpu.SemaphoreType.DMA((slots + 1,)),
+        ],
         out_shape=(
             jax.ShapeDtypeStruct((slots, pix, channels), jnp.bfloat16),
             jax.ShapeDtypeStruct((8, 128), jnp.float32),
-            jax.ShapeDtypeStruct((32, 2 * pix), jnp.float32),
-            jax.ShapeDtypeStruct((2, pix), jnp.float32),
+            jax.ShapeDtypeStruct((40, 2 * pix), jnp.float32),
         ),
-        compiler_params=pltpu.CompilerParams(vmem_limit_bytes=40 << 20),
+        compiler_params=pltpu.CompilerParams(vmem_limit_bytes=26 << 20),
         name="match_update",
-    )(info, *queries, old, state, hide1, hide3, *owns, *nexts, *weights, poses, inv_depth)
+    )(info, qt, old, state, hide1, hide3, *owns, *nexts, *weights, poses, inv_depth)
 
 
 def shards(features, poses, inv_depth, hidden, edges, counts, w_gates, w_cand, w_head):
@@ -580,16 +578,16 @@
     next1, next3 = following(own1), following(own3)
     next2a, next2b = following(own2a), following(own2b)
     queries = (own, own1, own3)
-    first = match_call(info, slot_count, col_count, queries, (own,), (next0,), None)
-    second = match_call(info, slot_count, col_count, queries, (own1, own3), (next1, next3), first)
+    acc, turned = first_call(info, slot_count, col_count, queries, own, next0)
+    acc = second_call(info, turned, acc, (own1, own3), (next1, next3))
     wg = w_gates.reshape(3, -1, w_gates.shape[2])
     wc = w_cand.reshape(3, -1, w_cand.shape[2])
     wc01 = jnp.concatenate([wc[0], wc[1]], axis=1)
     wh = jnp.concatenate([w_head, jnp.zeros_like(w_head)], axis=0)
-    fresh, block, pull, scale = fused_call(
+    fresh, block, pull = fused_call(
         info,
-        queries,
-        second,
+        turned,
+        acc,
         state,
         hide1,
         hide3,
@@ -603,7 +601,7 @@
         col_count,
     )
     gathered = gathered_blocks(block)
-    pose_update, depth_update = solve_call(info[2 * slot_count + 1 :], gathered, pull, scale)
+    pose_update, depth_update = solve_call(info[2 * slot_count + 1 :], gathered, pull)
     return (fresh.reshape(hidden.shape), pose_update, depth_update)
 
 

time: 165 us -> 151 us (0.915)
  Pallas kernels: 55.5 us -> 28.8 us
  waiting for transfers between devices: 16.7 us -> 27.2 us
  starting transfers between devices: 60 us -> 65.1 us
    pallas_call x3, Pallas kernels: 49.4 us -> 22.8 us  [the longest x1 19.2 us: fused_call(): pl.pallas_call(functools.partial(fused_body, dims), in_specs=[SMEM] + [VM...]
    ppermute x16, waiting for transfers between devices: 16.7 us -> 26.9 us  [swapped(): return lax.ppermute(value, axis, [(i, i ^ step) for i in range(count)])]
    ppermute x16, starting transfers between devices: 53.4 us -> 58.7 us  [swapped(): return lax.ppermute(value, axis, [(i, i ^ step) for i in range(count)])]
  transfers between devices with their start and end apart: 21 -> 21, of which waited for: 10 -> 12; matrix products, arithmetic and copies ran while one was open for 3% -> 4% of each run, Pallas kernels for 6% -> 2%
where the time goes in v1:
time: 151 us
  starting transfers between devices  65.1 us (43%)
  Pallas kernels  28.8 us (19%)
  waiting for transfers between devices  27.2 us (18%)
  blocking collectives  21.8 us (14%)
  local copies, waits for them, and re-layouts  5.23 us (3%)
  other arithmetic  1.52 us (1%)
    ppermute x16, starting transfers between devices, swapped(): return lax.ppermute(value, axis, [(i, i ^ step) for i in range(count)])  58.7 us
    ppermute x16, waiting for transfers between devices, swapped(): return lax.ppermute(value, axis, [(i, i ^ step) for i in range(count)])  26.9 us
    all_gather x1, blocking collectives, gathered_blocks(): parts = lax.all_gather(block, 'core', axis=0)  21.8 us
    pallas_call x1, Pallas kernels, fused_call(): pl.pallas_call(functools.partial(fused_body, dims), in_specs=[SMEM] + [VM...  19.2 us
    ppermute x5, starting transfers between devices, following(): return lax.ppermute(value, EDGE, [(i + 1, i) for i in range(nodes - 1)])  6.43 us
    pallas_call x1, Pallas kernels, solve_call(): pl.pallas_call(functools.partial(solve_body, nodes, pix), out_shape=(jax....  6.06 us
  transfers between devices with their start and end apart: 21, of which 12 were waited for; matrix products, arithmetic and copies ran while one was open for 4% of the time, Pallas kernels for 2%

profile of v1, /device:TPU:6, one launch (start us, length us, event | category | flops | bytes accessed | tf_op | source)
XLA Modules:
  0.0 151.2 jit_solution(13906675865434239299)
XLA Ops:
  0.6 0.0 copy-start.2
  0.6 0.9 collective-permute-start
  1.6 1.5 collective-permute-start.1
  3.0 1.3 collective-permute-start.2
  4.3 1.0 constant_dynamic-slice_fusion
  5.3 1.4 collective-permute-start.5
  6.7 0.8 copy.14
  7.5 0.1 reshape.31
  8.2 0.8 copy.15.refs_19_
  9.0 0.7 concatenate.12.refs_18_
  9.7 1.2 fusion.2
  10.9 2.0 %collective-permute-done.side1.refs_0_.refs_6_ = bf16[2,768,128]{2,1,0:T(8,128)(2,1)S(1)} collective-permute-done((bf16[2,768,128]{2,1,0:T(8,128)(2,1)}, bf16[2,768,128]{2,1,0:T(8,128)(2,1)S(1)}, u32[]{:S(2)}, u32[]{:S(2)}) %collective-permute-start) | collective-permute-done | bytes 393248 | tf_op jit(solution)/shard_map/ppermute | solution.py:21
  12.9 1.3 collective-permute-start.3
  14.2 0.0 collective-permute-done.1.side3.refs_1_.refs_7_
  14.2 1.3 collective-permute-start.4
  15.5 0.1 pad_add_fusion.info
  15.6 0.9 collective-permute-start.8
  16.6 0.0 collective-permute-done.2.after.refs_10_
  16.6 1.5 collective-permute-start.7
  18.1 0.0 copy-done.2
  18.1 1.5 %match_first.1 = (f32[4,136,1024]{2,1,0:T(8,128)S(1)}, bf16[4,128,1024]{2,1,0:T(8,128)(2,1)S(1)}) custom-call(s32[11]{0:T(128)S(1)} %pad_add_fusion.info, bf16[2,768,128]{2,1,0:T(8,128)(2,1)S(1)} %bitcast.30, bf16[2,768,128]{2,1,0:T(8,128)(2,1)S(1)} %collective-permute-done.side1.refs_0_.refs_6_, ...), custom_call_target="tpu_custom_call" | custom-call | flops 3221225472 | bytes 4456448 | tf_op jit(solution)/shard_map/match_first/pallas_call | solution.py:487
  19.6 3.2 %collective-permute-done.8.refs_9_ = bf16[2,384,128]{2,1,0:T(8,128)(2,1)S(1)} collective-permute-done((bf16[2,384,128]{2,1,0:T(8,128)(2,1)S(1)}, bf16[2,384,128]{2,1,0:T(8,128)(2,1)S(1)}, u32[]{:S(2)}, u32[]{:S(2)}) %collective-permute-start.8) | collective-permute-done | bytes 196640 | tf_op jit(solution)/shard_map/ppermute | solution.py:21
  22.7 0.4 collective-permute-start.6
  23.1 2.1 %collective-permute-done.7.refs_8_ = bf16[2,384,128]{2,1,0:T(8,128)(2,1)S(1)} collective-permute-done((bf16[2,384,128]{2,1,0:T(8,128)(2,1)S(1)}, bf16[2,384,128]{2,1,0:T(8,128)(2,1)S(1)}, u32[]{:S(2)}, u32[]{:S(2)}) %collective-permute-start.7) | collective-permute-done | bytes 196640 | tf_op jit(solution)/shard_map/ppermute | solution.py:21
  25.2 1.3 collective-permute-start.10
  26.5 0.0 collective-permute-done.3.refs_2_.refs_11_
  26.5 1.3 collective-permute-start.9
  27.8 0.0 collective-permute-done.4.refs_3_.refs_12_
  27.8 0.0 copy-start
  27.8 0.0 copy-start.1
  27.8 0.0 copy-start.4
  27.9 2.1 %match_second.1.refs_1_ = f32[4,136,1024]{2,1,0:T(8,128)S(1)} custom-call(s32[11]{0:T(128)S(1)} %pad_add_fusion.info, bf16[4,128,1024]{2,1,0:T(8,128)(2,1)S(1)} %get-tuple-element.10.qt_ref.refs_0_, f32[4,136,1024]{2,1,0:T(8,128)S(1)} %get-tuple-element.11.old, bf16[2,768,128]{2,1,0:T(8,128)(2,1)S(1)} %collective-permute-done.side1.refs_0_.refs_6_, ...), custom_call_target="tpu_custom_call" | custom-call | flops 6442450944 | bytes 4456448 | tf_op jit(solution)/shard_map/match_second/pallas_call | solution.py:505
  29.9 0.0 collective-permute-done.5.refs_3_
  29.9 0.3 collective-permute-done.6.refs_4_
  30.2 0.0 collective-permute-done.10.refs_14_
  30.2 0.2 collective-permute-done.9.refs_13_
  30.5 0.0 copy-done
  30.5 0.0 copy-done.1
  30.5 19.2 %match_update.1 = (bf16[4,768,128]{2,1,0:T(8,128)(2,1)}, f32[8,128]{1,0:T(8,128)S(1)}, f32[40,1536]{1,0:T(8,128)S(1)}) custom-call(s32[11]{0:T(128)S(1)} %pad_add_fusion.info, bf16[4,128,1024]{2,1,0:T(8,128)(2,1)S(1)} %get-tuple-element.10.qt_ref.refs_0_, f32[4,136,1024]{2,1,0:T(8,128)S(1)} %match_second.1.refs_1_, bf16[4,768,128]{2,1,0:T(8,128)(2,1)S(1)} %bitcast.24, ...), custom_call_target="tpu_custom_call" | custom-call | tf_op jit(solution)/shard_map/match_update/pallas_call | solution.py:524
  49.7 0.7 copy-done.3
  50.4 0.0 collective-permute-start.11
  50.4 2.9 %collective-permute-start.12 = (f32[8,128]{1,0:T(8,128)S(1)}, f32[8,128]{1,0:T(8,128)S(1)}, u32[]{:S(2)}, u32[]{:S(2)}) collective-permute-start(f32[8,128]{1,0:T(8,128)S(1)} %get-tuple-element.13), channel_id=1, source_target_pairs={{0,2},{1,3},{2,0},{3,1},{4,6},{5,7},{6,4},{7,5},{8,10},{9,11},{10,... | collective-permute-start | bytes 12296 | tf_op jit(solution)/shard_map/ppermute | solution.py:21
  53.3 1.8 %collective-permute-start.13 = (f32[8,128]{1,0:T(8,128)S(1)}, f32[8,128]{1,0:T(8,128)S(1)}, u32[]{:S(2)}, u32[]{:S(2)}) collective-permute-start(f32[8,128]{1,0:T(8,128)S(1)} %get-tuple-element.13), channel_id=1, source_target_pairs={{0,3},{1,2},{2,1},{3,0},{4,7},{5,6},{6,5},{7,4},{8,11},{9,10},{10,... | collective-permute-start | bytes 12296 | tf_op jit(solution)/shard_map/ppermute | solution.py:21
  55.1 0.0 collective-permute-done.11
  55.1 0.4 collective-permute-done.12
  55.5 2.6 %collective-permute-done.13 = f32[8,128]{1,0:T(8,128)S(1)} collective-permute-done((f32[8,128]{1,0:T(8,128)S(1)}, f32[8,128]{1,0:T(8,128)S(1)}, u32[]{:S(2)}, u32[]{:S(2)}) %collective-permute-start.13) | collective-permute-done | bytes 4128 | tf_op jit(solution)/shard_map/ppermute | solution.py:21
  58.1 21.8 %all-gather = f32[16,128]{1,0:T(8,128)S(1)} all-gather(f32[8,128]{1,0:T(8,128)S(1)} %add_add_fusion), channel_id=2, replica_groups=mesh['y'=4,'z'=8,'core'=2,'x'=4] {'core'}, dimensions={0}, use_global_device_ids=true | all-gather | bytes 12288 | tf_op jit(solution)/shard_map/all_gather | solution.py:27
  79.9 2.1 %collective-permute-start.14 = (f32[2,8,128]{2,1,0:T(8,128)S(1)}, f32[2,8,128]{2,1,0:T(8,128)S(1)}, u32[]{:S(2)}, u32[]{:S(2)}) collective-permute-start(f32[2,8,128]{2,1,0:T(8,128)S(1)} %bitcast.39), channel_id=1, source_target_pairs={{0,8},{8,0},{16,24},{24,16},{32,40},{40,32},{48,56},{56,48},{1,9},... | collective-permute-start | bytes 24584 | tf_op jit(solution)/shard_map/ppermute | solution.py:21
  82.1 40.5 %collective-permute-start.15 = (f32[2,8,128]{2,1,0:T(8,128)S(1)}, f32[2,8,128]{2,1,0:T(8,128)S(1)}, u32[]{:S(2)}, u32[]{:S(2)}) collective-permute-start(f32[2,8,128]{2,1,0:T(8,128)S(1)} %bitcast.40), channel_id=1, source_target_pairs={{0,16},{8,24},{16,0},{24,8},{32,48},{40,56},{48,32},{56,40},{1,17}... | collective-permute-start | bytes 24584 | tf_op jit(solution)/shard_map/ppermute | solution.py:21
  122.6 0.0 collective-permute-start.16
  122.6 0.0 collective-permute-done.14
  122.6 1.6 %collective-permute-done.15 = f32[2,8,128]{2,1,0:T(8,128)S(1)} collective-permute-done((f32[2,8,128]{2,1,0:T(8,128)S(1)}, f32[2,8,128]{2,1,0:T(8,128)S(1)}, u32[]{:S(2)}, u32[]{:S(2)}) %collective-permute-start.15) | collective-permute-done | bytes 8224 | tf_op jit(solution)/shard_map/ppermute | solution.py:21
  124.2 3.9 %collective-permute-done.16 = f32[2,8,128]{2,1,0:T(8,128)S(1)} collective-permute-done((f32[2,8,128]{2,1,0:T(8,128)S(1)}, f32[2,8,128]{2,1,0:T(8,128)S(1)}, u32[]{:S(2)}, u32[]{:S(2)}) %collective-permute-start.16) | collective-permute-done | bytes 8224 | tf_op jit(solution)/shard_map/ppermute | solution.py:21
  128.1 0.0 collective-permute-start.17
  128.1 7.8 %collective-permute-done.17 = f32[4,2,8,128]{3,2,1,0:T(8,128)S(1)} collective-permute-done((f32[4,2,8,128]{3,2,1,0:T(8,128)S(1)}, f32[4,2,8,128]{3,2,1,0:T(8,128)S(1)}, u32[]{:S(2)}, u32[]{:S(2)}) %collective-permute-start.17) | collective-permute-done | bytes 32800 | tf_op jit(solution)/shard_map/ppermute | solution.py:21
  136.0 0.1 collective-permute-start.18
  136.1 2.9 %collective-permute-start.19 = (f32[2,4,2,8,128]{4,3,2,1,0:T(8,128)S(1)}, f32[2,4,2,8,128]{4,3,2,1,0:T(8,128)S(1)}, u32[]{:S(2)}, u32[]{:S(2)}) collective-permute-start(f32[2,4,2,8,128]{4,3,2,1,0:T(8,128)S(1)} %get-tuple-element.23), channel_id=1, source_target_pairs={{0,128},{64,192},{128,0},{192,64},{1,129},{65,193},{129,1},{193,65... | collective-permute-start | bytes 196616 | tf_op jit(solution)/shard_map/ppermute | solution.py:21
  139.0 1.8 %collective-permute-start.20 = (f32[2,4,2,8,128]{4,3,2,1,0:T(8,128)S(1)}, f32[2,4,2,8,128]{4,3,2,1,0:T(8,128)S(1)}, u32[]{:S(2)}, u32[]{:S(2)}) collective-permute-start(f32[2,4,2,8,128]{4,3,2,1,0:T(8,128)S(1)} %get-tuple-element.23), channel_id=1, source_target_pairs={{0,192},{64,128},{128,64},{192,0},{1,193},{65,129},{129,65},{193,1... | collective-permute-start | bytes 196616 | tf_op jit(solution)/shard_map/ppermute | solution.py:21
  140.7 0.7 pad_add_fusion.1.info
  141.4 0.0 collective-permute-done.18
  141.4 0.5 collective-permute-done.19
  141.9 2.5 %collective-permute-done.20 = f32[2,4,2,8,128]{4,3,2,1,0:T(8,128)S(1)} collective-permute-done((f32[2,4,2,8,128]{4,3,2,1,0:T(8,128)S(1)}, f32[2,4,2,8,128]{4,3,2,1,0:T(8,128)S(1)}, u32[]{:S(2)}, u32[]{:S(2)}) %collective-permute-start.20) | collective-permute-done | bytes 65568 | tf_op jit(solution)/shard_map/ppermute | solution.py:21
  144.5 0.7 pad_maximum_fusion.1
  145.2 6.1 %pose_solve.1 = (f32[2,6]{1,0:T(2,128)}, f32[2,768]{1,0:T(2,128)}) custom-call(s32[2]{0:T(128)} %pad_add_fusion.1.info, f32[64,8,128]{2,1,0:T(8,128)} %bitcast.33, f32[40,1536]{1,0:T(8,128)} %copy-done.3), custom_call_target="tpu_custom_call" | custom-call | tf_op jit(solution)/shard_map/pose_solve/pallas_call | solution.py:219
  (8 shorter events, 0.1 us)
Async XLA Ops:
  0.6 17.4 %copy-start.2 = (bf16[2,12,64,128]{3,2,1,0:T(8,128)(2,1)S(1)}, bf16[2,12,64,128]{3,2,1,0:T(8,128)(2,1)}, u32[]{:S(2)}) copy-start(bf16[2,12,64,128]{3,2,1,0:T(8,128)(2,1)} %param.9) | copy-start | bytes 1179652
  0.6 12.3 %collective-permute-start = (bf16[2,768,128]{2,1,0:T(8,128)(2,1)}, bf16[2,768,128]{2,1,0:T(8,128)(2,1)S(1)}, u32[]{:S(2)}, u32[]{:S(2)}) collective-permute-start(bf16[2,768,128]{2,1,0:T(8,128)(2,1)} %bitcast.27), channel_id=1, source_target_pairs={{0,1},{1,0},{2,3},{3,2},{4,5},{5,4},{6,7},{7,6},{8,9},{9,8},{10,11... | collective-permute-start | bytes 1179656 | tf_op jit(solution)/shard_map/ppermute | solution.py:21
  1.6 12.7 %collective-permute-start.1 = (bf16[2,768,128]{2,1,0:T(8,128)(2,1)}, bf16[2,768,128]{2,1,0:T(8,128)(2,1)S(1)}, u32[]{:S(2)}, u32[]{:S(2)}) collective-permute-start(bf16[2,768,128]{2,1,0:T(8,128)(2,1)} %bitcast.28), channel_id=1, source_target_pairs={{0,3},{1,2},{2,1},{3,0},{4,7},{5,6},{6,5},{7,4},{8,11},{9,10},{10,... | collective-permute-start | bytes 1179656 | tf_op jit(solution)/shard_map/ppermute | solution.py:21
  3.0 13.5 %collective-permute-start.2 = (bf16[2,768,128]{2,1,0:T(8,128)(2,1)}, bf16[2,768,128]{2,1,0:T(8,128)(2,1)S(1)}, u32[]{:S(2)}, u32[]{:S(2)}) collective-permute-start(bf16[2,768,128]{2,1,0:T(8,128)(2,1)} %bitcast.29), channel_id=1, source_target_pairs={{4,0},{8,4},{12,8},{16,12},{20,16},{24,20},{28,24},{32,28},{36,32}... | collective-permute-start | bytes 1179656 | tf_op jit(solution)/shard_map/ppermute | solution.py:565
  5.3 24.6 %collective-permute-start.5 = (bf16[4,128,128]{2,1,0:T(8,128)(2,1)S(1)}, bf16[4,128,128]{2,1,0:T(8,128)(2,1)S(1)}, u32[]{:S(2)}, u32[]{:S(2)}) collective-permute-start(bf16[4,128,128]{2,1,0:T(8,128)(2,1)S(1)} %get-tuple-element.18), channel_id=1, source_target_pairs={{0,1},{1,0},{2,3},{3,2},{4,5},{5,4},{6,7},{7,6},{8,9},{9,8},{10,11... | collective-permute-start | bytes 393224 | tf_op jit(solution)/shard_map/ppermute | solution.py:21
  12.9 13.6 %collective-permute-start.3 = (bf16[2,768,128]{2,1,0:T(8,128)(2,1)S(1)}, bf16[2,768,128]{2,1,0:T(8,128)(2,1)S(1)}, u32[]{:S(2)}, u32[]{:S(2)}) collective-permute-start(bf16[2,768,128]{2,1,0:T(8,128)(2,1)S(1)} %collective-permute-done.side1.refs_0_.refs_6_), channel_id=1, source_target_pairs={{4,0},{8,4},{12,8},{16,12},{20,16},{24,20},{28,24},{32,28},{36,32}... | collective-permute-start | bytes 1179656 | tf_op jit(solution)/shard_map/ppermute | solution.py:565
  14.2 13.6 %collective-permute-start.4 = (bf16[2,768,128]{2,1,0:T(8,128)(2,1)S(1)}, bf16[2,768,128]{2,1,0:T(8,128)(2,1)S(1)}, u32[]{:S(2)}, u32[]{:S(2)}) collective-permute-start(bf16[2,768,128]{2,1,0:T(8,128)(2,1)S(1)} %collective-permute-done.1.side3.refs_1_.refs_7_), channel_id=1, source_target_pairs={{4,0},{8,4},{12,8},{16,12},{20,16},{24,20},{28,24},{32,28},{36,32}... | collective-permute-start | bytes 1179656 | tf_op jit(solution)/shard_map/ppermute | solution.py:565
  15.6 7.1 %collective-permute-start.8 = (bf16[2,384,128]{2,1,0:T(8,128)(2,1)S(1)}, bf16[2,384,128]{2,1,0:T(8,128)(2,1)S(1)}, u32[]{:S(2)}, u32[]{:S(2)}) collective-permute-start(bf16[2,384,128]{2,1,0:T(8,128)(2,1)S(1)} %slice.24), channel_id=1, source_target_pairs={{0,1},{1,0},{2,3},{3,2},{4,5},{5,4},{6,7},{7,6},{8,9},{9,8},{10,11... | collective-permute-start | bytes 589832 | tf_op jit(solution)/shard_map/ppermute | solution.py:21
  16.6 8.6 %collective-permute-start.7 = (bf16[2,384,128]{2,1,0:T(8,128)(2,1)S(1)}, bf16[2,384,128]{2,1,0:T(8,128)(2,1)S(1)}, u32[]{:S(2)}, u32[]{:S(2)}) collective-permute-start(bf16[2,384,128]{2,1,0:T(8,128)(2,1)S(1)} %slice.23), channel_id=1, source_target_pairs={{0,3},{1,2},{2,1},{3,0},{4,7},{5,6},{6,5},{7,4},{8,11},{9,10},{10,... | collective-permute-start | bytes 589832 | tf_op jit(solution)/shard_map/ppermute | solution.py:21
  22.7 7.5 %collective-permute-start.6 = (bf16[4,128,128]{2,1,0:T(8,128)(2,1)S(1)}, bf16[4,128,128]{2,1,0:T(8,128)(2,1)S(1)}, u32[]{:S(2)}, u32[]{:S(2)}) collective-permute-start(bf16[4,128,128]{2,1,0:T(8,128)(2,1)S(1)} %get-tuple-element.17), channel_id=1, source_target_pairs={{0,3},{1,2},{2,1},{3,0},{4,7},{5,6},{6,5},{7,4},{8,11},{9,10},{10,... | collective-permute-start | bytes 393224 | tf_op jit(solution)/shard_map/ppermute | solution.py:21
  25.2 5.0 %collective-permute-start.10 = (bf16[2,384,128]{2,1,0:T(8,128)(2,1)S(1)}, bf16[2,384,128]{2,1,0:T(8,128)(2,1)S(1)}, u32[]{:S(2)}, u32[]{:S(2)}) collective-permute-start(bf16[2,384,128]{2,1,0:T(8,128)(2,1)S(1)} %collective-permute-done.8.refs_9_), channel_id=1, source_target_pairs={{4,0},{8,4},{12,8},{16,12},{20,16},{24,20},{28,24},{32,28},{36,32}... | collective-permute-start | bytes 589832 | tf_op jit(solution)/shard_map/ppermute | solution.py:565
  26.5 4.0 %collective-permute-start.9 = (bf16[2,384,128]{2,1,0:T(8,128)(2,1)S(1)}, bf16[2,384,128]{2,1,0:T(8,128)(2,1)S(1)}, u32[]{:S(2)}, u32[]{:S(2)}) collective-permute-start(bf16[2,384,128]{2,1,0:T(8,128)(2,1)S(1)} %collective-permute-done.7.refs_8_), channel_id=1, source_target_pairs={{4,0},{8,4},{12,8},{16,12},{20,16},{24,20},{28,24},{32,28},{36,32}... | collective-permute-start | bytes 589832 | tf_op jit(solution)/shard_map/ppermute | solution.py:565
  27.8 2.7 %copy-start = (bf16[4,12,64,128]{3,2,1,0:T(8,128)(2,1)S(1)}, bf16[4,12,64,128]{3,2,1,0:T(8,128)(2,1)}, u32[]{:S(2)}) copy-start(bf16[4,12,64,128]{3,2,1,0:T(8,128)(2,1)} %param.12) | copy-start | bytes 2359300
  27.8 2.6 %copy-start.1 = (bf16[9,256,256]{2,1,0:T(8,128)(2,1)S(1)}, bf16[9,256,256]{2,1,0:T(8,128)(2,1)}, u32[]{:S(2)}) copy-start(bf16[9,256,256]{2,1,0:T(8,128)(2,1)} %param.15) | copy-start | bytes 3538948
  27.8 2.6 %copy-start.4 = (f32[2,768]{1,0:T(2,128)S(1)}, f32[2,768]{1,0:T(2,128)}, u32[]{:S(2)}) copy-start(f32[2,768]{1,0:T(2,128)} %refs_20_.1) | copy-start | bytes 18436
  49.7 0.7 copy-start.3
  50.4 4.7 %collective-permute-start.11 = (f32[8,128]{1,0:T(8,128)S(1)}, f32[8,128]{1,0:T(8,128)S(1)}, u32[]{:S(2)}, u32[]{:S(2)}) collective-permute-start(f32[8,128]{1,0:T(8,128)S(1)} %get-tuple-element.13), channel_id=1, source_target_pairs={{0,1},{1,0},{2,3},{3,2},{4,5},{5,4},{6,7},{7,6},{8,9},{9,8},{10,11... | collective-permute-start | bytes 12296 | tf_op jit(solution)/shard_map/ppermute | solution.py:21
  50.4 5.1 %collective-permute-start.12 = (f32[8,128]{1,0:T(8,128)S(1)}, f32[8,128]{1,0:T(8,128)S(1)}, u32[]{:S(2)}, u32[]{:S(2)}) collective-permute-start(f32[8,128]{1,0:T(8,128)S(1)} %get-tuple-element.13), channel_id=1, source_target_pairs={{0,2},{1,3},{2,0},{3,1},{4,6},{5,7},{6,4},{7,5},{8,10},{9,11},{10,... | collective-permute-start | bytes 12296 | tf_op jit(solution)/shard_map/ppermute | solution.py:21
  53.3 4.8 %collective-permute-start.13 = (f32[8,128]{1,0:T(8,128)S(1)}, f32[8,128]{1,0:T(8,128)S(1)}, u32[]{:S(2)}, u32[]{:S(2)}) collective-permute-start(f32[8,128]{1,0:T(8,128)S(1)} %get-tuple-element.13), channel_id=1, source_target_pairs={{0,3},{1,2},{2,1},{3,0},{4,7},{5,6},{6,5},{7,4},{8,11},{9,10},{10,... | collective-permute-start | bytes 12296 | tf_op jit(solution)/shard_map/ppermute | solution.py:21
  79.9 42.6 %collective-permute-start.14 = (f32[2,8,128]{2,1,0:T(8,128)S(1)}, f32[2,8,128]{2,1,0:T(8,128)S(1)}, u32[]{:S(2)}, u32[]{:S(2)}) collective-permute-start(f32[2,8,128]{2,1,0:T(8,128)S(1)} %bitcast.39), channel_id=1, source_target_pairs={{0,8},{8,0},{16,24},{24,16},{32,40},{40,32},{48,56},{56,48},{1,9},... | collective-permute-start | bytes 24584 | tf_op jit(solution)/shard_map/ppermute | solution.py:21
  82.1 42.1 %collective-permute-start.15 = (f32[2,8,128]{2,1,0:T(8,128)S(1)}, f32[2,8,128]{2,1,0:T(8,128)S(1)}, u32[]{:S(2)}, u32[]{:S(2)}) collective-permute-start(f32[2,8,128]{2,1,0:T(8,128)S(1)} %bitcast.40), channel_id=1, source_target_pairs={{0,16},{8,24},{16,0},{24,8},{32,48},{40,56},{48,32},{56,40},{1,17}... | collective-permute-start | bytes 24584 | tf_op jit(solution)/shard_map/ppermute | solution.py:21
  122.6 5.5 %collective-permute-start.16 = (f32[2,8,128]{2,1,0:T(8,128)S(1)}, f32[2,8,128]{2,1,0:T(8,128)S(1)}, u32[]{:S(2)}, u32[]{:S(2)}) collective-permute-start(f32[2,8,128]{2,1,0:T(8,128)S(1)} %bitcast.41), channel_id=1, source_target_pairs={{0,24},{8,16},{16,8},{24,0},{32,56},{40,48},{48,40},{56,32},{1,25}... | collective-permute-start | bytes 24584 | tf_op jit(solution)/shard_map/ppermute | solution.py:21
  128.1 7.8 %collective-permute-start.17 = (f32[4,2,8,128]{3,2,1,0:T(8,128)S(1)}, f32[4,2,8,128]{3,2,1,0:T(8,128)S(1)}, u32[]{:S(2)}, u32[]{:S(2)}) collective-permute-start(f32[4,2,8,128]{3,2,1,0:T(8,128)S(1)} %get-tuple-element.25), channel_id=1, source_target_pairs={{0,32},{8,40},{16,48},{24,56},{32,0},{40,8},{48,16},{56,24},{1,33}... | collective-permute-start | bytes 98312 | tf_op jit(solution)/shard_map/ppermute | solution.py:21
  136.0 5.5 %collective-permute-start.18 = (f32[2,4,2,8,128]{4,3,2,1,0:T(8,128)S(1)}, f32[2,4,2,8,128]{4,3,2,1,0:T(8,128)S(1)}, u32[]{:S(2)}, u32[]{:S(2)}) collective-permute-start(f32[2,4,2,8,128]{4,3,2,1,0:T(8,128)S(1)} %get-tuple-element.23), channel_id=1, source_target_pairs={{0,64},{64,0},{128,192},{192,128},{1,65},{65,1},{129,193},{193,129... | collective-permute-start | bytes 196616 | tf_op jit(solution)/shard_map/ppermute | solution.py:21
  136.1 5.8 %collective-permute-start.19 = (f32[2,4,2,8,128]{4,3,2,1,0:T(8,128)S(1)}, f32[2,4,2,8,128]{4,3,2,1,0:T(8,128)S(1)}, u32[]{:S(2)}, u32[]{:S(2)}) collective-permute-start(f32[2,4,2,8,128]{4,3,2,1,0:T(8,128)S(1)} %get-tuple-element.23), channel_id=1, source_target_pairs={{0,128},{64,192},{128,0},{192,64},{1,129},{65,193},{129,1},{193,65... | collective-permute-start | bytes 196616 | tf_op jit(solution)/shard_map/ppermute | solution.py:21
  139.0 5.5 %collective-permute-start.20 = (f32[2,4,2,8,128]{4,3,2,1,0:T(8,128)S(1)}, f32[2,4,2,8,128]{4,3,2,1,0:T(8,128)S(1)}, u32[]{:S(2)}, u32[]{:S(2)}) collective-permute-start(f32[2,4,2,8,128]{4,3,2,1,0:T(8,128)S(1)} %get-tuple-element.23), channel_id=1, source_target_pairs={{0,192},{64,128},{128,64},{192,0},{1,193},{65,129},{129,65},{193,1... | collective-permute-start | bytes 196616 | tf_op jit(solution)/shard_map/ppermute | solution.py:21

commit v2 on v1

--- a/solution.py
+++ b/solution.py
@@ -24,22 +24,42 @@
 def gathered_blocks(block):
     pair = block + swapped(block, "x", 1)
     block = pair + (swapped(block, "x", 2) + swapped(block, "x", 3))
-    parts = lax.all_gather(block, "core", axis=0)
+    parts = jnp.stack([block, swapped(block, "core", 1)])
     parts = jnp.stack([parts] + [swapped(parts, "z", s) for s in (1, 2, 3)])
     parts = jnp.stack([parts, swapped(parts, "z", 4)])
     parts = jnp.stack([parts] + [swapped(parts, "y", s) for s in (1, 2, 3)])
     return parts.reshape((-1,) + block.shape)
 
 
+class Facts:
+    def __init__(self, edges, counts, ranks):
+        self.edges, self.counts, self.ranks = edges, counts, ranks
+
+    def source(self, slot):
+        return self.edges[0, slot]
+
+    def target(self, slot):
+        return self.edges[1, slot]
+
+    def live(self):
+        return self.counts[0]
+
+    def node(self):
+        return self.ranks[0]
+
+    def pix(self):
+        return self.ranks[1]
+
+
 def bundle_body(slots, rows_all, cols, info, poses, rho_ref, head, out, h_ref, h_out, a_ref, w_ref, sem):
     pix = rho_ref.shape[1]
     rows = pix // cols
     shift = cols.bit_length() - 1
-    base = 2 * info[2 * slots + 1]
-    live = info[2 * slots]
+    base = 2 * info.node()
+    live = info.live()
     lane = lax.broadcasted_iota(jnp.int32, (1, pix), 1)
     col = (lane & (cols - 1)).astype(jnp.float32)
-    row = ((lane >> shift) + info[2 * slots + 2] * rows).astype(jnp.float32)
+    row = ((lane >> shift) + info.pix() * rows).astype(jnp.float32)
     half = cols / 2.0
     u = (col - (cols - 1) / 2.0) / half
     v = (row - (rows_all - 1) / 2.0) / half
@@ -50,16 +70,17 @@
     lead_v = jnp.where(sub == 1, 1.0, jnp.where(sub == 2, -v, zero))
     rest_v = jnp.where(sub == 3, -(1.0 + v * v), jnp.where(sub == 4, u * v, jnp.where(sub == 5, u, zero)))
     sub1 = lax.broadcasted_iota(jnp.int32, (8, 1), 0)
-    eye = lax.broadcasted_iota(jnp.int32, (8, 6), 0) == lax.broadcasted_iota(jnp.int32, (8, 6), 1)
+    frame = lax.broadcasted_iota(jnp.int32, (1, poses.shape[1]), 1)
     picks, sels = [], []
     for s in range(slots):
-        src, tgt = info[2 * s], info[2 * s + 1]
+        src, tgt = info.source(s), info.target(s)
         a_loc, b_loc = src - base, tgt - base
         alive = jnp.where(s < live, 1.0, 0.0)
         picks.append([jnp.where(a_loc == f, 1.0, 0.0) for f in range(2)])
         sels.append([jnp.where(b_loc == g, 1.0, 0.0) - jnp.where(a_loc == g, 1.0, 0.0) for g in range(4)])
-        d_row = poses[pl.ds(tgt, 1), :] - poses[pl.ds(src, 1), :]
-        d = jnp.sum(jnp.where(eye, jnp.broadcast_to(d_row, (8, 6)), 0.0), axis=1, keepdims=True)
+        pick_d = jnp.where(frame == tgt, 1.0, 0.0) - jnp.where(frame == src, 1.0, 0.0)
+        d = jnp.sum(poses[...] * pick_d, axis=1, keepdims=True)
+        d = jnp.concatenate([d, jnp.zeros((2, 1), jnp.float32)], axis=0)
         rho = rho_ref[pl.ds(a_loc, 1), :]
         conf_h = jax.nn.sigmoid(head[8 * s + 2 : 8 * s + 3, :]) * alive
         conf_v = jax.nn.sigmoid(head[8 * s + 3 : 8 * s + 4, :]) * alive
@@ -153,9 +174,8 @@
     lane = lax.broadcasted_iota(jnp.int32, (16, 128), 1)
     sub = lax.broadcasted_iota(jnp.int32, (16, 128), 0)
     me = info[0]
-    flip = me - (me & 1)
     for n in range(nodes):
-        t_ref[n] = g_ref[n ^ flip]
+        t_ref[n] = g_ref[n ^ me]
     rest = jnp.zeros((128 - nodes, 128), jnp.float32)
     for k in range(6):
         t = jnp.concatenate([t_ref[:, k, :], rest], axis=0).T
@@ -231,6 +251,7 @@
             pltpu.VMEM((12, 16, 128), jnp.float32),
             pltpu.VMEM((4, 12, 16, 128), jnp.float32),
         ],
+        compiler_params=pltpu.CompilerParams(vmem_limit_bytes=12 << 20),
         name="pose_solve",
     )(me, gathered, h)
 
@@ -241,7 +262,7 @@
 
 
 def spots(info, slots, pix, halo):
-    odd = (info[2 * slots + 2] & 1) == 1
+    odd = (info.pix() & 1) == 1
     at1 = pl.multiple_of(jnp.where(odd, 0, halo + pix), halo)
     at3 = pl.multiple_of(jnp.where(odd, halo + pix, 0), halo)
     return at1, at3
@@ -297,10 +318,10 @@
     pix, halo = own_q.shape[1], qt_ref.shape[2] - own_q.shape[1]
     halo = halo // 2
     at1, at3 = spots(info, slots, pix, halo)
-    odd = (info[2 * slots + 2] & 1) == 1
+    odd = (info.pix() & 1) == 1
     from1 = pl.multiple_of(jnp.where(odd, pix - halo, 0), halo)
     from3 = pl.multiple_of(jnp.where(odd, 0, pix - halo), halo)
-    src = info[2 * slot] - 2 * info[2 * slots + 1]
+    src = info.source(slot) - 2 * info.node()
     qt_ref[slot, :, halo : halo + pix] = turned(own_q[src])
     qt_ref[slot, :, pl.ds(at1, halo)] = turned(side1[src, pl.ds(from1, halo), :])
     qt_ref[slot, :, pl.ds(at3, halo)] = turned(side3[src, pl.ds(from3, halo), :])
@@ -310,9 +331,11 @@
     return 2.0 / math.sqrt(channels) * math.log2(math.e)
 
 
-def first_body(slots, info, own_q, side1, side3, own, after, acc_ref, qt_ref, k_ref, vt_ref):
+def first_body(slots, edges, counts, ranks, own_q, side1, side3, own, after, acc_ref, qt_ref, k_ref, vt_ref):
+    info = Facts(edges, counts, ranks)
+
     def one(slot, carry):
-        target = info[2 * slot + 1] - 2 * info[2 * slots + 1]
+        target = info.target(slot) - 2 * info.node()
         load_queries(info, slots, slot, own_q, side1, side3, qt_ref)
         load_keys(target, (own,), (after,), k_ref, vt_ref)
 
@@ -323,15 +346,16 @@
         add_keys(slot, k_ref, vt_ref, qt_ref, None, match_factor(k_ref.shape[1]), put)
         return carry
 
-    lax.fori_loop(0, info[2 * slots], one, 0)
-
-
-def second_body(slots, parts, info, qt_ref, old, *refs):
+    lax.fori_loop(0, info.live(), one, 0)
+
+
+def second_body(slots, parts, edges, counts, ranks, qt_ref, old, *refs):
+    info = Facts(edges, counts, ranks)
     owns, nexts = refs[:parts], refs[parts : 2 * parts]
     acc_ref, k_ref, vt_ref = refs[2 * parts :]
 
     def one(slot, carry):
-        target = info[2 * slot + 1] - 2 * info[2 * slots + 1]
+        target = info.target(slot) - 2 * info.node()
         load_keys(target, owns, nexts, k_ref, vt_ref)
 
 
@@ -341,26 +365,26 @@
         add_keys(slot, k_ref, vt_ref, qt_ref, old, match_factor(k_ref.shape[1]), put)
         return carry
 
-    lax.fori_loop(0, info[2 * slots], one, 0)
-
-
-def fused_body(dims, info, *refs):
+    lax.fori_loop(0, info.live(), one, 0)
+
+
+def fused_body(dims, edges, counts, ranks, *refs):
+    info = Facts(edges, counts, ranks)
     slots, total_rows, rows, cols, last, parts = dims
     (qt_ref, old), refs = refs[:2], refs[2:]
-    (state, hide1, hide3), refs = refs[:3], refs[3:]
+    (state, hide_up, hide_down), refs = refs[:3], refs[3:]
     owns, refs = refs[:parts], refs[parts:]
     nexts, refs = refs[:parts], refs[parts:]
-    (wg, wc01, wc2, wh, poses, rho_ref), refs = refs[:6], refs[6:]
+    (wg, wc, wh, poses, rho_ref), refs = refs[:5], refs[5:]
     (fresh_out, block_ref, pull_out), refs = refs[:3], refs[3:]
     fresh_ref, pull_ref, k_ref, vt_ref, acc_ref, kall_ref, vtall_ref, x_ref, h_ref = refs[:9]
-    head_ref, a_ref, w_ref, sems = refs[9:]
-    pix_rank = info[2 * slots + 2]
+    head_ref, a_ref, w_ref, wc01, sems = refs[9:]
+    pix_rank = info.pix()
     pix = rows * cols
     halo = 2 * cols
     ext = pix + 2 * halo
     channels = state.shape[-1]
     factor = match_factor(channels)
-    at1, at3 = spots(info, slots, pix, halo)
     px = lax.broadcasted_iota(jnp.int32, (ext, 1), 0)
 
     def inside(px):
@@ -368,6 +392,8 @@
         return jnp.where((grow >= 0) & (grow < total_rows), 1.0, 0.0)
 
     valid = inside(px)
+    wc01[:, :channels] = wc[0]
+    wc01[:, channels:] = wc[1]
 
     def send(slot):
         return pltpu.make_async_copy(fresh_ref.at[slot], fresh_out.at[slot], sems.at[slot])
@@ -378,10 +404,10 @@
         send(slot).start()
         return carry
 
-    lax.fori_loop(info[2 * slots], slots, keep, 0)
+    lax.fori_loop(info.live(), slots, keep, 0)
 
     def one(slot, carry):
-        target = info[2 * slot + 1] - 2 * info[2 * slots + 1]
+        target = info.target(slot) - 2 * info.node()
         load_keys(target, owns[parts - last :], nexts[parts - last :], k_ref, vt_ref)
 
         def put(at, value):
@@ -424,8 +450,8 @@
             lax.fori_loop(0, ext // TILE, exact, 0)
 
         h_ref[halo : halo + pix, :] = state[slot]
-        h_ref[pl.ds(at1, halo), :] = hide1[slot]
-        h_ref[pl.ds(at3, halo), :] = hide3[slot]
+        h_ref[:halo, :] = hide_up[slot]
+        h_ref[halo + pix :, :] = hide_down[slot]
         col = px & (cols - 1)
         first, final = col == 0, col == cols - 1
 
@@ -450,18 +476,18 @@
         inner = slice(cols, cols + mid)
         spread(jax.nn.sigmoid(gates[:, channels:]) * wide[inner], inner, 0)
         pair = jnp.dot(x_ref[cols : 2 * cols + pix, :], wc01[...], preferred_element_type=jnp.float32)
-        cand = jnp.dot(x_ref[3 * cols : 3 * cols + pix, :], wc2[...], preferred_element_type=jnp.float32)
+        cand = jnp.dot(x_ref[3 * cols : 3 * cols + pix, :], wc[2], preferred_element_type=jnp.float32)
         cand = cand + pair[:pix, :channels] + pair[cols : cols + pix, channels:]
         update = jax.nn.sigmoid(gates[cols : cols + pix, :channels])
         kept = wide[halo : halo + pix]
         fresh = ((1.0 - update) * kept + update * jnp.tanh(cand)).astype(jnp.bfloat16)
         fresh_ref[slot] = fresh
         head = lax.dot_general(wh[...], fresh, NT, preferred_element_type=jnp.float32)
-        head_ref[pl.ds(pl.multiple_of(8 * slot, 8), 8), :] = head
+        head_ref[pl.ds(pl.multiple_of(8 * slot, 8), 4), :] = head
         send(slot).start()
         return carry
 
-    lax.fori_loop(0, info[2 * slots], one, 0)
+    lax.fori_loop(0, info.live(), one, 0)
     bundle_body(
         slots, total_rows, cols, info, poses, rho_ref, head_ref, block_ref, pull_ref, pull_out, a_ref, w_ref, sems.at[slots]
     )
@@ -481,12 +507,12 @@
     )
 
 
-def first_call(info, slots, cols, queries, own, after):
+def first_call(facts, slots, cols, queries, own, after):
     pix, channels = own.shape[1:]
     ext = pix + 4 * cols
     return pl.pallas_call(
         functools.partial(first_body, slots),
-        in_specs=[SMEM] + [VMEM] * 5,
+        in_specs=[SMEM] * 3 + [VMEM] * 5,
         out_specs=(VMEM, VMEM),
         scratch_shapes=[pltpu.VMEM((pix, channels), jnp.bfloat16), pltpu.VMEM((channels + 8, pix), jnp.bfloat16)],
         out_shape=(
@@ -496,25 +522,25 @@
         cost_estimate=work(slots, ext, pix, channels),
         compiler_params=pltpu.CompilerParams(vmem_limit_bytes=14 << 20),
         name="match_first",
-    )(info, *queries, own, after)
-
-
-def second_call(info, qt, old, owns, nexts):
+    )(*facts, *queries, own, after)
+
+
+def second_call(facts, qt, old, owns, nexts):
     slots, channels, ext = qt.shape
     keys = sum(part.shape[1] for part in owns)
     return pl.pallas_call(
         functools.partial(second_body, slots, len(owns)),
-        in_specs=[SMEM] + [VMEM] * (2 + 2 * len(owns)),
+        in_specs=[SMEM] * 3 + [VMEM] * (2 + 2 * len(owns)),
         out_specs=VMEM,
         scratch_shapes=[pltpu.VMEM((keys, channels), jnp.bfloat16), pltpu.VMEM((channels + 8, keys), jnp.bfloat16)],
         out_shape=jax.ShapeDtypeStruct(old.shape, jnp.float32),
         cost_estimate=work(slots, ext, keys, channels),
         compiler_params=pltpu.CompilerParams(vmem_limit_bytes=14 << 20),
         name="match_second",
-    )(info, qt, old, *owns, *nexts)
-
-
-def fused_call(info, qt, old, state, hide1, hide3, owns, nexts, last, weights, poses, inv_depth, total_rows, cols):
+    )(*facts, qt, old, *owns, *nexts)
+
+
+def fused_call(facts, qt, old, state, hide_up, hide_down, owns, nexts, last, weights, poses, inv_depth, total_rows, cols):
     slots, pix, channels = state.shape
     ext = qt.shape[2]
     keys = sum(part.shape[1] for part in owns)
@@ -523,7 +549,7 @@
     wide = channels + 8
     return pl.pallas_call(
         functools.partial(fused_body, dims),
-        in_specs=[SMEM] + [VMEM] * (5 + 2 * len(owns) + len(weights) + 2),
+        in_specs=[SMEM] * 3 + [VMEM] * (5 + 2 * len(owns) + len(weights) + 2),
         out_specs=(pl.BlockSpec(memory_space=pltpu.HBM), VMEM, pl.BlockSpec(memory_space=pltpu.HBM)),
         scratch_shapes=[
             pltpu.VMEM((slots, pix, channels), jnp.bfloat16),
@@ -538,6 +564,7 @@
             pltpu.VMEM((8 * slots, pix), jnp.float32),
             pltpu.VMEM((8 * slots, 2 * pix), jnp.float32),
             pltpu.VMEM((8 * slots, 2 * pix), jnp.float32),
+            pltpu.VMEM((weights[1].shape[1], 2 * channels), jnp.bfloat16),
             pltpu.SemaphoreType.DMA((slots + 1,)),
         ],
         out_shape=(
@@ -547,7 +574,7 @@
         ),
         compiler_params=pltpu.CompilerParams(vmem_limit_bytes=26 << 20),
         name="match_update",
-    )(info, qt, old, state, hide1, hide3, *owns, *nexts, *weights, poses, inv_depth)
+    )(*facts, qt, old, state, hide_up, hide_down, *owns, *nexts, *weights, poses, inv_depth)
 
 
 def shards(features, poses, inv_depth, hidden, edges, counts, w_gates, w_cand, w_head):
@@ -559,49 +586,42 @@
     pix = row_count * col_count
     nodes = lax.axis_size(EDGE)
     halo = 2 * col_count
-    info = jnp.concatenate([edges.reshape(-1), counts, jnp.stack([node_rank, pix_rank])]).astype(jnp.int32)
+    facts = (edges.T, counts, jnp.stack([node_rank, pix_rank]).astype(jnp.int32))
 
     def following(value):
         return lax.ppermute(value, EDGE, [(i + 1, i) for i in range(nodes - 1)])
 
     own = features.reshape(2, pix, channels)
     state = hidden.reshape(slot_count, pix, hid_width)
-    own1, own3 = swapped(own, "x", 1), swapped(own, "x", 3)
+    own1, own3, own2 = [swapped(own, "x", step) for step in (1, 3, 2)]
     next0 = following(own)
-    odd = pix_rank & 1
-    send1 = lax.dynamic_slice_in_dim(state, (1 - odd) * (pix - halo), halo, axis=1)
-    send3 = lax.dynamic_slice_in_dim(state, odd * (pix - halo), halo, axis=1)
-    hide1, hide3 = swapped(send1, "x", 1), swapped(send3, "x", 3)
-    half = pix // 2
-    own2a = swapped(own1[:, :half], "x", 3)
-    own2b = swapped(own3[:, half:], "x", 1)
-    next1, next3 = following(own1), following(own3)
-    next2a, next2b = following(own2a), following(own2b)
-    queries = (own, own1, own3)
-    acc, turned = first_call(info, slot_count, col_count, queries, own, next0)
-    acc = second_call(info, turned, acc, (own1, own3), (next1, next3))
+    next1, next3, next2 = following(own1), following(own3), following(own2)
+    acc, turned_q = first_call(facts, slot_count, col_count, (own, own1, own3), own, next0)
+    acc, late = lax.optimization_barrier((acc, state))
+    rows_x = lax.axis_size("x")
+    hide_up = lax.ppermute(late[:, pix - halo :], "x", [(i, i + 1) for i in range(rows_x - 1)])
+    hide_down = lax.ppermute(late[:, :halo], "x", [(i + 1, i) for i in range(rows_x - 1)])
+    acc = second_call(facts, turned_q, acc, (own1, own3), (next1, next3))
     wg = w_gates.reshape(3, -1, w_gates.shape[2])
     wc = w_cand.reshape(3, -1, w_cand.shape[2])
-    wc01 = jnp.concatenate([wc[0], wc[1]], axis=1)
-    wh = jnp.concatenate([w_head, jnp.zeros_like(w_head)], axis=0)
     fresh, block, pull = fused_call(
-        info,
-        turned,
+        facts,
+        turned_q,
         acc,
         state,
-        hide1,
-        hide3,
-        (own, own1, own3, own2a, own2b),
-        (next0, next1, next3, next2a, next2b),
-        2,
-        (wg, wc01, wc[2], wh),
-        poses,
+        hide_up,
+        hide_down,
+        (own, own1, own3, own2),
+        (next0, next1, next3, next2),
+        1,
+        (wg, wc, w_head),
+        poses.T,
         inv_depth,
         total_rows,
         col_count,
     )
     gathered = gathered_blocks(block)
-    pose_update, depth_update = solve_call(info[2 * slot_count + 1 :], gathered, pull)
+    pose_update, depth_update = solve_call(facts[2], gathered, pull)
     return (fresh.reshape(hidden.shape), pose_update, depth_update)
 
 

time: 151 us -> 155 us (1.026); the launches traced: 151 us -> 153 us
  Pallas kernels: 28.8 us -> 86.5 us
  starting transfers between devices: 65.1 us -> 29.8 us
  blocking collectives: 21.8 us -> 0 us
  waiting for transfers between devices: 27.2 us -> 33.4 us
  local copies, waits for them, and re-layouts: 5.23 us -> 1.74 us
    pallas_call x2, Pallas kernels: 20.7 us -> 74.4 us  [the longest x1 70 us: fused_call(): pl.pallas_call(functools.partial(fused_body, dims), in_specs=[SMEM] * 3 +...]
    ppermute x16 -> x14, starting transfers between devices: 58.7 us -> 18.8 us  [swapped(): return lax.ppermute(value, axis, [(i, i ^ step) for i in range(count)])]
    all_gather x1 -> x0, blocking collectives: 21.8 us -> none  [gathered_blocks(): parts = lax.all_gather(block, 'core', axis=0)]
    ppermute x16 -> x14, waiting for transfers between devices: 26.9 us -> 33.4 us  [swapped(): return lax.ppermute(value, axis, [(i, i ^ step) for i in range(count)])]
    ppermute x0 -> x2, starting transfers between devices: none -> 5.85 us  [the longest x1 4.55 us: shards(): lax.ppermute(late[:, :halo], 'x', [(i + 1, i) for i in range(rows_x - 1)])]
    pallas_call x1, Pallas kernels: 2.05 us -> 6.59 us  [second_call(): pl.pallas_call(functools.partial(second_body, slots, len(owns)), in_specs...]
    ppermute x5 -> x4, starting transfers between devices: 6.43 us -> 5.13 us  [following(): return lax.ppermute(value, EDGE, [(i + 1, i) for i in range(nodes - 1)])]
  transfers between devices with their start and end apart: 21 -> 20, of which waited for: 12 -> 10; matrix products, arithmetic and copies ran while one was open for 4% -> 0% of each run, Pallas kernels for 2% -> 7%
where the time goes in v2:
time: 155 us; the launch traced here: 153 us
  Pallas kernels  86.5 us (56%)
  waiting for transfers between devices  33.4 us (22%)
  starting transfers between devices  29.8 us (19%)
  local copies, waits for them, and re-layouts  1.74 us (1%)
  between operations  1.6 us (1%)
    pallas_call x1, Pallas kernels, fused_call(): pl.pallas_call(functools.partial(fused_body, dims), in_specs=[SMEM] * 3 +...  70 us
    ppermute x14, waiting for transfers between devices, swapped(): return lax.ppermute(value, axis, [(i, i ^ step) for i in range(count)])  33.4 us
    ppermute x14, starting transfers between devices, swapped(): return lax.ppermute(value, axis, [(i, i ^ step) for i in range(count)])  18.8 us
    pallas_call x1, Pallas kernels, second_call(): pl.pallas_call(functools.partial(second_body, slots, len(owns)), in_specs...  6.59 us
    pallas_call x1, Pallas kernels, solve_call(): pl.pallas_call(functools.partial(solve_body, nodes, pix), out_shape=(jax....  5.56 us
    ppermute x4, starting transfers between devices, following(): return lax.ppermute(value, EDGE, [(i + 1, i) for i in range(nodes - 1)])  5.13 us
    ppermute x1, starting transfers between devices, shards(): lax.ppermute(late[:, :halo], 'x', [(i + 1, i) for i in range(rows_x - 1)])  4.55 us
    pallas_call x1, Pallas kernels, first_call(): pl.pallas_call(functools.partial(first_body, slots), in_specs=[SMEM] * 3...  4.41 us
  transfers between devices with their start and end apart: 20, of which 10 were waited for; matrix products, arithmetic and copies ran while one was open for 0% of the time, Pallas kernels for 7%

profile of v2, /device:TPU:6, one launch (start us, length us, event | category | flops | bytes accessed | tf_op | source)
XLA Modules:
  0.0 153.3 jit_solution(632896959519095703)
XLA Ops:
  0.6 0.9 collective-permute-start
  1.5 1.5 collective-permute-start.1
  3.0 1.3 collective-permute-start.2
  4.3 1.9 %collective-permute-start.7 = (bf16[2,768,128]{2,1,0:T(8,128)(2,1)}, bf16[2,768,128]{2,1,0:T(8,128)(2,1)S(1)}, u32[]{:S(2)}, u32[]{:S(2)}) collective-permute-start(bf16[2,768,128]{2,1,0:T(8,128)(2,1)} %bitcast.33), channel_id=1, source_target_pairs={{0,2},{1,3},{2,0},{3,1},{4,6},{5,7},{6,4},{7,5},{8,10},{9,11},{10,... | collective-permute-start | bytes 1179656 | tf_op jit(solution)/shard_map/ppermute | solution.py:21
  6.8 0.1 pad_add_fusion.ranks.info
  6.9 6.0 %collective-permute-done.side1.refs_0_.refs_6_ = bf16[2,768,128]{2,1,0:T(8,128)(2,1)S(1)} collective-permute-done((bf16[2,768,128]{2,1,0:T(8,128)(2,1)}, bf16[2,768,128]{2,1,0:T(8,128)(2,1)S(1)}, u32[]{:S(2)}, u32[]{:S(2)}) %collective-permute-start) | collective-permute-done | bytes 393248 | tf_op jit(solution)/shard_map/ppermute | solution.py:21
  12.9 1.3 collective-permute-start.3
  14.2 7.8 %collective-permute-done.1.side3.refs_1_.refs_7_ = bf16[2,768,128]{2,1,0:T(8,128)(2,1)S(1)} collective-permute-done((bf16[2,768,128]{2,1,0:T(8,128)(2,1)}, bf16[2,768,128]{2,1,0:T(8,128)(2,1)S(1)}, u32[]{:S(2)}, u32[]{:S(2)}) %collective-permute-start.1) | collective-permute-done | bytes 393248 | tf_op jit(solution)/shard_map/ppermute | solution.py:21
  22.0 1.3 collective-permute-start.4
  23.3 0.0 collective-permute-done.2.after.refs_9_
  23.3 0.0 copy-start.3
  23.3 1.0 copy-done.3
  24.3 0.0 copy-start.7
  24.3 0.7 copy-done.7
  24.9 4.4 %match_first.1 = (f32[4,136,1024]{2,1,0:T(8,128)S(1)}, bf16[4,128,1024]{2,1,0:T(8,128)(2,1)S(1)}) custom-call(s32[2,4]{1,0:T(2,128)S(1)} %bitcast.38, s32[1]{0:T(128)S(6)} %copy.12.counts, s32[2]{0:T(128)S(1)} %pad_add_fusion.ranks.info, bf16[2,768,128]{2,1,0:T(8,128)(2,1)S(1)} %bitcast.34, ...), custom_call_target="tpu_custom_call" | custom-call | flops 3221225472 | bytes 4456448 | tf_op jit(solution)/shard_map/match_first/pallas_call | solution.py:513
  29.4 0.0 copy-done
  29.4 1.3 collective-permute-start.5
  30.7 4.6 %collective-permute-start.6 = (bf16[4,128,128]{2,1,0:T(8,128)(2,1)S(1)}, bf16[4,128,128]{2,1,0:T(8,128)(2,1)S(1)}, u32[]{:S(2)}, u32[]{:S(2)}) collective-permute-start(bf16[4,128,128]{2,1,0:T(8,128)(2,1)S(1)} %get-tuple-element.21), channel_id=1, source_target_pairs={{1,0},{2,1},{3,2},{5,4},{6,5},{7,6},{9,8},{10,9},{11,10},{13,12},{... | collective-permute-start | bytes 393224 | tf_op jit(solution)/shard_map/ppermute | solution.py:603
  35.3 0.0 collective-permute-done.7.refs_8_
  35.3 1.3 collective-permute-start.8
  36.6 0.0 collective-permute-done.3.refs_2_.refs_10_
  36.6 0.0 collective-permute-done.4.refs_3_.refs_11_
  36.6 0.0 copy-start.1
  36.6 0.0 copy-start.2
  36.6 0.0 copy-start.4
  36.6 0.0 copy-start.5
  36.6 0.0 copy-start.6
  36.7 0.0 copy-start.8
  36.7 0.0 copy-start.9
  36.7 6.6 %match_second.1.refs_1_ = f32[4,136,1024]{2,1,0:T(8,128)S(1)} custom-call(s32[2,4]{1,0:T(2,128)S(1)} %bitcast.39, s32[1]{0:T(128)S(6)} %copy.12.counts, s32[2]{0:T(128)S(1)} %pad_add_fusion.ranks.info, bf16[4,128,1024]{2,1,0:T(8,128)(2,1)S(1)} %get-tuple-element.12.qt_ref.refs_0_, f32[4,136,1024]{2,1,0:T(8,128)S(1)} %get-tuple-element.14.old, ...), custom_call_target="tpu_custom_call" | custom-call | flops 6442450944 | bytes 4456448 | tf_op jit(solution)/shard_map/match_second/pallas_call | solution.py:531
  43.3 0.0 collective-permute-done.5.refs_3_
  43.3 0.0 collective-permute-done.6.refs_4_
  43.3 0.0 collective-permute-done.8.refs_12_
  43.3 0.0 copy-done.1
  43.3 0.0 copy-done.2
  43.3 0.0 copy-done.4
  43.3 0.0 copy-done.5
  43.4 0.0 copy-done.6
  43.4 0.0 copy-done.8
  43.4 0.0 copy-done.9
  43.4 70.0 %match_update.1 = (bf16[4,768,128]{2,1,0:T(8,128)(2,1)}, f32[8,128]{1,0:T(8,128)S(1)}, f32[40,1536]{1,0:T(8,128)S(1)}) custom-call(s32[2,4]{1,0:T(2,128)S(1)} %bitcast.40, s32[1]{0:T(128)S(6)} %copy.12.counts, s32[2]{0:T(128)S(1)} %pad_add_fusion.ranks.info, bf16[4,128,1024]{2,1,0:T(8,128)(2,1)S(1)} %get-tuple-element.12.qt_ref.refs_0_, ...), custom_call_target="tpu_custom_call" | custom-call | tf_op jit(solution)/shard_map/match_update/pallas_call | solution.py:550
  113.4 0.1 collective-permute-start.10
  113.5 2.6 %collective-permute-start.11 = (f32[8,128]{1,0:T(8,128)S(1)}, f32[8,128]{1,0:T(8,128)S(1)}, u32[]{:S(2)}, u32[]{:S(2)}) collective-permute-start(f32[8,128]{1,0:T(8,128)S(1)} %get-tuple-element.17), channel_id=1, source_target_pairs={{0,3},{1,2},{2,1},{3,0},{4,7},{5,6},{6,5},{7,4},{8,11},{9,10},{10,... | collective-permute-start | bytes 12296 | tf_op jit(solution)/shard_map/ppermute | solution.py:21
  116.2 0.8 collective-permute-start.9
  116.9 1.6 %collective-permute-done.10 = f32[8,128]{1,0:T(8,128)S(1)} collective-permute-done((f32[8,128]{1,0:T(8,128)S(1)}, f32[8,128]{1,0:T(8,128)S(1)}, u32[]{:S(2)}, u32[]{:S(2)}) %collective-permute-start.10) | collective-permute-done | bytes 4128 | tf_op jit(solution)/shard_map/ppermute | solution.py:21
  118.6 0.0 collective-permute-done.11
  118.6 1.2 collective-permute-done.9
  119.8 0.0 collective-permute-start.12
  119.8 1.2 collective-permute-done.12
  120.9 0.0 collective-permute-start.13
  120.9 6.2 %collective-permute-start.14 = (f32[2,8,128]{2,1,0:T(8,128)S(1)}, f32[2,8,128]{2,1,0:T(8,128)S(1)}, u32[]{:S(2)}, u32[]{:S(2)}) collective-permute-start(f32[2,8,128]{2,1,0:T(8,128)S(1)} %get-tuple-element.28), channel_id=1, source_target_pairs={{0,16},{8,24},{16,0},{24,8},{32,48},{40,56},{48,32},{56,40},{1,17}... | collective-permute-start | bytes 24584 | tf_op jit(solution)/shard_map/ppermute | solution.py:21
  127.2 0.0 collective-permute-start.15
  127.2 0.0 collective-permute-done.13
  127.2 1.6 %collective-permute-done.14 = f32[2,8,128]{2,1,0:T(8,128)S(1)} collective-permute-done((f32[2,8,128]{2,1,0:T(8,128)S(1)}, f32[2,8,128]{2,1,0:T(8,128)S(1)}, u32[]{:S(2)}, u32[]{:S(2)}) %collective-permute-start.14) | collective-permute-done | bytes 8224 | tf_op jit(solution)/shard_map/ppermute | solution.py:21
  128.8 4.0 %collective-permute-done.15 = f32[2,8,128]{2,1,0:T(8,128)S(1)} collective-permute-done((f32[2,8,128]{2,1,0:T(8,128)S(1)}, f32[2,8,128]{2,1,0:T(8,128)S(1)}, u32[]{:S(2)}, u32[]{:S(2)}) %collective-permute-start.15) | collective-permute-done | bytes 8224 | tf_op jit(solution)/shard_map/ppermute | solution.py:21
  132.8 0.0 collective-permute-start.16
  132.8 7.8 %collective-permute-done.16 = f32[4,2,8,128]{3,2,1,0:T(8,128)S(1)} collective-permute-done((f32[4,2,8,128]{3,2,1,0:T(8,128)S(1)}, f32[4,2,8,128]{3,2,1,0:T(8,128)S(1)}, u32[]{:S(2)}, u32[]{:S(2)}) %collective-permute-start.16) | collective-permute-done | bytes 32800 | tf_op jit(solution)/shard_map/ppermute | solution.py:21
  140.6 0.1 collective-permute-start.17
  140.7 0.1 collective-permute-start.18
  140.8 4.6 %collective-permute-start.19 = (f32[2,4,2,8,128]{4,3,2,1,0:T(8,128)S(1)}, f32[2,4,2,8,128]{4,3,2,1,0:T(8,128)S(1)}, u32[]{:S(2)}, u32[]{:S(2)}) collective-permute-start(f32[2,4,2,8,128]{4,3,2,1,0:T(8,128)S(1)} %get-tuple-element.24), channel_id=1, source_target_pairs={{0,192},{64,128},{128,64},{192,0},{1,193},{65,129},{129,65},{193,1... | collective-permute-start | bytes 196616 | tf_op jit(solution)/shard_map/ppermute | solution.py:21
  145.4 0.0 collective-permute-done.17
  145.4 1.2 collective-permute-done.18
  146.6 1.1 collective-permute-done.19
  147.7 5.6 %pose_solve.1 = (f32[2,6]{1,0:T(2,128)}, f32[2,768]{1,0:T(2,128)}) custom-call(s32[2]{0:T(128)S(1)} %pad_add_fusion.ranks.info, f32[64,8,128]{2,1,0:T(8,128)S(1)} %bitcast.28, f32[40,1536]{1,0:T(8,128)S(1)} %get-tuple-element.18.h_ref), custom_call_target="tpu_custom_call" | custom-call | tf_op jit(solution)/shard_map/pose_solve/pallas_call | solution.py:239
  (7 shorter events, 0.1 us)
Async XLA Ops:
  0.6 12.3 %collective-permute-start = (bf16[2,768,128]{2,1,0:T(8,128)(2,1)}, bf16[2,768,128]{2,1,0:T(8,128)(2,1)S(1)}, u32[]{:S(2)}, u32[]{:S(2)}) collective-permute-start(bf16[2,768,128]{2,1,0:T(8,128)(2,1)} %bitcast.30), channel_id=1, source_target_pairs={{0,1},{1,0},{2,3},{3,2},{4,5},{5,4},{6,7},{7,6},{8,9},{9,8},{10,11... | collective-permute-start | bytes 1179656 | tf_op jit(solution)/shard_map/ppermute | solution.py:21
  1.5 20.4 %collective-permute-start.1 = (bf16[2,768,128]{2,1,0:T(8,128)(2,1)}, bf16[2,768,128]{2,1,0:T(8,128)(2,1)S(1)}, u32[]{:S(2)}, u32[]{:S(2)}) collective-permute-start(bf16[2,768,128]{2,1,0:T(8,128)(2,1)} %bitcast.31), channel_id=1, source_target_pairs={{0,3},{1,2},{2,1},{3,0},{4,7},{5,6},{6,5},{7,4},{8,11},{9,10},{10,... | collective-permute-start | bytes 1179656 | tf_op jit(solution)/shard_map/ppermute | solution.py:21
  3.0 20.2 %collective-permute-start.2 = (bf16[2,768,128]{2,1,0:T(8,128)(2,1)}, bf16[2,768,128]{2,1,0:T(8,128)(2,1)S(1)}, u32[]{:S(2)}, u32[]{:S(2)}) collective-permute-start(bf16[2,768,128]{2,1,0:T(8,128)(2,1)} %bitcast.32), channel_id=1, source_target_pairs={{4,0},{8,4},{12,8},{16,12},{20,16},{24,20},{28,24},{32,28},{36,32}... | collective-permute-start | bytes 1179656 | tf_op jit(solution)/shard_map/ppermute | solution.py:592
  4.3 31.0 %collective-permute-start.7 = (bf16[2,768,128]{2,1,0:T(8,128)(2,1)}, bf16[2,768,128]{2,1,0:T(8,128)(2,1)S(1)}, u32[]{:S(2)}, u32[]{:S(2)}) collective-permute-start(bf16[2,768,128]{2,1,0:T(8,128)(2,1)} %bitcast.33), channel_id=1, source_target_pairs={{0,2},{1,3},{2,0},{3,1},{4,6},{5,7},{6,4},{7,5},{8,10},{9,11},{10,... | collective-permute-start | bytes 1179656 | tf_op jit(solution)/shard_map/ppermute | solution.py:21
  12.9 23.7 %collective-permute-start.3 = (bf16[2,768,128]{2,1,0:T(8,128)(2,1)S(1)}, bf16[2,768,128]{2,1,0:T(8,128)(2,1)S(1)}, u32[]{:S(2)}, u32[]{:S(2)}) collective-permute-start(bf16[2,768,128]{2,1,0:T(8,128)(2,1)S(1)} %collective-permute-done.side1.refs_0_.refs_6_), channel_id=1, source_target_pairs={{4,0},{8,4},{12,8},{16,12},{20,16},{24,20},{28,24},{32,28},{36,32}... | collective-permute-start | bytes 1179656 | tf_op jit(solution)/shard_map/ppermute | solution.py:592
  22.0 14.6 %collective-permute-start.4 = (bf16[2,768,128]{2,1,0:T(8,128)(2,1)S(1)}, bf16[2,768,128]{2,1,0:T(8,128)(2,1)S(1)}, u32[]{:S(2)}, u32[]{:S(2)}) collective-permute-start(bf16[2,768,128]{2,1,0:T(8,128)(2,1)S(1)} %collective-permute-done.1.side3.refs_1_.refs_7_), channel_id=1, source_target_pairs={{4,0},{8,4},{12,8},{16,12},{20,16},{24,20},{28,24},{32,28},{36,32}... | collective-permute-start | bytes 1179656 | tf_op jit(solution)/shard_map/ppermute | solution.py:592
  23.3 1.0 copy-start.3
  24.3 0.7 copy-start.7
  24.9 4.4 %copy-start = (bf16[4,12,64,128]{3,2,1,0:T(8,128)(2,1)S(1)}, bf16[4,12,64,128]{3,2,1,0:T(8,128)(2,1)}, u32[]{:S(2)}) copy-start(bf16[4,12,64,128]{3,2,1,0:T(8,128)(2,1)} %param.12) | copy-start | bytes 2359300
  29.4 13.9 %collective-permute-start.5 = (bf16[4,128,128]{2,1,0:T(8,128)(2,1)S(1)}, bf16[4,128,128]{2,1,0:T(8,128)(2,1)S(1)}, u32[]{:S(2)}, u32[]{:S(2)}) collective-permute-start(bf16[4,128,128]{2,1,0:T(8,128)(2,1)S(1)} %get-tuple-element.22), channel_id=1, source_target_pairs={{0,1},{1,2},{2,3},{4,5},{5,6},{6,7},{8,9},{9,10},{10,11},{12,13},{... | collective-permute-start | bytes 393224 | tf_op jit(solution)/shard_map/ppermute | solution.py:602
  30.7 12.6 %collective-permute-start.6 = (bf16[4,128,128]{2,1,0:T(8,128)(2,1)S(1)}, bf16[4,128,128]{2,1,0:T(8,128)(2,1)S(1)}, u32[]{:S(2)}, u32[]{:S(2)}) collective-permute-start(bf16[4,128,128]{2,1,0:T(8,128)(2,1)S(1)} %get-tuple-element.21), channel_id=1, source_target_pairs={{1,0},{2,1},{3,2},{5,4},{6,5},{7,6},{9,8},{10,9},{11,10},{13,12},{... | collective-permute-start | bytes 393224 | tf_op jit(solution)/shard_map/ppermute | solution.py:603
  35.3 8.0 %collective-permute-start.8 = (bf16[2,768,128]{2,1,0:T(8,128)(2,1)S(1)}, bf16[2,768,128]{2,1,0:T(8,128)(2,1)S(1)}, u32[]{:S(2)}, u32[]{:S(2)}) collective-permute-start(bf16[2,768,128]{2,1,0:T(8,128)(2,1)S(1)} %collective-permute-done.7.refs_8_), channel_id=1, source_target_pairs={{4,0},{8,4},{12,8},{16,12},{20,16},{24,20},{28,24},{32,28},{36,32}... | collective-permute-start | bytes 1179656 | tf_op jit(solution)/shard_map/ppermute | solution.py:592
  36.6 6.7 %copy-start.1 = (bf16[9,256,256]{2,1,0:T(8,128)(2,1)S(1)}, bf16[9,256,256]{2,1,0:T(8,128)(2,1)}, u32[]{:S(2)}) copy-start(bf16[9,256,256]{2,1,0:T(8,128)(2,1)} %param.15) | copy-start | bytes 3538948
  36.6 6.7 %copy-start.2 = (bf16[9,256,128]{2,1,0:T(8,128)(2,1)S(1)}, bf16[9,256,128]{2,1,0:T(8,128)(2,1)}, u32[]{:S(2)}) copy-start(bf16[9,256,128]{2,1,0:T(8,128)(2,1)} %param.16) | copy-start | bytes 1769476
  36.6 6.7 %copy-start.4 = (bf16[2,12,64,128]{3,2,1,0:T(8,128)(2,1)S(1)}, bf16[2,12,64,128]{3,2,1,0:T(8,128)(2,1)}, u32[]{:S(2)}) copy-start(bf16[2,12,64,128]{3,2,1,0:T(8,128)(2,1)} %param.9) | copy-start | bytes 1179652
  36.6 6.7 %copy-start.5 = (f32[2,768]{1,0:T(2,128)S(1)}, f32[2,768]{1,0:T(2,128)}, u32[]{:S(2)}) copy-start(f32[2,768]{1,0:T(2,128)} %refs_17_.1) | copy-start | bytes 18436
  36.6 6.7 %copy-start.6 = (f32[128,6]{0,1:T(8,128)S(1)}, f32[128,6]{0,1:T(8,128)}, u32[]{:S(2)}) copy-start(f32[128,6]{0,1:T(8,128)} %param.10) | copy-start | bytes 9220
  36.7 6.7 %copy-start.8 = (s32[4,2]{0,1:T(2,128)S(1)}, s32[4,2]{0,1:T(2,128)}, u32[]{:S(2)}) copy-start(s32[4,2]{0,1:T(2,128)} %param.13) | copy-start | bytes 100
  36.7 6.7 %copy-start.9 = (bf16[4,128]{1,0:T(4,128)(2,1)S(1)}, bf16[4,128]{1,0:T(4,128)(2,1)}, u32[]{:S(2)}) copy-start(bf16[4,128]{1,0:T(4,128)(2,1)} %refs_15_.1) | copy-start | bytes 3076
  113.4 5.2 %collective-permute-start.10 = (f32[8,128]{1,0:T(8,128)S(1)}, f32[8,128]{1,0:T(8,128)S(1)}, u32[]{:S(2)}, u32[]{:S(2)}) collective-permute-start(f32[8,128]{1,0:T(8,128)S(1)} %get-tuple-element.17), channel_id=1, source_target_pairs={{0,2},{1,3},{2,0},{3,1},{4,6},{5,7},{6,4},{7,5},{8,10},{9,11},{10,... | collective-permute-start | bytes 12296 | tf_op jit(solution)/shard_map/ppermute | solution.py:21
  113.5 5.1 %collective-permute-start.11 = (f32[8,128]{1,0:T(8,128)S(1)}, f32[8,128]{1,0:T(8,128)S(1)}, u32[]{:S(2)}, u32[]{:S(2)}) collective-permute-start(f32[8,128]{1,0:T(8,128)S(1)} %get-tuple-element.17), channel_id=1, source_target_pairs={{0,3},{1,2},{2,1},{3,0},{4,7},{5,6},{6,5},{7,4},{8,11},{9,10},{10,... | collective-permute-start | bytes 12296 | tf_op jit(solution)/shard_map/ppermute | solution.py:21
  116.2 3.6 %collective-permute-start.9 = (f32[8,128]{1,0:T(8,128)S(1)}, f32[8,128]{1,0:T(8,128)S(1)}, u32[]{:S(2)}, u32[]{:S(2)}) collective-permute-start(f32[8,128]{1,0:T(8,128)S(1)} %get-tuple-element.17), channel_id=1, source_target_pairs={{0,1},{1,0},{2,3},{3,2},{4,5},{5,4},{6,7},{7,6},{8,9},{9,8},{10,11... | collective-permute-start | bytes 12296 | tf_op jit(solution)/shard_map/ppermute | solution.py:21
  119.8 1.2 collective-permute-start.12
  120.9 6.2 %collective-permute-start.13 = (f32[2,8,128]{2,1,0:T(8,128)S(1)}, f32[2,8,128]{2,1,0:T(8,128)S(1)}, u32[]{:S(2)}, u32[]{:S(2)}) collective-permute-start(f32[2,8,128]{2,1,0:T(8,128)S(1)} %get-tuple-element.28), channel_id=1, source_target_pairs={{0,8},{8,0},{16,24},{24,16},{32,40},{40,32},{48,56},{56,48},{1,9},... | collective-permute-start | bytes 24584 | tf_op jit(solution)/shard_map/ppermute | solution.py:21
  120.9 7.8 %collective-permute-start.14 = (f32[2,8,128]{2,1,0:T(8,128)S(1)}, f32[2,8,128]{2,1,0:T(8,128)S(1)}, u32[]{:S(2)}, u32[]{:S(2)}) collective-permute-start(f32[2,8,128]{2,1,0:T(8,128)S(1)} %get-tuple-element.28), channel_id=1, source_target_pairs={{0,16},{8,24},{16,0},{24,8},{32,48},{40,56},{48,32},{56,40},{1,17}... | collective-permute-start | bytes 24584 | tf_op jit(solution)/shard_map/ppermute | solution.py:21
  127.2 5.6 %collective-permute-start.15 = (f32[2,8,128]{2,1,0:T(8,128)S(1)}, f32[2,8,128]{2,1,0:T(8,128)S(1)}, u32[]{:S(2)}, u32[]{:S(2)}) collective-permute-start(f32[2,8,128]{2,1,0:T(8,128)S(1)} %get-tuple-element.28), channel_id=1, source_target_pairs={{0,24},{8,16},{16,8},{24,0},{32,56},{40,48},{48,40},{56,32},{1,25}... | collective-permute-start | bytes 24584 | tf_op jit(solution)/shard_map/ppermute | solution.py:21
  132.8 7.8 %collective-permute-start.16 = (f32[4,2,8,128]{3,2,1,0:T(8,128)S(1)}, f32[4,2,8,128]{3,2,1,0:T(8,128)S(1)}, u32[]{:S(2)}, u32[]{:S(2)}) collective-permute-start(f32[4,2,8,128]{3,2,1,0:T(8,128)S(1)} %get-tuple-element.26), channel_id=1, source_target_pairs={{0,32},{8,40},{16,48},{24,56},{32,0},{40,8},{48,16},{56,24},{1,33}... | collective-permute-start | bytes 98312 | tf_op jit(solution)/shard_map/ppermute | solution.py:21
  140.6 4.8 %collective-permute-start.17 = (f32[2,4,2,8,128]{4,3,2,1,0:T(8,128)S(1)}, f32[2,4,2,8,128]{4,3,2,1,0:T(8,128)S(1)}, u32[]{:S(2)}, u32[]{:S(2)}) collective-permute-start(f32[2,4,2,8,128]{4,3,2,1,0:T(8,128)S(1)} %get-tuple-element.24), channel_id=1, source_target_pairs={{0,64},{64,0},{128,192},{192,128},{1,65},{65,1},{129,193},{193,129... | collective-permute-start | bytes 196616 | tf_op jit(solution)/shard_map/ppermute | solution.py:21
  140.7 5.9 %collective-permute-start.18 = (f32[2,4,2,8,128]{4,3,2,1,0:T(8,128)S(1)}, f32[2,4,2,8,128]{4,3,2,1,0:T(8,128)S(1)}, u32[]{:S(2)}, u32[]{:S(2)}) collective-permute-start(f32[2,4,2,8,128]{4,3,2,1,0:T(8,128)S(1)} %get-tuple-element.24), channel_id=1, source_target_pairs={{0,128},{64,192},{128,0},{192,64},{1,129},{65,193},{129,1},{193,65... | collective-permute-start | bytes 196616 | tf_op jit(solution)/shard_map/ppermute | solution.py:21
  140.8 6.8 %collective-permute-start.19 = (f32[2,4,2,8,128]{4,3,2,1,0:T(8,128)S(1)}, f32[2,4,2,8,128]{4,3,2,1,0:T(8,128)S(1)}, u32[]{:S(2)}, u32[]{:S(2)}) collective-permute-start(f32[2,4,2,8,128]{4,3,2,1,0:T(8,128)S(1)} %get-tuple-element.24), channel_id=1, source_target_pairs={{0,192},{64,128},{128,64},{192,0},{1,193},{65,129},{129,65},{193,1... | collective-permute-start | bytes 196616 | tf_op jit(solution)/shard_map/ppermute | solution.py:21

commit v3 on v2

--- a/solution.py
+++ b/solution.py
@@ -593,9 +593,12 @@
 
     own = features.reshape(2, pix, channels)
     state = hidden.reshape(slot_count, pix, hid_width)
-    own1, own3, own2 = [swapped(own, "x", step) for step in (1, 3, 2)]
+    own1, own3 = swapped(own, "x", 1), swapped(own, "x", 3)
     next0 = following(own)
-    next1, next3, next2 = following(own1), following(own3), following(own2)
+    next1, next3 = following(own1), following(own3)
+    half = pix // 2
+    own2a, own2b = swapped(own1[:, :half], "x", 3), swapped(own3[:, half:], "x", 1)
+    next2a, next2b = following(own2a), following(own2b)
     acc, turned_q = first_call(facts, slot_count, col_count, (own, own1, own3), own, next0)
     acc, late = lax.optimization_barrier((acc, state))
     rows_x = lax.axis_size("x")
@@ -611,9 +614,9 @@
         state,
         hide_up,
         hide_down,
-        (own, own1, own3, own2),
-        (next0, next1, next3, next2),
-        1,
+        (own, own1, own3, own2a, own2b),
+        (next0, next1, next3, next2a, next2b),
+        2,
         (wg, wc, w_head),
         poses.T,
         inv_depth,

time: 155 us -> 155 us (level)
  starting transfers between devices: 29.8 us -> 60.5 us
  Pallas kernels: 86.5 us -> 67.2 us
  waiting for transfers between devices: 33.4 us -> 22.8 us
    ppermute x14 -> x15, starting transfers between devices: 18.8 us -> 50.7 us  [swapped(): return lax.ppermute(value, axis, [(i, i ^ step) for i in range(count)])]
    pallas_call x1, Pallas kernels: 70 us -> 53.1 us  [fused_call(): pl.pallas_call(functools.partial(fused_body, dims), in_specs=[SMEM] * 3 +...]
    ppermute x14 -> x15, waiting for transfers between devices: 33.4 us -> 22.7 us  [swapped(): return lax.ppermute(value, axis, [(i, i ^ step) for i in range(count)])]
    ppermute x1, starting transfers between devices: 4.55 us -> 2.02 us  [shards(): lax.ppermute(late[:, :halo], 'x', [(i + 1, i) for i in range(rows_x - 1)])]
    ppermute x4 -> x5, starting transfers between devices: 5.13 us -> 6.43 us  [following(): return lax.ppermute(value, EDGE, [(i + 1, i) for i in range(nodes - 1)])]
  transfers between devices with their start and end apart: 20 -> 22, of which waited for: 10 -> 11; matrix products, arithmetic and copies ran while one was open for 0% -> 0% of each run, Pallas kernels for 7% -> 6%
where the time goes in v3:
time: 155 us; the launch traced here: 154 us
  Pallas kernels  67.2 us (43%)
  starting transfers between devices  60.5 us (39%)
  waiting for transfers between devices  22.8 us (15%)
  local copies, waits for them, and re-layouts  1.76 us (1%)
  between operations  1.6 us (1%)
    pallas_call x1, Pallas kernels, fused_call(): pl.pallas_call(functools.partial(fused_body, dims), in_specs=[SMEM] * 3 +...  53.1 us
    ppermute x15, starting transfers between devices, swapped(): return lax.ppermute(value, axis, [(i, i ^ step) for i in range(count)])  50.7 us
    ppermute x15, waiting for transfers between devices, swapped(): return lax.ppermute(value, axis, [(i, i ^ step) for i in range(count)])  22.7 us
    ppermute x5, starting transfers between devices, following(): return lax.ppermute(value, EDGE, [(i + 1, i) for i in range(nodes - 1)])  6.43 us
    pallas_call x1, Pallas kernels, solve_call(): pl.pallas_call(functools.partial(solve_body, nodes, pix), out_shape=(jax....  5.56 us
    pallas_call x1, Pallas kernels, second_call(): pl.pallas_call(functools.partial(second_body, slots, len(owns)), in_specs...  5.09 us
    pallas_call x1, Pallas kernels, first_call(): pl.pallas_call(functools.partial(first_body, slots), in_specs=[SMEM] * 3...  3.45 us
  transfers between devices with their start and end apart: 22, of which 11 were waited for; matrix products, arithmetic and copies ran while one was open for 0% of the time, Pallas kernels for 6%

profile of v3, /device:TPU:6, one launch (start us, length us, event | category | flops | bytes accessed | tf_op | source)
XLA Modules:
  0.0 153.9 jit_solution(8214827529137501148)
XLA Ops:
  0.6 0.9 collective-permute-start
  1.5 1.5 collective-permute-start.1
  3.0 1.3 collective-permute-start.2
  5.0 0.1 pad_add_fusion.ranks.info
  5.1 6.7 %collective-permute-done.side1.refs_0_.refs_6_ = bf16[2,768,128]{2,1,0:T(8,128)(2,1)S(1)} collective-permute-done((bf16[2,768,128]{2,1,0:T(8,128)(2,1)}, bf16[2,768,128]{2,1,0:T(8,128)(2,1)S(1)}, u32[]{:S(2)}, u32[]{:S(2)}) %collective-permute-start) | collective-permute-done | bytes 393248 | tf_op jit(solution)/shard_map/ppermute | solution.py:21
  11.8 1.3 collective-permute-start.3
  13.1 0.5 collective-permute-done.1.side3.refs_1_.refs_7_
  13.5 1.3 collective-permute-start.4
  14.8 0.0 collective-permute-done.2.after.refs_10_
  14.8 0.0 copy-start.3
  14.9 1.0 copy-done.3
  15.8 0.7 copy-done.7
  16.5 3.5 %match_first.1 = (f32[4,136,1024]{2,1,0:T(8,128)S(1)}, bf16[4,128,1024]{2,1,0:T(8,128)(2,1)S(1)}) custom-call(s32[2,4]{1,0:T(2,128)S(1)} %bitcast.37, s32[1]{0:T(128)S(6)} %copy.12.counts, s32[2]{0:T(128)S(1)} %pad_add_fusion.ranks.info, bf16[2,768,128]{2,1,0:T(8,128)(2,1)S(1)} %bitcast.33, ...), custom_call_target="tpu_custom_call" | custom-call | flops 3221225472 | bytes 4456448 | tf_op jit(solution)/shard_map/match_first/pallas_call | solution.py:513
  20.0 0.5 collective-permute-start.8
  20.5 1.2 collective-permute-start.7
  21.7 0.0 copy-done
  21.7 1.3 collective-permute-start.5
  23.0 3.9 %collective-permute-done.8.refs_9_ = bf16[2,384,128]{2,1,0:T(8,128)(2,1)S(1)} collective-permute-done((bf16[2,384,128]{2,1,0:T(8,128)(2,1)S(1)}, bf16[2,384,128]{2,1,0:T(8,128)(2,1)S(1)}, u32[]{:S(2)}, u32[]{:S(2)}) %collective-permute-start.8) | collective-permute-done | bytes 196640 | tf_op jit(solution)/shard_map/ppermute | solution.py:21
  27.0 2.0 %collective-permute-start.6 = (bf16[4,128,128]{2,1,0:T(8,128)(2,1)S(1)}, bf16[4,128,128]{2,1,0:T(8,128)(2,1)S(1)}, u32[]{:S(2)}, u32[]{:S(2)}) collective-permute-start(bf16[4,128,128]{2,1,0:T(8,128)(2,1)S(1)} %get-tuple-element.21), channel_id=1, source_target_pairs={{1,0},{2,1},{3,2},{5,4},{6,5},{7,6},{9,8},{10,9},{11,10},{13,12},{... | collective-permute-start | bytes 393224 | tf_op jit(solution)/shard_map/ppermute | solution.py:606
  29.0 0.0 collective-permute-done.7.refs_8_
  29.0 1.3 collective-permute-start.10
  30.3 0.0 collective-permute-done.3.refs_2_.refs_11_
  30.3 1.3 collective-permute-start.9
  31.6 0.0 collective-permute-done.4.refs_3_.refs_12_
  31.6 0.0 copy-start.1
  31.7 0.0 copy-start.2
  31.7 0.0 copy-start.4
  31.7 0.0 copy-start.5
  31.7 0.0 copy-start.6
  31.7 0.0 copy-start.8
  31.7 0.0 copy-start.9
  31.7 5.1 %match_second.1.refs_1_ = f32[4,136,1024]{2,1,0:T(8,128)S(1)} custom-call(s32[2,4]{1,0:T(2,128)S(1)} %bitcast.38, s32[1]{0:T(128)S(6)} %copy.12.counts, s32[2]{0:T(128)S(1)} %pad_add_fusion.ranks.info, bf16[4,128,1024]{2,1,0:T(8,128)(2,1)S(1)} %get-tuple-element.12.qt_ref.refs_0_, f32[4,136,1024]{2,1,0:T(8,128)S(1)} %get-tuple-element.14.old, ...), custom_call_target="tpu_custom_call" | custom-call | flops 6442450944 | bytes 4456448 | tf_op jit(solution)/shard_map/match_second/pallas_call | solution.py:531
  36.8 0.0 collective-permute-done.5.refs_3_
  36.8 0.0 collective-permute-done.6.refs_4_
  36.8 0.0 collective-permute-done.10.refs_14_
  36.9 0.0 collective-permute-done.9.refs_13_
  36.9 0.0 copy-done.1
  36.9 0.0 copy-done.2
  36.9 0.0 copy-done.4
  36.9 0.0 copy-done.5
  36.9 53.1 %match_update.1 = (bf16[4,768,128]{2,1,0:T(8,128)(2,1)}, f32[8,128]{1,0:T(8,128)S(1)}, f32[40,1536]{1,0:T(8,128)S(1)}) custom-call(s32[2,4]{1,0:T(2,128)S(1)} %bitcast.39, s32[1]{0:T(128)S(6)} %copy.12.counts, s32[2]{0:T(128)S(1)} %pad_add_fusion.ranks.info, bf16[4,128,1024]{2,1,0:T(8,128)(2,1)S(1)} %get-tuple-element.12.qt_ref.refs_0_, ...), custom_call_target="tpu_custom_call" | custom-call | tf_op jit(solution)/shard_map/match_update/pallas_call | solution.py:550
  90.0 0.6 collective-permute-start.11
  90.6 1.2 collective-permute-start.12
  91.8 3.0 %collective-permute-start.13 = (f32[8,128]{1,0:T(8,128)S(1)}, f32[8,128]{1,0:T(8,128)S(1)}, u32[]{:S(2)}, u32[]{:S(2)}) collective-permute-start(f32[8,128]{1,0:T(8,128)S(1)} %get-tuple-element.17), channel_id=1, source_target_pairs={{0,3},{1,2},{2,1},{3,0},{4,7},{5,6},{6,5},{7,4},{8,11},{9,10},{10,... | collective-permute-start | bytes 12296 | tf_op jit(solution)/shard_map/ppermute | solution.py:21
  94.8 0.0 collective-permute-done.11
  94.8 0.9 collective-permute-done.12
  95.7 0.9 collective-permute-done.13
  96.6 0.0 collective-permute-start.14
  96.6 1.2 collective-permute-done.14
  97.8 0.0 collective-permute-start.15
  97.8 0.0 collective-permute-start.16
  97.8 4.4 %collective-permute-start.17 = (f32[2,8,128]{2,1,0:T(8,128)S(1)}, f32[2,8,128]{2,1,0:T(8,128)S(1)}, u32[]{:S(2)}, u32[]{:S(2)}) collective-permute-start(f32[2,8,128]{2,1,0:T(8,128)S(1)} %get-tuple-element.28), channel_id=1, source_target_pairs={{0,24},{8,16},{16,8},{24,0},{32,56},{40,48},{48,40},{56,32},{1,25}... | collective-permute-start | bytes 24584 | tf_op jit(solution)/shard_map/ppermute | solution.py:21
  102.2 0.0 collective-permute-done.15
  102.2 0.2 collective-permute-done.16
  102.3 1.5 %collective-permute-done.17 = f32[2,8,128]{2,1,0:T(8,128)S(1)} collective-permute-done((f32[2,8,128]{2,1,0:T(8,128)S(1)}, f32[2,8,128]{2,1,0:T(8,128)S(1)}, u32[]{:S(2)}, u32[]{:S(2)}) %collective-permute-start.17) | collective-permute-done | bytes 8224 | tf_op jit(solution)/shard_map/ppermute | solution.py:21
  103.9 27.0 %collective-permute-start.18 = (f32[4,2,8,128]{3,2,1,0:T(8,128)S(1)}, f32[4,2,8,128]{3,2,1,0:T(8,128)S(1)}, u32[]{:S(2)}, u32[]{:S(2)}) collective-permute-start(f32[4,2,8,128]{3,2,1,0:T(8,128)S(1)} %get-tuple-element.26), channel_id=1, source_target_pairs={{0,32},{8,40},{16,48},{24,56},{32,0},{40,8},{48,16},{56,24},{1,33}... | collective-permute-start | bytes 98312 | tf_op jit(solution)/shard_map/ppermute | solution.py:21
  130.9 1.9 %collective-permute-done.18 = f32[4,2,8,128]{3,2,1,0:T(8,128)S(1)} collective-permute-done((f32[4,2,8,128]{3,2,1,0:T(8,128)S(1)}, f32[4,2,8,128]{3,2,1,0:T(8,128)S(1)}, u32[]{:S(2)}, u32[]{:S(2)}) %collective-permute-start.18) | collective-permute-done | bytes 32800 | tf_op jit(solution)/shard_map/ppermute | solution.py:21
  132.9 4.8 %collective-permute-start.19 = (f32[2,4,2,8,128]{4,3,2,1,0:T(8,128)S(1)}, f32[2,4,2,8,128]{4,3,2,1,0:T(8,128)S(1)}, u32[]{:S(2)}, u32[]{:S(2)}) collective-permute-start(f32[2,4,2,8,128]{4,3,2,1,0:T(8,128)S(1)} %get-tuple-element.24), channel_id=1, source_target_pairs={{0,64},{64,0},{128,192},{192,128},{1,65},{65,1},{129,193},{193,129... | collective-permute-start | bytes 196616 | tf_op jit(solution)/shard_map/ppermute | solution.py:21
  137.6 5.2 %collective-permute-start.20 = (f32[2,4,2,8,128]{4,3,2,1,0:T(8,128)S(1)}, f32[2,4,2,8,128]{4,3,2,1,0:T(8,128)S(1)}, u32[]{:S(2)}, u32[]{:S(2)}) collective-permute-start(f32[2,4,2,8,128]{4,3,2,1,0:T(8,128)S(1)} %get-tuple-element.24), channel_id=1, source_target_pairs={{0,128},{64,192},{128,0},{192,64},{1,129},{65,193},{129,1},{193,65... | collective-permute-start | bytes 196616 | tf_op jit(solution)/shard_map/ppermute | solution.py:21
  142.8 0.5 collective-permute-start.21
  143.3 0.0 collective-permute-done.19
  143.3 2.5 %collective-permute-done.20 = f32[2,4,2,8,128]{4,3,2,1,0:T(8,128)S(1)} collective-permute-done((f32[2,4,2,8,128]{4,3,2,1,0:T(8,128)S(1)}, f32[2,4,2,8,128]{4,3,2,1,0:T(8,128)S(1)}, u32[]{:S(2)}, u32[]{:S(2)}) %collective-permute-start.20) | collective-permute-done | bytes 65568 | tf_op jit(solution)/shard_map/ppermute | solution.py:21
  145.8 2.5 %collective-permute-done.21 = f32[2,4,2,8,128]{4,3,2,1,0:T(8,128)S(1)} collective-permute-done((f32[2,4,2,8,128]{4,3,2,1,0:T(8,128)S(1)}, f32[2,4,2,8,128]{4,3,2,1,0:T(8,128)S(1)}, u32[]{:S(2)}, u32[]{:S(2)}) %collective-permute-start.21) | collective-permute-done | bytes 65568 | tf_op jit(solution)/shard_map/ppermute | solution.py:21
  148.3 5.6 %pose_solve.1 = (f32[2,6]{1,0:T(2,128)}, f32[2,768]{1,0:T(2,128)}) custom-call(s32[2]{0:T(128)S(1)} %pad_add_fusion.ranks.info, f32[64,8,128]{2,1,0:T(8,128)S(1)} %bitcast.28, f32[40,1536]{1,0:T(8,128)S(1)} %get-tuple-element.18.h_ref), custom_call_target="tpu_custom_call" | custom-call | tf_op jit(solution)/shard_map/pose_solve/pallas_call | solution.py:239
  (13 shorter events, 0.1 us)
Async XLA Ops:
  0.6 11.2 %collective-permute-start = (bf16[2,768,128]{2,1,0:T(8,128)(2,1)}, bf16[2,768,128]{2,1,0:T(8,128)(2,1)S(1)}, u32[]{:S(2)}, u32[]{:S(2)}) collective-permute-start(bf16[2,768,128]{2,1,0:T(8,128)(2,1)} %bitcast.30), channel_id=1, source_target_pairs={{0,1},{1,0},{2,3},{3,2},{4,5},{5,4},{6,7},{7,6},{8,9},{9,8},{10,11... | collective-permute-start | bytes 1179656 | tf_op jit(solution)/shard_map/ppermute | solution.py:21
  1.5 12.0 %collective-permute-start.1 = (bf16[2,768,128]{2,1,0:T(8,128)(2,1)}, bf16[2,768,128]{2,1,0:T(8,128)(2,1)S(1)}, u32[]{:S(2)}, u32[]{:S(2)}) collective-permute-start(bf16[2,768,128]{2,1,0:T(8,128)(2,1)} %bitcast.31), channel_id=1, source_target_pairs={{0,3},{1,2},{2,1},{3,0},{4,7},{5,6},{6,5},{7,4},{8,11},{9,10},{10,... | collective-permute-start | bytes 1179656 | tf_op jit(solution)/shard_map/ppermute | solution.py:21
  3.0 11.8 %collective-permute-start.2 = (bf16[2,768,128]{2,1,0:T(8,128)(2,1)}, bf16[2,768,128]{2,1,0:T(8,128)(2,1)S(1)}, u32[]{:S(2)}, u32[]{:S(2)}) collective-permute-start(bf16[2,768,128]{2,1,0:T(8,128)(2,1)} %bitcast.32), channel_id=1, source_target_pairs={{4,0},{8,4},{12,8},{16,12},{20,16},{24,20},{28,24},{32,28},{36,32}... | collective-permute-start | bytes 1179656 | tf_op jit(solution)/shard_map/ppermute | solution.py:592
  11.8 18.5 %collective-permute-start.3 = (bf16[2,768,128]{2,1,0:T(8,128)(2,1)S(1)}, bf16[2,768,128]{2,1,0:T(8,128)(2,1)S(1)}, u32[]{:S(2)}, u32[]{:S(2)}) collective-permute-start(bf16[2,768,128]{2,1,0:T(8,128)(2,1)S(1)} %collective-permute-done.side1.refs_0_.refs_6_), channel_id=1, source_target_pairs={{4,0},{8,4},{12,8},{16,12},{20,16},{24,20},{28,24},{32,28},{36,32}... | collective-permute-start | bytes 1179656 | tf_op jit(solution)/shard_map/ppermute | solution.py:592
  13.5 18.1 %collective-permute-start.4 = (bf16[2,768,128]{2,1,0:T(8,128)(2,1)S(1)}, bf16[2,768,128]{2,1,0:T(8,128)(2,1)S(1)}, u32[]{:S(2)}, u32[]{:S(2)}) collective-permute-start(bf16[2,768,128]{2,1,0:T(8,128)(2,1)S(1)} %collective-permute-done.1.side3.refs_1_.refs_7_), channel_id=1, source_target_pairs={{4,0},{8,4},{12,8},{16,12},{20,16},{24,20},{28,24},{32,28},{36,32}... | collective-permute-start | bytes 1179656 | tf_op jit(solution)/shard_map/ppermute | solution.py:592
  14.8 1.0 copy-start.3
  15.8 0.7 copy-start.7
  16.5 5.2 %copy-start = (bf16[4,12,64,128]{3,2,1,0:T(8,128)(2,1)S(1)}, bf16[4,12,64,128]{3,2,1,0:T(8,128)(2,1)}, u32[]{:S(2)}) copy-start(bf16[4,12,64,128]{3,2,1,0:T(8,128)(2,1)} %param.12) | copy-start | bytes 2359300
  20.0 7.0 %collective-permute-start.8 = (bf16[2,384,128]{2,1,0:T(8,128)(2,1)S(1)}, bf16[2,384,128]{2,1,0:T(8,128)(2,1)S(1)}, u32[]{:S(2)}, u32[]{:S(2)}) collective-permute-start(bf16[2,384,128]{2,1,0:T(8,128)(2,1)S(1)} %slice.17), channel_id=1, source_target_pairs={{0,1},{1,0},{2,3},{3,2},{4,5},{5,4},{6,7},{7,6},{8,9},{9,8},{10,11... | collective-permute-start | bytes 589832 | tf_op jit(solution)/shard_map/ppermute | solution.py:21
  20.5 8.5 %collective-permute-start.7 = (bf16[2,384,128]{2,1,0:T(8,128)(2,1)S(1)}, bf16[2,384,128]{2,1,0:T(8,128)(2,1)S(1)}, u32[]{:S(2)}, u32[]{:S(2)}) collective-permute-start(bf16[2,384,128]{2,1,0:T(8,128)(2,1)S(1)} %slice.16), channel_id=1, source_target_pairs={{0,3},{1,2},{2,1},{3,0},{4,7},{5,6},{6,5},{7,4},{8,11},{9,10},{10,... | collective-permute-start | bytes 589832 | tf_op jit(solution)/shard_map/ppermute | solution.py:21
  21.7 15.1 %collective-permute-start.5 = (bf16[4,128,128]{2,1,0:T(8,128)(2,1)S(1)}, bf16[4,128,128]{2,1,0:T(8,128)(2,1)S(1)}, u32[]{:S(2)}, u32[]{:S(2)}) collective-permute-start(bf16[4,128,128]{2,1,0:T(8,128)(2,1)S(1)} %get-tuple-element.22), channel_id=1, source_target_pairs={{0,1},{1,2},{2,3},{4,5},{5,6},{6,7},{8,9},{9,10},{10,11},{12,13},{... | collective-permute-start | bytes 393224 | tf_op jit(solution)/shard_map/ppermute | solution.py:605
  27.0 9.9 %collective-permute-start.6 = (bf16[4,128,128]{2,1,0:T(8,128)(2,1)S(1)}, bf16[4,128,128]{2,1,0:T(8,128)(2,1)S(1)}, u32[]{:S(2)}, u32[]{:S(2)}) collective-permute-start(bf16[4,128,128]{2,1,0:T(8,128)(2,1)S(1)} %get-tuple-element.21), channel_id=1, source_target_pairs={{1,0},{2,1},{3,2},{5,4},{6,5},{7,6},{9,8},{10,9},{11,10},{13,12},{... | collective-permute-start | bytes 393224 | tf_op jit(solution)/shard_map/ppermute | solution.py:606
  29.0 7.8 %collective-permute-start.10 = (bf16[2,384,128]{2,1,0:T(8,128)(2,1)S(1)}, bf16[2,384,128]{2,1,0:T(8,128)(2,1)S(1)}, u32[]{:S(2)}, u32[]{:S(2)}) collective-permute-start(bf16[2,384,128]{2,1,0:T(8,128)(2,1)S(1)} %collective-permute-done.8.refs_9_), channel_id=1, source_target_pairs={{4,0},{8,4},{12,8},{16,12},{20,16},{24,20},{28,24},{32,28},{36,32}... | collective-permute-start | bytes 589832 | tf_op jit(solution)/shard_map/ppermute | solution.py:592
  30.3 6.5 %collective-permute-start.9 = (bf16[2,384,128]{2,1,0:T(8,128)(2,1)S(1)}, bf16[2,384,128]{2,1,0:T(8,128)(2,1)S(1)}, u32[]{:S(2)}, u32[]{:S(2)}) collective-permute-start(bf16[2,384,128]{2,1,0:T(8,128)(2,1)S(1)} %collective-permute-done.7.refs_8_), channel_id=1, source_target_pairs={{4,0},{8,4},{12,8},{16,12},{20,16},{24,20},{28,24},{32,28},{36,32}... | collective-permute-start | bytes 589832 | tf_op jit(solution)/shard_map/ppermute | solution.py:592
  31.6 5.2 %copy-start.1 = (bf16[9,256,256]{2,1,0:T(8,128)(2,1)S(1)}, bf16[9,256,256]{2,1,0:T(8,128)(2,1)}, u32[]{:S(2)}) copy-start(bf16[9,256,256]{2,1,0:T(8,128)(2,1)} %param.15) | copy-start | bytes 3538948
  31.7 5.2 %copy-start.2 = (bf16[9,256,128]{2,1,0:T(8,128)(2,1)S(1)}, bf16[9,256,128]{2,1,0:T(8,128)(2,1)}, u32[]{:S(2)}) copy-start(bf16[9,256,128]{2,1,0:T(8,128)(2,1)} %param.16) | copy-start | bytes 1769476
  31.7 5.2 %copy-start.4 = (bf16[2,12,64,128]{3,2,1,0:T(8,128)(2,1)S(1)}, bf16[2,12,64,128]{3,2,1,0:T(8,128)(2,1)}, u32[]{:S(2)}) copy-start(bf16[2,12,64,128]{3,2,1,0:T(8,128)(2,1)} %param.9) | copy-start | bytes 1179652
  31.7 5.2 %copy-start.5 = (f32[2,768]{1,0:T(2,128)S(1)}, f32[2,768]{1,0:T(2,128)}, u32[]{:S(2)}) copy-start(f32[2,768]{1,0:T(2,128)} %refs_19_.1) | copy-start | bytes 18436
  31.7 5.2 %copy-start.6 = (f32[128,6]{0,1:T(8,128)S(1)}, f32[128,6]{0,1:T(8,128)}, u32[]{:S(2)}) copy-start(f32[128,6]{0,1:T(8,128)} %param.10) | copy-start | bytes 9220
  31.7 5.2 %copy-start.8 = (s32[4,2]{0,1:T(2,128)S(1)}, s32[4,2]{0,1:T(2,128)}, u32[]{:S(2)}) copy-start(s32[4,2]{0,1:T(2,128)} %param.13) | copy-start | bytes 100
  31.7 5.2 %copy-start.9 = (bf16[4,128]{1,0:T(4,128)(2,1)S(1)}, bf16[4,128]{1,0:T(4,128)(2,1)}, u32[]{:S(2)}) copy-start(bf16[4,128]{1,0:T(4,128)(2,1)} %refs_17_.1) | copy-start | bytes 3076
  90.0 4.8 %collective-permute-start.11 = (f32[8,128]{1,0:T(8,128)S(1)}, f32[8,128]{1,0:T(8,128)S(1)}, u32[]{:S(2)}, u32[]{:S(2)}) collective-permute-start(f32[8,128]{1,0:T(8,128)S(1)} %get-tuple-element.17), channel_id=1, source_target_pairs={{0,1},{1,0},{2,3},{3,2},{4,5},{5,4},{6,7},{7,6},{8,9},{9,8},{10,11... | collective-permute-start | bytes 12296 | tf_op jit(solution)/shard_map/ppermute | solution.py:21
  90.6 5.1 %collective-permute-start.12 = (f32[8,128]{1,0:T(8,128)S(1)}, f32[8,128]{1,0:T(8,128)S(1)}, u32[]{:S(2)}, u32[]{:S(2)}) collective-permute-start(f32[8,128]{1,0:T(8,128)S(1)} %get-tuple-element.17), channel_id=1, source_target_pairs={{0,2},{1,3},{2,0},{3,1},{4,6},{5,7},{6,4},{7,5},{8,10},{9,11},{10,... | collective-permute-start | bytes 12296 | tf_op jit(solution)/shard_map/ppermute | solution.py:21
  91.8 4.8 %collective-permute-start.13 = (f32[8,128]{1,0:T(8,128)S(1)}, f32[8,128]{1,0:T(8,128)S(1)}, u32[]{:S(2)}, u32[]{:S(2)}) collective-permute-start(f32[8,128]{1,0:T(8,128)S(1)} %get-tuple-element.17), channel_id=1, source_target_pairs={{0,3},{1,2},{2,1},{3,0},{4,7},{5,6},{6,5},{7,4},{8,11},{9,10},{10,... | collective-permute-start | bytes 12296 | tf_op jit(solution)/shard_map/ppermute | solution.py:21
  96.6 1.2 collective-permute-start.14
  97.8 4.4 %collective-permute-start.15 = (f32[2,8,128]{2,1,0:T(8,128)S(1)}, f32[2,8,128]{2,1,0:T(8,128)S(1)}, u32[]{:S(2)}, u32[]{:S(2)}) collective-permute-start(f32[2,8,128]{2,1,0:T(8,128)S(1)} %get-tuple-element.28), channel_id=1, source_target_pairs={{0,8},{8,0},{16,24},{24,16},{32,40},{40,32},{48,56},{56,48},{1,9},... | collective-permute-start | bytes 24584 | tf_op jit(solution)/shard_map/ppermute | solution.py:21
  97.8 4.6 %collective-permute-start.16 = (f32[2,8,128]{2,1,0:T(8,128)S(1)}, f32[2,8,128]{2,1,0:T(8,128)S(1)}, u32[]{:S(2)}, u32[]{:S(2)}) collective-permute-start(f32[2,8,128]{2,1,0:T(8,128)S(1)} %get-tuple-element.28), channel_id=1, source_target_pairs={{0,16},{8,24},{16,0},{24,8},{32,48},{40,56},{48,32},{56,40},{1,17}... | collective-permute-start | bytes 24584 | tf_op jit(solution)/shard_map/ppermute | solution.py:21
  97.8 6.1 %collective-permute-start.17 = (f32[2,8,128]{2,1,0:T(8,128)S(1)}, f32[2,8,128]{2,1,0:T(8,128)S(1)}, u32[]{:S(2)}, u32[]{:S(2)}) collective-permute-start(f32[2,8,128]{2,1,0:T(8,128)S(1)} %get-tuple-element.28), channel_id=1, source_target_pairs={{0,24},{8,16},{16,8},{24,0},{32,56},{40,48},{48,40},{56,32},{1,25}... | collective-permute-start | bytes 24584 | tf_op jit(solution)/shard_map/ppermute | solution.py:21
  103.9 28.9 %collective-permute-start.18 = (f32[4,2,8,128]{3,2,1,0:T(8,128)S(1)}, f32[4,2,8,128]{3,2,1,0:T(8,128)S(1)}, u32[]{:S(2)}, u32[]{:S(2)}) collective-permute-start(f32[4,2,8,128]{3,2,1,0:T(8,128)S(1)} %get-tuple-element.26), channel_id=1, source_target_pairs={{0,32},{8,40},{16,48},{24,56},{32,0},{40,8},{48,16},{56,24},{1,33}... | collective-permute-start | bytes 98312 | tf_op jit(solution)/shard_map/ppermute | solution.py:21
  132.9 10.4 %collective-permute-start.19 = (f32[2,4,2,8,128]{4,3,2,1,0:T(8,128)S(1)}, f32[2,4,2,8,128]{4,3,2,1,0:T(8,128)S(1)}, u32[]{:S(2)}, u32[]{:S(2)}) collective-permute-start(f32[2,4,2,8,128]{4,3,2,1,0:T(8,128)S(1)} %get-tuple-element.24), channel_id=1, source_target_pairs={{0,64},{64,0},{128,192},{192,128},{1,65},{65,1},{129,193},{193,129... | collective-permute-start | bytes 196616 | tf_op jit(solution)/shard_map/ppermute | solution.py:21
  137.6 8.1 %collective-permute-start.20 = (f32[2,4,2,8,128]{4,3,2,1,0:T(8,128)S(1)}, f32[2,4,2,8,128]{4,3,2,1,0:T(8,128)S(1)}, u32[]{:S(2)}, u32[]{:S(2)}) collective-permute-start(f32[2,4,2,8,128]{4,3,2,1,0:T(8,128)S(1)} %get-tuple-element.24), channel_id=1, source_target_pairs={{0,128},{64,192},{128,0},{192,64},{1,129},{65,193},{129,1},{193,65... | collective-permute-start | bytes 196616 | tf_op jit(solution)/shard_map/ppermute | solution.py:21
  142.8 5.5 %collective-permute-start.21 = (f32[2,4,2,8,128]{4,3,2,1,0:T(8,128)S(1)}, f32[2,4,2,8,128]{4,3,2,1,0:T(8,128)S(1)}, u32[]{:S(2)}, u32[]{:S(2)}) collective-permute-start(f32[2,4,2,8,128]{4,3,2,1,0:T(8,128)S(1)} %get-tuple-element.24), channel_id=1, source_target_pairs={{0,192},{64,128},{128,64},{192,0},{1,193},{65,129},{129,65},{193,1... | collective-permute-start | bytes 196616 | tf_op jit(solution)/shard_map/ppermute | solution.py:21

commit v4 on v3

--- a/solution.py
+++ b/solution.py
@@ -600,10 +600,9 @@
     own2a, own2b = swapped(own1[:, :half], "x", 3), swapped(own3[:, half:], "x", 1)
     next2a, next2b = following(own2a), following(own2b)
     acc, turned_q = first_call(facts, slot_count, col_count, (own, own1, own3), own, next0)
-    acc, late = lax.optimization_barrier((acc, state))
     rows_x = lax.axis_size("x")
-    hide_up = lax.ppermute(late[:, pix - halo :], "x", [(i, i + 1) for i in range(rows_x - 1)])
-    hide_down = lax.ppermute(late[:, :halo], "x", [(i + 1, i) for i in range(rows_x - 1)])
+    hide_up = lax.ppermute(state[:, pix - halo :], "x", [(i, i + 1) for i in range(rows_x - 1)])
+    hide_down = lax.ppermute(state[:, :halo], "x", [(i + 1, i) for i in range(rows_x - 1)])
     acc = second_call(facts, turned_q, acc, (own1, own3), (next1, next3))
     wg = w_gates.reshape(3, -1, w_gates.shape[2])
     wc = w_cand.reshape(3, -1, w_cand.shape[2])

time: 155 us -> 152 us (0.981)
  Pallas kernels: 67.2 us -> 28.4 us
  starting transfers between devices: 60.5 us -> 93.2 us
  waiting for transfers between devices: 22.8 us -> 24.9 us
    pallas_call x1, Pallas kernels: 53.1 us -> 19.3 us  [fused_call(): pl.pallas_call(functools.partial(fused_body, dims), in_specs=[SMEM] * 3 +...]
    ppermute x15, starting transfers between devices: 50.7 us -> 82.2 us  [swapped(): return lax.ppermute(value, axis, [(i, i ^ step) for i in range(count)])]
    pallas_call x1, Pallas kernels: 5.09 us -> 2.06 us  [second_call(): pl.pallas_call(functools.partial(second_body, slots, len(owns)), in_specs...]
    pallas_call x1, Pallas kernels: 3.45 us -> 1.52 us  [first_call(): pl.pallas_call(functools.partial(first_body, slots), in_specs=[SMEM] * 3...]
    ppermute x15, waiting for transfers between devices: 22.7 us -> 24.5 us  [swapped(): return lax.ppermute(value, axis, [(i, i ^ step) for i in range(count)])]
  transfers between devices with their start and end apart: 22 -> 22, of which waited for: 11 -> 11; matrix products, arithmetic and copies ran while one was open for 0% -> 1% of each run, Pallas kernels for 6% -> 2%
where the time goes in v4:
time: 152 us; the launch traced here: 151 us
  starting transfers between devices  93.2 us (61%)
  Pallas kernels  28.4 us (19%)
  waiting for transfers between devices  24.9 us (16%)
  local copies, waits for them, and re-layouts  2.74 us (2%)
  between operations  1.58 us (1%)
    ppermute x15, starting transfers between devices, swapped(): return lax.ppermute(value, axis, [(i, i ^ step) for i in range(count)])  82.2 us
    ppermute x15, waiting for transfers between devices, swapped(): return lax.ppermute(value, axis, [(i, i ^ step) for i in range(count)])  24.5 us
    pallas_call x1, Pallas kernels, fused_call(): pl.pallas_call(functools.partial(fused_body, dims), in_specs=[SMEM] * 3 +...  19.3 us
    ppermute x5, starting transfers between devices, following(): return lax.ppermute(value, EDGE, [(i + 1, i) for i in range(nodes - 1)])  6.44 us
    pallas_call x1, Pallas kernels, solve_call(): pl.pallas_call(functools.partial(solve_body, nodes, pix), out_shape=(jax....  5.56 us
    ppermute x1, starting transfers between devices, shards(): lax.ppermute(state[:, :halo], 'x', [(i + 1, i) for i in range(rows_x - 1)])  3.31 us
  transfers between devices with their start and end apart: 22, of which 11 were waited for; matrix products, arithmetic and copies ran while one was open for 1% of the time, Pallas kernels for 2%

profile of v4, /device:TPU:6, one launch (start us, length us, event | category | flops | bytes accessed | tf_op | source)
XLA Modules:
  0.0 151.0 jit_solution(2234959434249575994)
XLA Ops:
  0.6 0.9 collective-permute-start
  1.5 1.5 collective-permute-start.1
  3.0 1.3 collective-permute-start.2
  4.3 1.0 fusion.3
  5.3 1.3 collective-permute-start.5
  7.3 5.3 %collective-permute-done.side1.refs_0_.refs_6_ = bf16[2,768,128]{2,1,0:T(8,128)(2,1)S(1)} collective-permute-done((bf16[2,768,128]{2,1,0:T(8,128)(2,1)}, bf16[2,768,128]{2,1,0:T(8,128)(2,1)S(1)}, u32[]{:S(2)}, u32[]{:S(2)}) %collective-permute-start) | collective-permute-done | bytes 393248 | tf_op jit(solution)/shard_map/ppermute | solution.py:21
  12.6 1.3 collective-permute-start.3
  13.8 0.0 collective-permute-done.1.side3.refs_1_.refs_7_
  13.9 1.3 collective-permute-start.4
  15.2 0.1 pad_add_fusion.ranks.info
  15.3 1.0 collective-permute-start.8
  16.2 0.0 collective-permute-done.2.after.refs_10_
  16.2 0.8 collective-permute-start.7
  17.1 1.0 copy-done.3
  18.0 0.7 copy-done.7
  18.7 1.5 %match_first.1 = (f32[4,136,1024]{2,1,0:T(8,128)S(1)}, bf16[4,128,1024]{2,1,0:T(8,128)(2,1)S(1)}) custom-call(s32[2,4]{1,0:T(2,128)S(1)} %bitcast.37, s32[1]{0:T(128)S(6)} %copy.12.counts, s32[2]{0:T(128)S(1)} %pad_add_fusion.ranks.info, bf16[2,768,128]{2,1,0:T(8,128)(2,1)S(1)} %bitcast.33, ...), custom_call_target="tpu_custom_call" | custom-call | flops 3221225472 | bytes 4456448 | tf_op jit(solution)/shard_map/match_first/pallas_call | solution.py:513
  20.3 2.1 %collective-permute-done.8.refs_9_ = bf16[2,384,128]{2,1,0:T(8,128)(2,1)S(1)} collective-permute-done((bf16[2,384,128]{2,1,0:T(8,128)(2,1)S(1)}, bf16[2,384,128]{2,1,0:T(8,128)(2,1)S(1)}, u32[]{:S(2)}, u32[]{:S(2)}) %collective-permute-start.8) | collective-permute-done | bytes 196640 | tf_op jit(solution)/shard_map/ppermute | solution.py:21
  22.4 3.3 %collective-permute-start.6 = (bf16[4,128,128]{2,1,0:T(8,128)(2,1)S(1)}, bf16[4,128,128]{2,1,0:T(8,128)(2,1)S(1)}, u32[]{:S(2)}, u32[]{:S(2)}) collective-permute-start(bf16[4,128,128]{2,1,0:T(8,128)(2,1)S(1)} %get-tuple-element.17), channel_id=1, source_target_pairs={{1,0},{2,1},{3,2},{5,4},{6,5},{7,6},{9,8},{10,9},{11,10},{13,12},{... | collective-permute-start | bytes 393224 | tf_op jit(solution)/shard_map/ppermute | solution.py:605
  25.7 0.0 collective-permute-done.7.refs_8_
  25.7 1.3 collective-permute-start.10
  27.0 0.0 collective-permute-done.3.refs_2_.refs_11_
  27.0 1.3 collective-permute-start.9
  28.3 0.0 collective-permute-done.4.refs_3_.refs_12_
  28.3 0.0 copy-start
  28.3 0.0 copy-start.1
  28.3 0.0 copy-start.2
  28.3 0.0 copy-start.4
  28.4 0.0 copy-start.5
  28.4 0.0 copy-start.6
  28.4 0.0 copy-start.8
  28.4 0.0 copy-start.9
  28.4 2.1 %match_second.1.refs_1_ = f32[4,136,1024]{2,1,0:T(8,128)S(1)} custom-call(s32[2,4]{1,0:T(2,128)S(1)} %bitcast.38, s32[1]{0:T(128)S(6)} %copy.12.counts, s32[2]{0:T(128)S(1)} %pad_add_fusion.ranks.info, bf16[4,128,1024]{2,1,0:T(8,128)(2,1)S(1)} %get-tuple-element.10.qt_ref.refs_0_, f32[4,136,1024]{2,1,0:T(8,128)S(1)} %get-tuple-element.11.old, ...), custom_call_target="tpu_custom_call" | custom-call | flops 6442450944 | bytes 4456448 | tf_op jit(solution)/shard_map/match_second/pallas_call | solution.py:531
  30.5 0.0 collective-permute-done.5.refs_3_
  30.5 0.0 collective-permute-done.6.refs_4_
  30.5 0.0 collective-permute-done.10.refs_14_
  30.5 0.5 collective-permute-done.9.refs_13_
  31.0 0.0 copy-done
  31.0 0.0 copy-done.1
  31.0 0.0 copy-done.2
  31.0 0.0 copy-done.4
  31.0 19.3 %match_update.1 = (bf16[4,768,128]{2,1,0:T(8,128)(2,1)}, f32[8,128]{1,0:T(8,128)S(1)}, f32[40,1536]{1,0:T(8,128)S(1)}) custom-call(s32[2,4]{1,0:T(2,128)S(1)} %bitcast.39, s32[1]{0:T(128)S(6)} %copy.12.counts, s32[2]{0:T(128)S(1)} %pad_add_fusion.ranks.info, bf16[4,128,1024]{2,1,0:T(8,128)(2,1)S(1)} %get-tuple-element.10.qt_ref.refs_0_, ...), custom_call_target="tpu_custom_call" | custom-call | tf_op jit(solution)/shard_map/match_update/pallas_call | solution.py:550
  50.3 0.6 collective-permute-start.11
  50.9 1.4 collective-permute-start.12
  52.2 2.9 %collective-permute-start.13 = (f32[8,128]{1,0:T(8,128)S(1)}, f32[8,128]{1,0:T(8,128)S(1)}, u32[]{:S(2)}, u32[]{:S(2)}) collective-permute-start(f32[8,128]{1,0:T(8,128)S(1)} %get-tuple-element.13), channel_id=1, source_target_pairs={{0,3},{1,2},{2,1},{3,0},{4,7},{5,6},{6,5},{7,4},{8,11},{9,10},{10,... | collective-permute-start | bytes 12296 | tf_op jit(solution)/shard_map/ppermute | solution.py:21
  55.1 0.0 collective-permute-done.11
  55.1 0.9 collective-permute-done.12
  56.0 1.1 collective-permute-done.13
  57.1 3.1 %collective-permute-start.14 = (f32[8,128]{1,0:T(8,128)S(1)}, f32[8,128]{1,0:T(8,128)S(1)}, u32[]{:S(2)}, u32[]{:S(2)}) collective-permute-start(f32[8,128]{1,0:T(8,128)S(1)} %add_add_fusion), channel_id=1, source_target_pairs={{0,4},{4,0},{1,5},{5,1},{2,6},{6,2},{3,7},{7,3},{8,12},{12,8},{9,1... | collective-permute-start | bytes 12296 | tf_op jit(solution)/shard_map/ppermute | solution.py:21
  60.2 0.8 collective-permute-done.14
  61.0 20.0 %collective-permute-start.15 = (f32[2,8,128]{2,1,0:T(8,128)S(1)}, f32[2,8,128]{2,1,0:T(8,128)S(1)}, u32[]{:S(2)}, u32[]{:S(2)}) collective-permute-start(f32[2,8,128]{2,1,0:T(8,128)S(1)} %get-tuple-element.24), channel_id=1, source_target_pairs={{0,8},{8,0},{16,24},{24,16},{32,40},{40,32},{48,56},{56,48},{1,9},... | collective-permute-start | bytes 24584 | tf_op jit(solution)/shard_map/ppermute | solution.py:21
  81.0 21.9 %collective-permute-start.16 = (f32[2,8,128]{2,1,0:T(8,128)S(1)}, f32[2,8,128]{2,1,0:T(8,128)S(1)}, u32[]{:S(2)}, u32[]{:S(2)}) collective-permute-start(f32[2,8,128]{2,1,0:T(8,128)S(1)} %get-tuple-element.24), channel_id=1, source_target_pairs={{0,16},{8,24},{16,0},{24,8},{32,48},{40,56},{48,32},{56,40},{1,17}... | collective-permute-start | bytes 24584 | tf_op jit(solution)/shard_map/ppermute | solution.py:21
  102.9 0.0 collective-permute-start.17
  102.9 0.0 collective-permute-done.15
  102.9 1.6 %collective-permute-done.16 = f32[2,8,128]{2,1,0:T(8,128)S(1)} collective-permute-done((f32[2,8,128]{2,1,0:T(8,128)S(1)}, f32[2,8,128]{2,1,0:T(8,128)S(1)}, u32[]{:S(2)}, u32[]{:S(2)}) %collective-permute-start.16) | collective-permute-done | bytes 8224 | tf_op jit(solution)/shard_map/ppermute | solution.py:21
  104.5 3.8 %collective-permute-done.17 = f32[2,8,128]{2,1,0:T(8,128)S(1)} collective-permute-done((f32[2,8,128]{2,1,0:T(8,128)S(1)}, f32[2,8,128]{2,1,0:T(8,128)S(1)}, u32[]{:S(2)}, u32[]{:S(2)}) %collective-permute-start.17) | collective-permute-done | bytes 8224 | tf_op jit(solution)/shard_map/ppermute | solution.py:21
  108.4 4.5 %collective-permute-start.18 = (f32[4,2,8,128]{3,2,1,0:T(8,128)S(1)}, f32[4,2,8,128]{3,2,1,0:T(8,128)S(1)}, u32[]{:S(2)}, u32[]{:S(2)}) collective-permute-start(f32[4,2,8,128]{3,2,1,0:T(8,128)S(1)} %get-tuple-element.22), channel_id=1, source_target_pairs={{0,32},{8,40},{16,48},{24,56},{32,0},{40,8},{48,16},{56,24},{1,33}... | collective-permute-start | bytes 98312 | tf_op jit(solution)/shard_map/ppermute | solution.py:21
  112.8 3.4 %collective-permute-done.18 = f32[4,2,8,128]{3,2,1,0:T(8,128)S(1)} collective-permute-done((f32[4,2,8,128]{3,2,1,0:T(8,128)S(1)}, f32[4,2,8,128]{3,2,1,0:T(8,128)S(1)}, u32[]{:S(2)}, u32[]{:S(2)}) %collective-permute-start.18) | collective-permute-done | bytes 32800 | tf_op jit(solution)/shard_map/ppermute | solution.py:21
  116.2 20.9 %collective-permute-start.19 = (f32[2,4,2,8,128]{4,3,2,1,0:T(8,128)S(1)}, f32[2,4,2,8,128]{4,3,2,1,0:T(8,128)S(1)}, u32[]{:S(2)}, u32[]{:S(2)}) collective-permute-start(f32[2,4,2,8,128]{4,3,2,1,0:T(8,128)S(1)} %get-tuple-element.20), channel_id=1, source_target_pairs={{0,64},{64,0},{128,192},{192,128},{1,65},{65,1},{129,193},{193,129... | collective-permute-start | bytes 196616 | tf_op jit(solution)/shard_map/ppermute | solution.py:21
  137.1 2.8 %collective-permute-start.20 = (f32[2,4,2,8,128]{4,3,2,1,0:T(8,128)S(1)}, f32[2,4,2,8,128]{4,3,2,1,0:T(8,128)S(1)}, u32[]{:S(2)}, u32[]{:S(2)}) collective-permute-start(f32[2,4,2,8,128]{4,3,2,1,0:T(8,128)S(1)} %get-tuple-element.20), channel_id=1, source_target_pairs={{0,128},{64,192},{128,0},{192,64},{1,129},{65,193},{129,1},{193,65... | collective-permute-start | bytes 196616 | tf_op jit(solution)/shard_map/ppermute | solution.py:21
  139.9 0.0 collective-permute-start.21
  139.9 0.0 collective-permute-done.19
  139.9 2.9 %collective-permute-done.20 = f32[2,4,2,8,128]{4,3,2,1,0:T(8,128)S(1)} collective-permute-done((f32[2,4,2,8,128]{4,3,2,1,0:T(8,128)S(1)}, f32[2,4,2,8,128]{4,3,2,1,0:T(8,128)S(1)}, u32[]{:S(2)}, u32[]{:S(2)}) %collective-permute-start.20) | collective-permute-done | bytes 65568 | tf_op jit(solution)/shard_map/ppermute | solution.py:21
  142.9 2.5 %collective-permute-done.21 = f32[2,4,2,8,128]{4,3,2,1,0:T(8,128)S(1)} collective-permute-done((f32[2,4,2,8,128]{4,3,2,1,0:T(8,128)S(1)}, f32[2,4,2,8,128]{4,3,2,1,0:T(8,128)S(1)}, u32[]{:S(2)}, u32[]{:S(2)}) %collective-permute-start.21) | collective-permute-done | bytes 65568 | tf_op jit(solution)/shard_map/ppermute | solution.py:21
  145.4 5.6 %pose_solve.1 = (f32[2,6]{1,0:T(2,128)}, f32[2,768]{1,0:T(2,128)}) custom-call(s32[2]{0:T(128)S(1)} %pad_add_fusion.ranks.info, f32[64,8,128]{2,1,0:T(8,128)S(1)} %bitcast.28, f32[40,1536]{1,0:T(8,128)S(1)} %get-tuple-element.14.h_ref), custom_call_target="tpu_custom_call" | custom-call | tf_op jit(solution)/shard_map/pose_solve/pallas_call | solution.py:239
  (13 shorter events, 0.1 us)
Async XLA Ops:
  0.6 11.9 %collective-permute-start = (bf16[2,768,128]{2,1,0:T(8,128)(2,1)}, bf16[2,768,128]{2,1,0:T(8,128)(2,1)S(1)}, u32[]{:S(2)}, u32[]{:S(2)}) collective-permute-start(bf16[2,768,128]{2,1,0:T(8,128)(2,1)} %bitcast.30), channel_id=1, source_target_pairs={{0,1},{1,0},{2,3},{3,2},{4,5},{5,4},{6,7},{7,6},{8,9},{9,8},{10,11... | collective-permute-start | bytes 1179656 | tf_op jit(solution)/shard_map/ppermute | solution.py:21
  1.5 12.3 %collective-permute-start.1 = (bf16[2,768,128]{2,1,0:T(8,128)(2,1)}, bf16[2,768,128]{2,1,0:T(8,128)(2,1)S(1)}, u32[]{:S(2)}, u32[]{:S(2)}) collective-permute-start(bf16[2,768,128]{2,1,0:T(8,128)(2,1)} %bitcast.31), channel_id=1, source_target_pairs={{0,3},{1,2},{2,1},{3,0},{4,7},{5,6},{6,5},{7,4},{8,11},{9,10},{10,... | collective-permute-start | bytes 1179656 | tf_op jit(solution)/shard_map/ppermute | solution.py:21
  3.0 13.2 %collective-permute-start.2 = (bf16[2,768,128]{2,1,0:T(8,128)(2,1)}, bf16[2,768,128]{2,1,0:T(8,128)(2,1)S(1)}, u32[]{:S(2)}, u32[]{:S(2)}) collective-permute-start(bf16[2,768,128]{2,1,0:T(8,128)(2,1)} %bitcast.32), channel_id=1, source_target_pairs={{4,0},{8,4},{12,8},{16,12},{20,16},{24,20},{28,24},{32,28},{36,32}... | collective-permute-start | bytes 1179656 | tf_op jit(solution)/shard_map/ppermute | solution.py:592
  5.3 25.2 %collective-permute-start.5 = (bf16[4,128,128]{2,1,0:T(8,128)(2,1)S(1)}, bf16[4,128,128]{2,1,0:T(8,128)(2,1)S(1)}, u32[]{:S(2)}, u32[]{:S(2)}) collective-permute-start(bf16[4,128,128]{2,1,0:T(8,128)(2,1)S(1)} %get-tuple-element.18), channel_id=1, source_target_pairs={{0,1},{1,2},{2,3},{4,5},{5,6},{6,7},{8,9},{9,10},{10,11},{12,13},{... | collective-permute-start | bytes 393224 | tf_op jit(solution)/shard_map/ppermute | solution.py:604
  12.6 14.4 %collective-permute-start.3 = (bf16[2,768,128]{2,1,0:T(8,128)(2,1)S(1)}, bf16[2,768,128]{2,1,0:T(8,128)(2,1)S(1)}, u32[]{:S(2)}, u32[]{:S(2)}) collective-permute-start(bf16[2,768,128]{2,1,0:T(8,128)(2,1)S(1)} %collective-permute-done.side1.refs_0_.refs_6_), channel_id=1, source_target_pairs={{4,0},{8,4},{12,8},{16,12},{20,16},{24,20},{28,24},{32,28},{36,32}... | collective-permute-start | bytes 1179656 | tf_op jit(solution)/shard_map/ppermute | solution.py:592
  13.9 14.4 %collective-permute-start.4 = (bf16[2,768,128]{2,1,0:T(8,128)(2,1)S(1)}, bf16[2,768,128]{2,1,0:T(8,128)(2,1)S(1)}, u32[]{:S(2)}, u32[]{:S(2)}) collective-permute-start(bf16[2,768,128]{2,1,0:T(8,128)(2,1)S(1)} %collective-permute-done.1.side3.refs_1_.refs_7_), channel_id=1, source_target_pairs={{4,0},{8,4},{12,8},{16,12},{20,16},{24,20},{28,24},{32,28},{36,32}... | collective-permute-start | bytes 1179656 | tf_op jit(solution)/shard_map/ppermute | solution.py:592
  15.3 7.1 %collective-permute-start.8 = (bf16[2,384,128]{2,1,0:T(8,128)(2,1)S(1)}, bf16[2,384,128]{2,1,0:T(8,128)(2,1)S(1)}, u32[]{:S(2)}, u32[]{:S(2)}) collective-permute-start(bf16[2,384,128]{2,1,0:T(8,128)(2,1)S(1)} %slice.19), channel_id=1, source_target_pairs={{0,1},{1,0},{2,3},{3,2},{4,5},{5,4},{6,7},{7,6},{8,9},{9,8},{10,11... | collective-permute-start | bytes 589832 | tf_op jit(solution)/shard_map/ppermute | solution.py:21
  16.2 9.5 %collective-permute-start.7 = (bf16[2,384,128]{2,1,0:T(8,128)(2,1)S(1)}, bf16[2,384,128]{2,1,0:T(8,128)(2,1)S(1)}, u32[]{:S(2)}, u32[]{:S(2)}) collective-permute-start(bf16[2,384,128]{2,1,0:T(8,128)(2,1)S(1)} %slice.18), channel_id=1, source_target_pairs={{0,3},{1,2},{2,1},{3,0},{4,7},{5,6},{6,5},{7,4},{8,11},{9,10},{10,... | collective-permute-start | bytes 589832 | tf_op jit(solution)/shard_map/ppermute | solution.py:21
  17.1 1.0 copy-start.3
  18.0 0.7 copy-start.7
  22.4 8.1 %collective-permute-start.6 = (bf16[4,128,128]{2,1,0:T(8,128)(2,1)S(1)}, bf16[4,128,128]{2,1,0:T(8,128)(2,1)S(1)}, u32[]{:S(2)}, u32[]{:S(2)}) collective-permute-start(bf16[4,128,128]{2,1,0:T(8,128)(2,1)S(1)} %get-tuple-element.17), channel_id=1, source_target_pairs={{1,0},{2,1},{3,2},{5,4},{6,5},{7,6},{9,8},{10,9},{11,10},{13,12},{... | collective-permute-start | bytes 393224 | tf_op jit(solution)/shard_map/ppermute | solution.py:605
  25.7 4.8 %collective-permute-start.10 = (bf16[2,384,128]{2,1,0:T(8,128)(2,1)S(1)}, bf16[2,384,128]{2,1,0:T(8,128)(2,1)S(1)}, u32[]{:S(2)}, u32[]{:S(2)}) collective-permute-start(bf16[2,384,128]{2,1,0:T(8,128)(2,1)S(1)} %collective-permute-done.8.refs_9_), channel_id=1, source_target_pairs={{4,0},{8,4},{12,8},{16,12},{20,16},{24,20},{28,24},{32,28},{36,32}... | collective-permute-start | bytes 589832 | tf_op jit(solution)/shard_map/ppermute | solution.py:592
  27.0 4.0 %collective-permute-start.9 = (bf16[2,384,128]{2,1,0:T(8,128)(2,1)S(1)}, bf16[2,384,128]{2,1,0:T(8,128)(2,1)S(1)}, u32[]{:S(2)}, u32[]{:S(2)}) collective-permute-start(bf16[2,384,128]{2,1,0:T(8,128)(2,1)S(1)} %collective-permute-done.7.refs_8_), channel_id=1, source_target_pairs={{4,0},{8,4},{12,8},{16,12},{20,16},{24,20},{28,24},{32,28},{36,32}... | collective-permute-start | bytes 589832 | tf_op jit(solution)/shard_map/ppermute | solution.py:592
  28.3 2.7 %copy-start = (bf16[4,12,64,128]{3,2,1,0:T(8,128)(2,1)S(1)}, bf16[4,12,64,128]{3,2,1,0:T(8,128)(2,1)}, u32[]{:S(2)}) copy-start(bf16[4,12,64,128]{3,2,1,0:T(8,128)(2,1)} %param.12) | copy-start | bytes 2359300
  28.3 2.6 %copy-start.1 = (bf16[9,256,256]{2,1,0:T(8,128)(2,1)S(1)}, bf16[9,256,256]{2,1,0:T(8,128)(2,1)}, u32[]{:S(2)}) copy-start(bf16[9,256,256]{2,1,0:T(8,128)(2,1)} %param.15) | copy-start | bytes 3538948
  28.3 2.6 %copy-start.2 = (bf16[9,256,128]{2,1,0:T(8,128)(2,1)S(1)}, bf16[9,256,128]{2,1,0:T(8,128)(2,1)}, u32[]{:S(2)}) copy-start(bf16[9,256,128]{2,1,0:T(8,128)(2,1)} %param.16) | copy-start | bytes 1769476
  28.3 2.6 %copy-start.4 = (bf16[2,12,64,128]{3,2,1,0:T(8,128)(2,1)S(1)}, bf16[2,12,64,128]{3,2,1,0:T(8,128)(2,1)}, u32[]{:S(2)}) copy-start(bf16[2,12,64,128]{3,2,1,0:T(8,128)(2,1)} %param.9) | copy-start | bytes 1179652
  28.4 2.6 %copy-start.5 = (f32[2,768]{1,0:T(2,128)S(1)}, f32[2,768]{1,0:T(2,128)}, u32[]{:S(2)}) copy-start(f32[2,768]{1,0:T(2,128)} %refs_19_.1) | copy-start | bytes 18436
  28.4 2.6 %copy-start.6 = (f32[128,6]{0,1:T(8,128)S(1)}, f32[128,6]{0,1:T(8,128)}, u32[]{:S(2)}) copy-start(f32[128,6]{0,1:T(8,128)} %param.10) | copy-start | bytes 9220
  28.4 2.6 %copy-start.8 = (s32[4,2]{0,1:T(2,128)S(1)}, s32[4,2]{0,1:T(2,128)}, u32[]{:S(2)}) copy-start(s32[4,2]{0,1:T(2,128)} %param.13) | copy-start | bytes 100
  28.4 2.6 %copy-start.9 = (bf16[4,128]{1,0:T(4,128)(2,1)S(1)}, bf16[4,128]{1,0:T(4,128)(2,1)}, u32[]{:S(2)}) copy-start(bf16[4,128]{1,0:T(4,128)(2,1)} %refs_17_.1) | copy-start | bytes 3076
  50.3 4.8 %collective-permute-start.11 = (f32[8,128]{1,0:T(8,128)S(1)}, f32[8,128]{1,0:T(8,128)S(1)}, u32[]{:S(2)}, u32[]{:S(2)}) collective-permute-start(f32[8,128]{1,0:T(8,128)S(1)} %get-tuple-element.13), channel_id=1, source_target_pairs={{0,1},{1,0},{2,3},{3,2},{4,5},{5,4},{6,7},{7,6},{8,9},{9,8},{10,11... | collective-permute-start | bytes 12296 | tf_op jit(solution)/shard_map/ppermute | solution.py:21
  50.9 5.1 %collective-permute-start.12 = (f32[8,128]{1,0:T(8,128)S(1)}, f32[8,128]{1,0:T(8,128)S(1)}, u32[]{:S(2)}, u32[]{:S(2)}) collective-permute-start(f32[8,128]{1,0:T(8,128)S(1)} %get-tuple-element.13), channel_id=1, source_target_pairs={{0,2},{1,3},{2,0},{3,1},{4,6},{5,7},{6,4},{7,5},{8,10},{9,11},{10,... | collective-permute-start | bytes 12296 | tf_op jit(solution)/shard_map/ppermute | solution.py:21
  52.2 4.8 %collective-permute-start.13 = (f32[8,128]{1,0:T(8,128)S(1)}, f32[8,128]{1,0:T(8,128)S(1)}, u32[]{:S(2)}, u32[]{:S(2)}) collective-permute-start(f32[8,128]{1,0:T(8,128)S(1)} %get-tuple-element.13), channel_id=1, source_target_pairs={{0,3},{1,2},{2,1},{3,0},{4,7},{5,6},{6,5},{7,4},{8,11},{9,10},{10,... | collective-permute-start | bytes 12296 | tf_op jit(solution)/shard_map/ppermute | solution.py:21
  57.1 3.9 %collective-permute-start.14 = (f32[8,128]{1,0:T(8,128)S(1)}, f32[8,128]{1,0:T(8,128)S(1)}, u32[]{:S(2)}, u32[]{:S(2)}) collective-permute-start(f32[8,128]{1,0:T(8,128)S(1)} %add_add_fusion), channel_id=1, source_target_pairs={{0,4},{4,0},{1,5},{5,1},{2,6},{6,2},{3,7},{7,3},{8,12},{12,8},{9,1... | collective-permute-start | bytes 12296 | tf_op jit(solution)/shard_map/ppermute | solution.py:21
  61.0 41.9 %collective-permute-start.15 = (f32[2,8,128]{2,1,0:T(8,128)S(1)}, f32[2,8,128]{2,1,0:T(8,128)S(1)}, u32[]{:S(2)}, u32[]{:S(2)}) collective-permute-start(f32[2,8,128]{2,1,0:T(8,128)S(1)} %get-tuple-element.24), channel_id=1, source_target_pairs={{0,8},{8,0},{16,24},{24,16},{32,40},{40,32},{48,56},{56,48},{1,9},... | collective-permute-start | bytes 24584 | tf_op jit(solution)/shard_map/ppermute | solution.py:21
  81.0 23.5 %collective-permute-start.16 = (f32[2,8,128]{2,1,0:T(8,128)S(1)}, f32[2,8,128]{2,1,0:T(8,128)S(1)}, u32[]{:S(2)}, u32[]{:S(2)}) collective-permute-start(f32[2,8,128]{2,1,0:T(8,128)S(1)} %get-tuple-element.24), channel_id=1, source_target_pairs={{0,16},{8,24},{16,0},{24,8},{32,48},{40,56},{48,32},{56,40},{1,17}... | collective-permute-start | bytes 24584 | tf_op jit(solution)/shard_map/ppermute | solution.py:21
  102.9 5.4 %collective-permute-start.17 = (f32[2,8,128]{2,1,0:T(8,128)S(1)}, f32[2,8,128]{2,1,0:T(8,128)S(1)}, u32[]{:S(2)}, u32[]{:S(2)}) collective-permute-start(f32[2,8,128]{2,1,0:T(8,128)S(1)} %get-tuple-element.24), channel_id=1, source_target_pairs={{0,24},{8,16},{16,8},{24,0},{32,56},{40,48},{48,40},{56,32},{1,25}... | collective-permute-start | bytes 24584 | tf_op jit(solution)/shard_map/ppermute | solution.py:21
  108.4 7.8 %collective-permute-start.18 = (f32[4,2,8,128]{3,2,1,0:T(8,128)S(1)}, f32[4,2,8,128]{3,2,1,0:T(8,128)S(1)}, u32[]{:S(2)}, u32[]{:S(2)}) collective-permute-start(f32[4,2,8,128]{3,2,1,0:T(8,128)S(1)} %get-tuple-element.22), channel_id=1, source_target_pairs={{0,32},{8,40},{16,48},{24,56},{32,0},{40,8},{48,16},{56,24},{1,33}... | collective-permute-start | bytes 98312 | tf_op jit(solution)/shard_map/ppermute | solution.py:21
  116.2 23.7 %collective-permute-start.19 = (f32[2,4,2,8,128]{4,3,2,1,0:T(8,128)S(1)}, f32[2,4,2,8,128]{4,3,2,1,0:T(8,128)S(1)}, u32[]{:S(2)}, u32[]{:S(2)}) collective-permute-start(f32[2,4,2,8,128]{4,3,2,1,0:T(8,128)S(1)} %get-tuple-element.20), channel_id=1, source_target_pairs={{0,64},{64,0},{128,192},{192,128},{1,65},{65,1},{129,193},{193,129... | collective-permute-start | bytes 196616 | tf_op jit(solution)/shard_map/ppermute | solution.py:21
  137.1 5.8 %collective-permute-start.20 = (f32[2,4,2,8,128]{4,3,2,1,0:T(8,128)S(1)}, f32[2,4,2,8,128]{4,3,2,1,0:T(8,128)S(1)}, u32[]{:S(2)}, u32[]{:S(2)}) collective-permute-start(f32[2,4,2,8,128]{4,3,2,1,0:T(8,128)S(1)} %get-tuple-element.20), channel_id=1, source_target_pairs={{0,128},{64,192},{128,0},{192,64},{1,129},{65,193},{129,1},{193,65... | collective-permute-start | bytes 196616 | tf_op jit(solution)/shard_map/ppermute | solution.py:21
  139.9 5.5 %collective-permute-start.21 = (f32[2,4,2,8,128]{4,3,2,1,0:T(8,128)S(1)}, f32[2,4,2,8,128]{4,3,2,1,0:T(8,128)S(1)}, u32[]{:S(2)}, u32[]{:S(2)}) collective-permute-start(f32[2,4,2,8,128]{4,3,2,1,0:T(8,128)S(1)} %get-tuple-element.20), channel_id=1, source_target_pairs={{0,192},{64,128},{128,64},{192,0},{1,193},{65,129},{129,65},{193,1... | collective-permute-start | bytes 196616 | tf_op jit(solution)/shard_map/ppermute | solution.py:21

commit v5 on v4

--- a/solution.py
+++ b/solution.py
@@ -27,8 +27,8 @@
     parts = jnp.stack([block, swapped(block, "core", 1)])
     parts = jnp.stack([parts] + [swapped(parts, "z", s) for s in (1, 2, 3)])
     parts = jnp.stack([parts, swapped(parts, "z", 4)])
-    parts = jnp.stack([parts] + [swapped(parts, "y", s) for s in (1, 2, 3)])
-    return parts.reshape((-1,) + block.shape)
+    parts = [parts] + [swapped(parts, "y", s) for s in (1, 2, 3)]
+    return [part.reshape((-1,) + block.shape) for part in parts]
 
 
 class Facts:
@@ -169,13 +169,16 @@
     return diag, sides
 
 
-def solve_body(nodes, pix, info, g_ref, h_ref, pose_ref, depth_ref, t_ref, d_ref, l_ref, u_ref, near):
+def solve_body(nodes, pix, groups, info, *refs):
+    g_refs, refs = refs[:groups], refs[groups:]
+    h_ref, pose_ref, depth_ref, t_ref, d_ref, l_ref, u_ref, near = refs
+    per = nodes // groups
     count = len(REAL)
     lane = lax.broadcasted_iota(jnp.int32, (16, 128), 1)
     sub = lax.broadcasted_iota(jnp.int32, (16, 128), 0)
     me = info[0]
     for n in range(nodes):
-        t_ref[n] = g_ref[n ^ me]
+        t_ref[n ^ me] = g_refs[n // per][n % per]
     rest = jnp.zeros((128 - nodes, 128), jnp.float32)
     for k in range(6):
         t = jnp.concatenate([t_ref[:, k, :], rest], axis=0).T
@@ -233,16 +236,16 @@
 
 
 def solve_call(me, gathered, h):
-    nodes = gathered.shape[0]
+    nodes = sum(part.shape[0] for part in gathered)
     pix = h.shape[1] // 2
     vmem = pl.BlockSpec(memory_space=pltpu.VMEM)
     return pl.pallas_call(
-        functools.partial(solve_body, nodes, pix),
+        functools.partial(solve_body, nodes, pix, len(gathered)),
         out_shape=(
             jax.ShapeDtypeStruct((2, 6), jnp.float32),
             jax.ShapeDtypeStruct((2, pix), jnp.float32),
         ),
-        in_specs=[pl.BlockSpec(memory_space=pltpu.SMEM), vmem, vmem],
+        in_specs=[pl.BlockSpec(memory_space=pltpu.SMEM)] + [vmem] * (len(gathered) + 1),
         out_specs=(vmem, vmem),
         scratch_shapes=[
             pltpu.VMEM((nodes, 8, 128), jnp.float32),
@@ -253,7 +256,7 @@
         ],
         compiler_params=pltpu.CompilerParams(vmem_limit_bytes=12 << 20),
         name="pose_solve",
-    )(me, gathered, h)
+    )(me, *gathered, h)
 
 
 NT = (((1,), (1,)), ((), ()))
@@ -596,9 +599,8 @@
     own1, own3 = swapped(own, "x", 1), swapped(own, "x", 3)
     next0 = following(own)
     next1, next3 = following(own1), following(own3)
-    half = pix // 2
-    own2a, own2b = swapped(own1[:, :half], "x", 3), swapped(own3[:, half:], "x", 1)
-    next2a, next2b = following(own2a), following(own2b)
+    own2 = swapped(own1, "x", 3)
+    next2 = following(own2)
     acc, turned_q = first_call(facts, slot_count, col_count, (own, own1, own3), own, next0)
     rows_x = lax.axis_size("x")
     hide_up = lax.ppermute(state[:, pix - halo :], "x", [(i, i + 1) for i in range(rows_x - 1)])
@@ -613,9 +615,9 @@
         state,
         hide_up,
         hide_down,
-        (own, own1, own3, own2a, own2b),
-        (next0, next1, next3, next2a, next2b),
-        2,
+        (own, own1, own3, own2),
+        (next0, next1, next3, next2),
+        1,
         (wg, wc, w_head),
         poses.T,
         inv_depth,

time: 152 us -> 148 us (0.974); the launches traced: 151 us -> 149 us
  starting transfers between devices: 93.2 us -> 91.3 us
    ppermute x5 -> x4, starting transfers between devices: 6.44 us -> 5.13 us  [following(): return lax.ppermute(value, EDGE, [(i + 1, i) for i in range(nodes - 1)])]
    ppermute x15 -> x14, starting transfers between devices: 82.2 us -> 82.1 us  [swapped(): return lax.ppermute(value, axis, [(i, i ^ step) for i in range(count)])]
    ppermute x15 -> x14, waiting for transfers between devices: 24.5 us -> 24.4 us  [swapped(): return lax.ppermute(value, axis, [(i, i ^ step) for i in range(count)])]
  transfers between devices with their start and end apart: 22 -> 20, of which waited for: 11 -> 10; matrix products, arithmetic and copies ran while one was open for 1% -> 1% of each run, Pallas kernels for 2% -> 2%
where the time goes in v5:
time: 148 us; the launch traced here: 149 us
  starting transfers between devices  91.3 us (62%)
  Pallas kernels  28.4 us (19%)
  waiting for transfers between devices  24.5 us (17%)
  local copies, waits for them, and re-layouts  2.71 us (2%)
  between operations  1.55 us (1%)
    ppermute x14, starting transfers between devices, swapped(): return lax.ppermute(value, axis, [(i, i ^ step) for i in range(count)])  82.1 us
    ppermute x14, waiting for transfers between devices, swapped(): return lax.ppermute(value, axis, [(i, i ^ step) for i in range(count)])  24.4 us
    pallas_call x1, Pallas kernels, fused_call(): pl.pallas_call(functools.partial(fused_body, dims), in_specs=[SMEM] * 3 +...  19.2 us
    pallas_call x1, Pallas kernels, solve_call(): pl.pallas_call(functools.partial(solve_body, nodes, pix, len(gathered)),...  5.56 us
    ppermute x4, starting transfers between devices, following(): return lax.ppermute(value, EDGE, [(i + 1, i) for i in range(nodes - 1)])  5.13 us
  transfers between devices with their start and end apart: 20, of which 10 were waited for; matrix products, arithmetic and copies ran while one was open for 1% of the time, Pallas kernels for 2%

profile of v5, /device:TPU:6, one launch (start us, length us, event | category | flops | bytes accessed | tf_op | source)
XLA Modules:
  0.0 148.6 jit_solution(15502799080254138333)
XLA Ops:
  0.6 0.9 collective-permute-start
  1.5 1.5 %collective-permute-start.1 = (bf16[2,768,128]{2,1,0:T(8,128)(2,1)}, bf16[2,768,128]{2,1,0:T(8,128)(2,1)S(1)}, u32[]{:S(2)}, u32[]{:S(2)}) collective-permute-start(bf16[2,768,128]{2,1,0:T(8,128)(2,1)} %bitcast.28), channel_id=1, source_target_pairs={{0,3},{1,2},{2,1},{3,0},{4,7},{5,6},{6,5},{7,4},{8,11},{9,10},{10,... | collective-permute-start | bytes 1179656 | tf_op jit(solution)/shard_map/ppermute | solution.py:21
  3.0 1.3 collective-permute-start.2
  4.3 1.0 fusion.2
  5.3 1.3 collective-permute-start.5
  7.3 5.3 %collective-permute-done.side1.refs_0_.refs_6_ = bf16[2,768,128]{2,1,0:T(8,128)(2,1)S(1)} collective-permute-done((bf16[2,768,128]{2,1,0:T(8,128)(2,1)}, bf16[2,768,128]{2,1,0:T(8,128)(2,1)S(1)}, u32[]{:S(2)}, u32[]{:S(2)}) %collective-permute-start) | collective-permute-done | bytes 393248 | tf_op jit(solution)/shard_map/ppermute | solution.py:21
  12.6 1.3 collective-permute-start.3
  13.8 0.1 collective-permute-start.7
  13.9 0.0 collective-permute-done.1.side3.refs_1_.refs_7_
  14.0 1.3 collective-permute-start.4
  15.3 0.1 pad_add_fusion.ranks.info
  15.3 0.0 collective-permute-done.2.after.refs_9_
  15.3 2.9 %collective-permute-start.6 = (bf16[4,128,128]{2,1,0:T(8,128)(2,1)S(1)}, bf16[4,128,128]{2,1,0:T(8,128)(2,1)S(1)}, u32[]{:S(2)}, u32[]{:S(2)}) collective-permute-start(bf16[4,128,128]{2,1,0:T(8,128)(2,1)S(1)} %get-tuple-element.17), channel_id=1, source_target_pairs={{1,0},{2,1},{3,2},{5,4},{6,5},{7,6},{9,8},{10,9},{11,10},{13,12},{... | collective-permute-start | bytes 393224 | tf_op jit(solution)/shard_map/ppermute | solution.py:607
  18.2 0.0 copy-start.3
  18.2 1.0 copy-done.3
  19.2 0.7 copy-done.7
  19.9 1.5 %match_first.1 = (f32[4,136,1024]{2,1,0:T(8,128)S(1)}, bf16[4,128,1024]{2,1,0:T(8,128)(2,1)S(1)}) custom-call(s32[2,4]{1,0:T(2,128)S(1)} %bitcast.38, s32[1]{0:T(128)S(6)} %copy.12.counts, s32[2]{0:T(128)S(1)} %pad_add_fusion.ranks.info, bf16[2,768,128]{2,1,0:T(8,128)(2,1)S(1)} %bitcast.30, ...), custom_call_target="tpu_custom_call" | custom-call | flops 3221225472 | bytes 4456448 | tf_op jit(solution)/shard_map/match_first/pallas_call | solution.py:516
  21.4 5.6 %collective-permute-done.7.refs_8_ = bf16[2,768,128]{2,1,0:T(8,128)(2,1)S(1)} collective-permute-done((bf16[2,768,128]{2,1,0:T(8,128)(2,1)S(1)}, bf16[2,768,128]{2,1,0:T(8,128)(2,1)S(1)}, u32[]{:S(2)}, u32[]{:S(2)}) %collective-permute-start.7) | collective-permute-done | bytes 393248 | tf_op jit(solution)/shard_map/ppermute | solution.py:21
  27.0 1.3 collective-permute-start.8
  28.3 0.0 collective-permute-done.3.refs_2_.refs_10_
  28.3 0.0 collective-permute-done.4.refs_3_.refs_11_
  28.3 0.0 copy-start
  28.3 0.0 copy-start.1
  28.3 0.0 copy-start.2
  28.3 0.0 copy-start.4
  28.3 0.0 copy-start.5
  28.3 0.0 copy-start.6
  28.4 0.0 copy-start.8
  28.4 0.0 copy-start.9
  28.4 2.1 %match_second.1.refs_1_ = f32[4,136,1024]{2,1,0:T(8,128)S(1)} custom-call(s32[2,4]{1,0:T(2,128)S(1)} %bitcast.39, s32[1]{0:T(128)S(6)} %copy.12.counts, s32[2]{0:T(128)S(1)} %pad_add_fusion.ranks.info, bf16[4,128,1024]{2,1,0:T(8,128)(2,1)S(1)} %get-tuple-element.10.qt_ref.refs_0_, f32[4,136,1024]{2,1,0:T(8,128)S(1)} %get-tuple-element.11.old, ...), custom_call_target="tpu_custom_call" | custom-call | flops 6442450944 | bytes 4456448 | tf_op jit(solution)/shard_map/match_second/pallas_call | solution.py:534
  30.5 0.0 collective-permute-done.5.refs_3_
  30.5 0.0 collective-permute-done.6.refs_4_
  30.5 0.1 collective-permute-done.8.refs_12_
  30.6 0.0 copy-done
  30.6 0.0 copy-done.2
  30.6 0.0 copy-done.4
  30.6 0.0 copy-done.5
  30.6 0.0 copy-done.6
  30.6 0.0 copy-done.8
  30.6 0.0 copy-done.9
  30.6 19.2 %match_update.1 = (bf16[4,768,128]{2,1,0:T(8,128)(2,1)}, f32[8,128]{1,0:T(8,128)S(1)}, f32[40,1536]{1,0:T(8,128)S(1)}) custom-call(s32[2,4]{1,0:T(2,128)S(1)} %bitcast.40, s32[1]{0:T(128)S(6)} %copy.12.counts, s32[2]{0:T(128)S(1)} %pad_add_fusion.ranks.info, bf16[4,128,1024]{2,1,0:T(8,128)(2,1)S(1)} %get-tuple-element.10.qt_ref.refs_0_, ...), custom_call_target="tpu_custom_call" | custom-call | tf_op jit(solution)/shard_map/match_update/pallas_call | solution.py:553
  49.9 0.1 collective-permute-start.10
  50.0 1.5 %collective-permute-start.11 = (f32[8,128]{1,0:T(8,128)S(1)}, f32[8,128]{1,0:T(8,128)S(1)}, u32[]{:S(2)}, u32[]{:S(2)}) collective-permute-start(f32[8,128]{1,0:T(8,128)S(1)} %get-tuple-element.13), channel_id=1, source_target_pairs={{0,3},{1,2},{2,1},{3,0},{4,7},{5,6},{6,5},{7,4},{8,11},{9,10},{10,... | collective-permute-start | bytes 12296 | tf_op jit(solution)/shard_map/ppermute | solution.py:21
  51.5 2.0 %collective-permute-start.9 = (f32[8,128]{1,0:T(8,128)S(1)}, f32[8,128]{1,0:T(8,128)S(1)}, u32[]{:S(2)}, u32[]{:S(2)}) collective-permute-start(f32[8,128]{1,0:T(8,128)S(1)} %get-tuple-element.13), channel_id=1, source_target_pairs={{0,1},{1,0},{2,3},{3,2},{4,5},{5,4},{6,7},{7,6},{8,9},{9,8},{10,11... | collective-permute-start | bytes 12296 | tf_op jit(solution)/shard_map/ppermute | solution.py:21
  53.5 1.6 %collective-permute-done.10 = f32[8,128]{1,0:T(8,128)S(1)} collective-permute-done((f32[8,128]{1,0:T(8,128)S(1)}, f32[8,128]{1,0:T(8,128)S(1)}, u32[]{:S(2)}, u32[]{:S(2)}) %collective-permute-start.10) | collective-permute-done | bytes 4128 | tf_op jit(solution)/shard_map/ppermute | solution.py:21
  55.1 0.0 collective-permute-done.11
  55.1 0.0 collective-permute-done.9
  55.1 5.4 %collective-permute-start.12 = (f32[8,128]{1,0:T(8,128)S(1)}, f32[8,128]{1,0:T(8,128)S(1)}, u32[]{:S(2)}, u32[]{:S(2)}) collective-permute-start(f32[8,128]{1,0:T(8,128)S(1)} %add_add_fusion), channel_id=1, source_target_pairs={{0,4},{4,0},{1,5},{5,1},{2,6},{6,2},{3,7},{7,3},{8,12},{12,8},{9,1... | collective-permute-start | bytes 12296 | tf_op jit(solution)/shard_map/ppermute | solution.py:21
  60.5 0.8 collective-permute-done.12
  61.4 18.9 %collective-permute-start.13 = (f32[2,8,128]{2,1,0:T(8,128)S(1)}, f32[2,8,128]{2,1,0:T(8,128)S(1)}, u32[]{:S(2)}, u32[]{:S(2)}) collective-permute-start(f32[2,8,128]{2,1,0:T(8,128)S(1)} %get-tuple-element.22), channel_id=1, source_target_pairs={{0,8},{8,0},{16,24},{24,16},{32,40},{40,32},{48,56},{56,48},{1,9},... | collective-permute-start | bytes 24584 | tf_op jit(solution)/shard_map/ppermute | solution.py:21
  80.2 18.5 %collective-permute-start.14 = (f32[2,8,128]{2,1,0:T(8,128)S(1)}, f32[2,8,128]{2,1,0:T(8,128)S(1)}, u32[]{:S(2)}, u32[]{:S(2)}) collective-permute-start(f32[2,8,128]{2,1,0:T(8,128)S(1)} %get-tuple-element.22), channel_id=1, source_target_pairs={{0,16},{8,24},{16,0},{24,8},{32,48},{40,56},{48,32},{56,40},{1,17}... | collective-permute-start | bytes 24584 | tf_op jit(solution)/shard_map/ppermute | solution.py:21
  98.8 1.5 collective-permute-start.15
  100.3 0.0 collective-permute-done.13
  100.3 0.2 collective-permute-done.14
  100.4 3.8 %collective-permute-done.15 = f32[2,8,128]{2,1,0:T(8,128)S(1)} collective-permute-done((f32[2,8,128]{2,1,0:T(8,128)S(1)}, f32[2,8,128]{2,1,0:T(8,128)S(1)}, u32[]{:S(2)}, u32[]{:S(2)}) %collective-permute-start.15) | collective-permute-done | bytes 8224 | tf_op jit(solution)/shard_map/ppermute | solution.py:21
  104.2 5.0 %collective-permute-start.16 = (f32[4,2,8,128]{3,2,1,0:T(8,128)S(1)}, f32[4,2,8,128]{3,2,1,0:T(8,128)S(1)}, u32[]{:S(2)}, u32[]{:S(2)}) collective-permute-start(f32[4,2,8,128]{3,2,1,0:T(8,128)S(1)} %get-tuple-element.20), channel_id=1, source_target_pairs={{0,32},{8,40},{16,48},{24,56},{32,0},{40,8},{48,16},{56,24},{1,33}... | collective-permute-start | bytes 98312 | tf_op jit(solution)/shard_map/ppermute | solution.py:21
  109.2 2.9 %collective-permute-done.16 = f32[4,2,8,128]{3,2,1,0:T(8,128)S(1)} collective-permute-done((f32[4,2,8,128]{3,2,1,0:T(8,128)S(1)}, f32[4,2,8,128]{3,2,1,0:T(8,128)S(1)}, u32[]{:S(2)}, u32[]{:S(2)}) %collective-permute-start.16) | collective-permute-done | bytes 32800 | tf_op jit(solution)/shard_map/ppermute | solution.py:21
  112.1 24.0 %collective-permute-start.17 = (f32[2,4,2,8,128]{4,3,2,1,0:T(8,128)S(1)}, f32[2,4,2,8,128]{4,3,2,1,0:T(8,128)S(1)}, u32[]{:S(2)}, u32[]{:S(2)}) collective-permute-start(f32[2,4,2,8,128]{4,3,2,1,0:T(8,128)S(1)} %pad_maximum_fusion), channel_id=1, source_target_pairs={{0,64},{64,0},{128,192},{192,128},{1,65},{65,1},{129,193},{193,129... | collective-permute-start | bytes 196616 | tf_op jit(solution)/shard_map/ppermute | solution.py:21
  136.0 1.5 %collective-permute-start.18 = (f32[2,4,2,8,128]{4,3,2,1,0:T(8,128)S(1)}, f32[2,4,2,8,128]{4,3,2,1,0:T(8,128)S(1)}, u32[]{:S(2)}, u32[]{:S(2)}) collective-permute-start(f32[2,4,2,8,128]{4,3,2,1,0:T(8,128)S(1)} %pad_maximum_fusion), channel_id=1, source_target_pairs={{0,128},{64,192},{128,0},{192,64},{1,129},{65,193},{129,1},{193,65... | collective-permute-start | bytes 196616 | tf_op jit(solution)/shard_map/ppermute | solution.py:21
  137.5 1.3 collective-permute-start.19
  138.8 0.0 collective-permute-done.17
  138.8 3.0 %collective-permute-done.18 = f32[2,4,2,8,128]{4,3,2,1,0:T(8,128)S(1)} collective-permute-done((f32[2,4,2,8,128]{4,3,2,1,0:T(8,128)S(1)}, f32[2,4,2,8,128]{4,3,2,1,0:T(8,128)S(1)}, u32[]{:S(2)}, u32[]{:S(2)}) %collective-permute-start.18) | collective-permute-done | bytes 65568 | tf_op jit(solution)/shard_map/ppermute | solution.py:21
  141.8 1.2 collective-permute-done.19
  143.0 5.6 %pose_solve.1 = (f32[2,6]{1,0:T(2,128)}, f32[2,768]{1,0:T(2,128)}) custom-call(s32[2]{0:T(128)S(1)} %pad_add_fusion.ranks.info, f32[16,8,128]{2,1,0:T(8,128)S(1)} %bitcast.33, f32[16,8,128]{2,1,0:T(8,128)S(1)} %bitcast.34, f32[16,8,128]{2,1,0:T(8,128)S(1)} %bitcast.35, f32[16,8,128]{2,1,0:T(8,128)S(1)} %bitcast.36, f32[40,1536]{1,0:T(8,128)S(1)} %get-tuple-element.14.refs_4_), custom_call_target="tpu_custom_call" | custom-call | tf_op jit(solution)/shard_map/pose_solve/pallas_call | solution.py:242
  (6 shorter events, 0.0 us)
Async XLA Ops:
  0.6 11.9 %collective-permute-start = (bf16[2,768,128]{2,1,0:T(8,128)(2,1)}, bf16[2,768,128]{2,1,0:T(8,128)(2,1)S(1)}, u32[]{:S(2)}, u32[]{:S(2)}) collective-permute-start(bf16[2,768,128]{2,1,0:T(8,128)(2,1)} %bitcast.27), channel_id=1, source_target_pairs={{0,1},{1,0},{2,3},{3,2},{4,5},{5,4},{6,7},{7,6},{8,9},{9,8},{10,11... | collective-permute-start | bytes 1179656 | tf_op jit(solution)/shard_map/ppermute | solution.py:21
  1.5 12.4 %collective-permute-start.1 = (bf16[2,768,128]{2,1,0:T(8,128)(2,1)}, bf16[2,768,128]{2,1,0:T(8,128)(2,1)S(1)}, u32[]{:S(2)}, u32[]{:S(2)}) collective-permute-start(bf16[2,768,128]{2,1,0:T(8,128)(2,1)} %bitcast.28), channel_id=1, source_target_pairs={{0,3},{1,2},{2,1},{3,0},{4,7},{5,6},{6,5},{7,4},{8,11},{9,10},{10,... | collective-permute-start | bytes 1179656 | tf_op jit(solution)/shard_map/ppermute | solution.py:21
  3.0 12.3 %collective-permute-start.2 = (bf16[2,768,128]{2,1,0:T(8,128)(2,1)}, bf16[2,768,128]{2,1,0:T(8,128)(2,1)S(1)}, u32[]{:S(2)}, u32[]{:S(2)}) collective-permute-start(bf16[2,768,128]{2,1,0:T(8,128)(2,1)} %bitcast.29), channel_id=1, source_target_pairs={{4,0},{8,4},{12,8},{16,12},{20,16},{24,20},{28,24},{32,28},{36,32}... | collective-permute-start | bytes 1179656 | tf_op jit(solution)/shard_map/ppermute | solution.py:595
  5.3 25.1 %collective-permute-start.5 = (bf16[4,128,128]{2,1,0:T(8,128)(2,1)S(1)}, bf16[4,128,128]{2,1,0:T(8,128)(2,1)S(1)}, u32[]{:S(2)}, u32[]{:S(2)}) collective-permute-start(bf16[4,128,128]{2,1,0:T(8,128)(2,1)S(1)} %get-tuple-element.18), channel_id=1, source_target_pairs={{0,1},{1,2},{2,3},{4,5},{5,6},{6,7},{8,9},{9,10},{10,11},{12,13},{... | collective-permute-start | bytes 393224 | tf_op jit(solution)/shard_map/ppermute | solution.py:606
  12.6 15.7 %collective-permute-start.3 = (bf16[2,768,128]{2,1,0:T(8,128)(2,1)S(1)}, bf16[2,768,128]{2,1,0:T(8,128)(2,1)S(1)}, u32[]{:S(2)}, u32[]{:S(2)}) collective-permute-start(bf16[2,768,128]{2,1,0:T(8,128)(2,1)S(1)} %collective-permute-done.side1.refs_0_.refs_6_), channel_id=1, source_target_pairs={{4,0},{8,4},{12,8},{16,12},{20,16},{24,20},{28,24},{32,28},{36,32}... | collective-permute-start | bytes 1179656 | tf_op jit(solution)/shard_map/ppermute | solution.py:595
  13.8 13.1 %collective-permute-start.7 = (bf16[2,768,128]{2,1,0:T(8,128)(2,1)S(1)}, bf16[2,768,128]{2,1,0:T(8,128)(2,1)S(1)}, u32[]{:S(2)}, u32[]{:S(2)}) collective-permute-start(bf16[2,768,128]{2,1,0:T(8,128)(2,1)S(1)} %collective-permute-done.side1.refs_0_.refs_6_), channel_id=1, source_target_pairs={{0,3},{1,2},{2,1},{3,0},{4,7},{5,6},{6,5},{7,4},{8,11},{9,10},{10,... | collective-permute-start | bytes 1179656 | tf_op jit(solution)/shard_map/ppermute | solution.py:21
  14.0 14.3 %collective-permute-start.4 = (bf16[2,768,128]{2,1,0:T(8,128)(2,1)S(1)}, bf16[2,768,128]{2,1,0:T(8,128)(2,1)S(1)}, u32[]{:S(2)}, u32[]{:S(2)}) collective-permute-start(bf16[2,768,128]{2,1,0:T(8,128)(2,1)S(1)} %collective-permute-done.1.side3.refs_1_.refs_7_), channel_id=1, source_target_pairs={{4,0},{8,4},{12,8},{16,12},{20,16},{24,20},{28,24},{32,28},{36,32}... | collective-permute-start | bytes 1179656 | tf_op jit(solution)/shard_map/ppermute | solution.py:595
  15.3 15.1 %collective-permute-start.6 = (bf16[4,128,128]{2,1,0:T(8,128)(2,1)S(1)}, bf16[4,128,128]{2,1,0:T(8,128)(2,1)S(1)}, u32[]{:S(2)}, u32[]{:S(2)}) collective-permute-start(bf16[4,128,128]{2,1,0:T(8,128)(2,1)S(1)} %get-tuple-element.17), channel_id=1, source_target_pairs={{1,0},{2,1},{3,2},{5,4},{6,5},{7,6},{9,8},{10,9},{11,10},{13,12},{... | collective-permute-start | bytes 393224 | tf_op jit(solution)/shard_map/ppermute | solution.py:607
  18.2 1.0 copy-start.3
  19.2 0.7 copy-start.7
  27.0 3.6 %collective-permute-start.8 = (bf16[2,768,128]{2,1,0:T(8,128)(2,1)S(1)}, bf16[2,768,128]{2,1,0:T(8,128)(2,1)S(1)}, u32[]{:S(2)}, u32[]{:S(2)}) collective-permute-start(bf16[2,768,128]{2,1,0:T(8,128)(2,1)S(1)} %collective-permute-done.7.refs_8_), channel_id=1, source_target_pairs={{4,0},{8,4},{12,8},{16,12},{20,16},{24,20},{28,24},{32,28},{36,32}... | collective-permute-start | bytes 1179656 | tf_op jit(solution)/shard_map/ppermute | solution.py:595
  28.3 2.3 %copy-start = (bf16[4,12,64,128]{3,2,1,0:T(8,128)(2,1)S(1)}, bf16[4,12,64,128]{3,2,1,0:T(8,128)(2,1)}, u32[]{:S(2)}) copy-start(bf16[4,12,64,128]{3,2,1,0:T(8,128)(2,1)} %param.12) | copy-start | bytes 2359300
  28.3 2.3 %copy-start.1 = (bf16[9,256,256]{2,1,0:T(8,128)(2,1)S(1)}, bf16[9,256,256]{2,1,0:T(8,128)(2,1)}, u32[]{:S(2)}) copy-start(bf16[9,256,256]{2,1,0:T(8,128)(2,1)} %param.15) | copy-start | bytes 3538948
  28.3 2.3 %copy-start.2 = (bf16[9,256,128]{2,1,0:T(8,128)(2,1)S(1)}, bf16[9,256,128]{2,1,0:T(8,128)(2,1)}, u32[]{:S(2)}) copy-start(bf16[9,256,128]{2,1,0:T(8,128)(2,1)} %param.16) | copy-start | bytes 1769476
  28.3 2.3 %copy-start.4 = (bf16[2,12,64,128]{3,2,1,0:T(8,128)(2,1)S(1)}, bf16[2,12,64,128]{3,2,1,0:T(8,128)(2,1)}, u32[]{:S(2)}) copy-start(bf16[2,12,64,128]{3,2,1,0:T(8,128)(2,1)} %param.9) | copy-start | bytes 1179652
  28.3 2.3 %copy-start.5 = (f32[2,768]{1,0:T(2,128)S(1)}, f32[2,768]{1,0:T(2,128)}, u32[]{:S(2)}) copy-start(f32[2,768]{1,0:T(2,128)} %refs_17_.1) | copy-start | bytes 18436
  28.3 2.3 %copy-start.6 = (f32[128,6]{0,1:T(8,128)S(1)}, f32[128,6]{0,1:T(8,128)}, u32[]{:S(2)}) copy-start(f32[128,6]{0,1:T(8,128)} %param.10) | copy-start | bytes 9220
  28.4 2.3 %copy-start.8 = (s32[4,2]{0,1:T(2,128)S(1)}, s32[4,2]{0,1:T(2,128)}, u32[]{:S(2)}) copy-start(s32[4,2]{0,1:T(2,128)} %param.13) | copy-start | bytes 100
  28.4 2.3 %copy-start.9 = (bf16[4,128]{1,0:T(4,128)(2,1)S(1)}, bf16[4,128]{1,0:T(4,128)(2,1)}, u32[]{:S(2)}) copy-start(bf16[4,128]{1,0:T(4,128)(2,1)} %refs_15_.1) | copy-start | bytes 3076
  49.9 5.2 %collective-permute-start.10 = (f32[8,128]{1,0:T(8,128)S(1)}, f32[8,128]{1,0:T(8,128)S(1)}, u32[]{:S(2)}, u32[]{:S(2)}) collective-permute-start(f32[8,128]{1,0:T(8,128)S(1)} %get-tuple-element.13), channel_id=1, source_target_pairs={{0,2},{1,3},{2,0},{3,1},{4,6},{5,7},{6,4},{7,5},{8,10},{9,11},{10,... | collective-permute-start | bytes 12296 | tf_op jit(solution)/shard_map/ppermute | solution.py:21
  50.0 5.1 %collective-permute-start.11 = (f32[8,128]{1,0:T(8,128)S(1)}, f32[8,128]{1,0:T(8,128)S(1)}, u32[]{:S(2)}, u32[]{:S(2)}) collective-permute-start(f32[8,128]{1,0:T(8,128)S(1)} %get-tuple-element.13), channel_id=1, source_target_pairs={{0,3},{1,2},{2,1},{3,0},{4,7},{5,6},{6,5},{7,4},{8,11},{9,10},{10,... | collective-permute-start | bytes 12296 | tf_op jit(solution)/shard_map/ppermute | solution.py:21
  51.5 3.6 %collective-permute-start.9 = (f32[8,128]{1,0:T(8,128)S(1)}, f32[8,128]{1,0:T(8,128)S(1)}, u32[]{:S(2)}, u32[]{:S(2)}) collective-permute-start(f32[8,128]{1,0:T(8,128)S(1)} %get-tuple-element.13), channel_id=1, source_target_pairs={{0,1},{1,0},{2,3},{3,2},{4,5},{5,4},{6,7},{7,6},{8,9},{9,8},{10,11... | collective-permute-start | bytes 12296 | tf_op jit(solution)/shard_map/ppermute | solution.py:21
  55.1 6.2 %collective-permute-start.12 = (f32[8,128]{1,0:T(8,128)S(1)}, f32[8,128]{1,0:T(8,128)S(1)}, u32[]{:S(2)}, u32[]{:S(2)}) collective-permute-start(f32[8,128]{1,0:T(8,128)S(1)} %add_add_fusion), channel_id=1, source_target_pairs={{0,4},{4,0},{1,5},{5,1},{2,6},{6,2},{3,7},{7,3},{8,12},{12,8},{9,1... | collective-permute-start | bytes 12296 | tf_op jit(solution)/shard_map/ppermute | solution.py:21
  61.4 38.9 %collective-permute-start.13 = (f32[2,8,128]{2,1,0:T(8,128)S(1)}, f32[2,8,128]{2,1,0:T(8,128)S(1)}, u32[]{:S(2)}, u32[]{:S(2)}) collective-permute-start(f32[2,8,128]{2,1,0:T(8,128)S(1)} %get-tuple-element.22), channel_id=1, source_target_pairs={{0,8},{8,0},{16,24},{24,16},{32,40},{40,32},{48,56},{56,48},{1,9},... | collective-permute-start | bytes 24584 | tf_op jit(solution)/shard_map/ppermute | solution.py:21
  80.2 20.2 %collective-permute-start.14 = (f32[2,8,128]{2,1,0:T(8,128)S(1)}, f32[2,8,128]{2,1,0:T(8,128)S(1)}, u32[]{:S(2)}, u32[]{:S(2)}) collective-permute-start(f32[2,8,128]{2,1,0:T(8,128)S(1)} %get-tuple-element.22), channel_id=1, source_target_pairs={{0,16},{8,24},{16,0},{24,8},{32,48},{40,56},{48,32},{56,40},{1,17}... | collective-permute-start | bytes 24584 | tf_op jit(solution)/shard_map/ppermute | solution.py:21
  98.8 5.4 %collective-permute-start.15 = (f32[2,8,128]{2,1,0:T(8,128)S(1)}, f32[2,8,128]{2,1,0:T(8,128)S(1)}, u32[]{:S(2)}, u32[]{:S(2)}) collective-permute-start(f32[2,8,128]{2,1,0:T(8,128)S(1)} %get-tuple-element.22), channel_id=1, source_target_pairs={{0,24},{8,16},{16,8},{24,0},{32,56},{40,48},{48,40},{56,32},{1,25}... | collective-permute-start | bytes 24584 | tf_op jit(solution)/shard_map/ppermute | solution.py:21
  104.2 7.8 %collective-permute-start.16 = (f32[4,2,8,128]{3,2,1,0:T(8,128)S(1)}, f32[4,2,8,128]{3,2,1,0:T(8,128)S(1)}, u32[]{:S(2)}, u32[]{:S(2)}) collective-permute-start(f32[4,2,8,128]{3,2,1,0:T(8,128)S(1)} %get-tuple-element.20), channel_id=1, source_target_pairs={{0,32},{8,40},{16,48},{24,56},{32,0},{40,8},{48,16},{56,24},{1,33}... | collective-permute-start | bytes 98312 | tf_op jit(solution)/shard_map/ppermute | solution.py:21
  112.1 26.7 %collective-permute-start.17 = (f32[2,4,2,8,128]{4,3,2,1,0:T(8,128)S(1)}, f32[2,4,2,8,128]{4,3,2,1,0:T(8,128)S(1)}, u32[]{:S(2)}, u32[]{:S(2)}) collective-permute-start(f32[2,4,2,8,128]{4,3,2,1,0:T(8,128)S(1)} %pad_maximum_fusion), channel_id=1, source_target_pairs={{0,64},{64,0},{128,192},{192,128},{1,65},{65,1},{129,193},{193,129... | collective-permute-start | bytes 196616 | tf_op jit(solution)/shard_map/ppermute | solution.py:21
  136.0 5.8 %collective-permute-start.18 = (f32[2,4,2,8,128]{4,3,2,1,0:T(8,128)S(1)}, f32[2,4,2,8,128]{4,3,2,1,0:T(8,128)S(1)}, u32[]{:S(2)}, u32[]{:S(2)}) collective-permute-start(f32[2,4,2,8,128]{4,3,2,1,0:T(8,128)S(1)} %pad_maximum_fusion), channel_id=1, source_target_pairs={{0,128},{64,192},{128,0},{192,64},{1,129},{65,193},{129,1},{193,65... | collective-permute-start | bytes 196616 | tf_op jit(solution)/shard_map/ppermute | solution.py:21
  137.5 5.5 %collective-permute-start.19 = (f32[2,4,2,8,128]{4,3,2,1,0:T(8,128)S(1)}, f32[2,4,2,8,128]{4,3,2,1,0:T(8,128)S(1)}, u32[]{:S(2)}, u32[]{:S(2)}) collective-permute-start(f32[2,4,2,8,128]{4,3,2,1,0:T(8,128)S(1)} %pad_maximum_fusion), channel_id=1, source_target_pairs={{0,192},{64,128},{128,64},{192,0},{1,193},{65,129},{129,65},{193,1... | collective-permute-start | bytes 196616 | tf_op jit(solution)/shard_map/ppermute | solution.py:21
